TPU v7x, 128 devices: a whole 4x4x4 slice. The times are simulated.
128 devices in a mesh: section: 8 (over z_hi, y), dp: 16 (over z_lo, x, core).
Axes of the slice: x: 4, y: 4, z: 4 (z_hi: 2, z_lo: 2; z = z_hi * 2 + z_lo), core: 2. Of those that a mesh axis runs over, the one named last changes fastest.
Arguments:
- queries: bfloat16 [8, 32, 128, 4096], P('section', 'dp'), may hold values from -240 to 240, as said below
- image_tokens: bfloat16 [32, 192, 8192], P('dp', 'section'), may hold values from -6 to 6
- key_weight: bfloat16 [8, 8192, 512], P('section'), may hold values from -0.0625 to 0.0625
- value_weight: bfloat16 [8, 8192, 512], P('section'), may hold values from -0.0625 to 0.0625
- cotangent: bfloat16 [8, 32, 128, 4096], P('section', 'dp'), may hold values from -6 to 6
- tile_counts: int32 [32], P('dp'), may hold values from 1 to 4
- text_lengths: int32 [32], P('dp'), may hold values from 32 to 128, as said below
Outputs:
- query_gradient: bfloat16 [8, 32, 128, 4096], P('section', 'dp')
- image_grad: bfloat16 [32, 192, 8192], P('dp', 'section')
- key_weight_grad: bfloat16 [8, 8192, 512], P('section', 'dp')
- value_weight_grad: bfloat16 [8, 8192, 512], P('section', 'dp')
Inputs may be any that keep to these rules, and one draw needn't show every extreme that they name: queries of one row share one scale. `text_lengths`: the live text tokens of a sample come first.
All inputs are finite; a program needn't handle non-finite values.
Results may differ from a plain program's by a relative error of at most 0.025.
The roundings to bfloat16 on the way count: a program that leaves them out, or rounds other values in their place, can miss the bound.
Values may be sent and summed in bfloat16 or wider, within the bound.
A program may use at most 192 MiB of HBM per device.

v0:
```python
import math

import jax
import jax.numpy as jnp
from jax import lax
from jax.sharding import PartitionSpec as P

QUERY_HEADS = 32
KEY_VALUE_HEADS = 4
HEAD_SIZE = 128
MAX_TILES = 4


def attend_one(queries, key_rows, value_rows, cotangent, key_limit, row_limit):
    total_rows = queries.shape[0]
    total_keys = key_rows.shape[0]
    group_width = QUERY_HEADS // KEY_VALUE_HEADS
    heads_of_queries = queries.reshape(total_rows, KEY_VALUE_HEADS, group_width, HEAD_SIZE)
    heads_of_keys = key_rows.reshape(total_keys, KEY_VALUE_HEADS, HEAD_SIZE)
    heads_of_values = value_rows.reshape(total_keys, KEY_VALUE_HEADS, HEAD_SIZE)
    row_live = (jnp.arange(total_rows) < row_limit)[:, None]
    active_cotangent = jnp.where(row_live, cotangent, jnp.zeros_like(cotangent))
    head_gradient = active_cotangent.reshape(total_rows, KEY_VALUE_HEADS, group_width, HEAD_SIZE)
    scaling = 1.0 / math.sqrt(HEAD_SIZE)
    scores = (
        jnp.einsum(
            "lhgd,nhd->hgln", heads_of_queries, heads_of_keys, preferred_element_type=jnp.float32
        )
        * scaling
    )
    key_live = jnp.arange(total_keys) < key_limit
    scores = jnp.where(key_live, scores, -jnp.inf)
    row_max = jnp.max(scores, axis=-1, keepdims=True)
    raised = jnp.exp(scores - row_max)
    weights = raised / jnp.sum(raised, axis=-1, keepdims=True)
    weights_low = weights.astype(jnp.bfloat16)
    value_gradient = jnp.einsum(
        "hgln,lhgd->nhd", weights_low, head_gradient, preferred_element_type=jnp.float32
    ).astype(jnp.bfloat16)
    prob_grad = jnp.einsum(
        "lhgd,nhd->hgln", head_gradient, heads_of_values, preferred_element_type=jnp.float32
    )
    row_dot = jnp.sum(weights * prob_grad, axis=-1, keepdims=True)
    score_grad = (weights * (prob_grad - row_dot) * scaling).astype(jnp.bfloat16)
    query_gradient = jnp.einsum(
        "hgln,nhd->lhgd", score_grad, heads_of_keys, preferred_element_type=jnp.float32
    ).astype(jnp.bfloat16)
    key_gradient = jnp.einsum(
        "hgln,lhgd->nhd", score_grad, heads_of_queries, preferred_element_type=jnp.float32
    ).astype(jnp.bfloat16)
    return (
        query_gradient.reshape(total_rows, QUERY_HEADS * HEAD_SIZE),
        key_gradient.reshape(total_keys, KEY_VALUE_HEADS * HEAD_SIZE),
        value_gradient.reshape(total_keys, KEY_VALUE_HEADS * HEAD_SIZE),
    )


def project(tokens, weight):
    return jnp.dot(tokens, weight, preferred_element_type=jnp.float32).astype(jnp.bfloat16)


def shards(queries, image_tokens, key_weight, value_weight, cotangent, tile_counts, text_lengths):
    gathered = lax.all_gather(image_tokens, "section", axis=1, tiled=True)
    samples_here = gathered.shape[0]
    image_len = gathered.shape[1]
    model_width = gathered.shape[2]
    tile_len = image_len // MAX_TILES
    w_key = key_weight[0]
    w_value = value_weight[0]
    query_local = queries[0]
    cotan_local = cotangent[0]
    query_list = []
    key_list = []
    value_list = []
    flat_tokens = gathered.reshape(samples_here * image_len, model_width)
    keys_all = project(flat_tokens, w_key).reshape(samples_here, image_len, -1)
    values_all = project(flat_tokens, w_value).reshape(samples_here, image_len, -1)
    for sample_index in range(samples_here):
        query_gradient, key_gradient, value_gradient = attend_one(
            query_local[sample_index],
            keys_all[sample_index],
            values_all[sample_index],
            cotan_local[sample_index],
            tile_counts[sample_index] * tile_len,
            text_lengths[sample_index],
        )
        query_list.append(query_gradient)
        key_list.append(key_gradient)
        value_list.append(value_gradient)
    query_out = jnp.stack(query_list)[None]
    key_grads = jnp.stack(key_list)
    value_grads = jnp.stack(value_list)
    image_term = jnp.einsum("stk,dk->std", key_grads, w_key, preferred_element_type=jnp.float32)
    image_term = image_term + jnp.einsum(
        "stk,dk->std", value_grads, w_value, preferred_element_type=jnp.float32
    )
    image_out = lax.psum_scatter(
        image_term.astype(jnp.bfloat16), "section", scatter_dimension=1, tiled=True
    )
    key_term = jnp.einsum("std,stk->dk", gathered, key_grads, preferred_element_type=jnp.float32)
    value_term = jnp.einsum(
        "std,stk->dk", gathered, value_grads, preferred_element_type=jnp.float32
    )
    key_sum, value_sum = (
        lax.psum_scatter(
            key_term.astype(jnp.bfloat16), "dp", scatter_dimension=0, tiled=True
        ).astype(jnp.float32),
        lax.psum_scatter(
            value_term.astype(jnp.bfloat16), "dp", scatter_dimension=0, tiled=True
        ).astype(jnp.float32),
    )
    return (
        query_out,
        image_out,
        key_sum.astype(jnp.bfloat16)[None],
        value_sum.astype(jnp.bfloat16)[None],
    )


def solution(mesh):
    placed = (
        P("section", "dp", None, None),
        P("dp", "section", None),
        P("section", None, None),
        P("section", None, None),
        P("section", "dp", None, None),
        P("dp"),
        P("dp"),
    )
    return jax.shard_map(
        shards,
        mesh=mesh,
        in_specs=placed,
        out_specs=(
            P("section", "dp", None, None),
            P("dp", "section", None),
            P("section", "dp", None),
            P("section", "dp", None),
        ),
        check_vma=False,
    )
```

profile of v0, /device:TPU:38, one launch (start us, length us, event | category | flops | bytes accessed | tf_op | source)
XLA Modules:
  0.0 451.1 jit_solution(1482975594506760739)
XLA Ops:
  18.3 82.8 %all-gather.2.cloned.1.call-done = bf16[2,192,8192]{2,1,0:T(8,128)(2,1)} async-done(((bf16[2,24,8192]{2,1,0:T(8,128)(2,1)}), bf16[2,192,8192]{2,1,0:T(8,128)(2,1)}) %all-gather.2.cloned.1.call-update) | async-done | bytes 6291472 | tf_op jit(solution)/shard_map/all_gather | solution.py:63
  101.0 8.6 %fusion.44 = bf16[384,512]{1,0:T(8,128)(2,1)S(1)} fusion(bf16[384,8192]{1,0:T(8,128)(2,1)} %bitcast.203, bf16[1,8192,512]{2,1,0:T(8,128)(2,1)} %param.10), kind=kOutput, calls=%fused_computation.56 | convolution fusion | flops 3221422080 | bytes 15073280 | tf_op jit(solution)/shard_map/dot_general | solution.py:59
  109.8 8.6 %fusion.41 = bf16[384,512]{1,0:T(8,128)(2,1)S(1)} fusion(bf16[384,8192]{1,0:T(8,128)(2,1)} %bitcast.204, bf16[1,8192,512]{2,1,0:T(8,128)(2,1)} %param.9), kind=kOutput, calls=%fused_computation.55 | convolution fusion | flops 3221422080 | bytes 15073280 | tf_op jit(solution)/shard_map/dot_general | solution.py:59
  122.5 2.3 fusion.72
  124.8 3.7 fusion.116
  128.5 3.4 fusion.68
  131.9 6.6 %fusion.63 = bf16[192,4,128]{2,0,1:T(8,128)(2,1)} fusion(bf16[128,4,8,128]{0,3,2,1:T(8,128)(2,1)S(1)} %bitcast.215, f32[4,192,128,8]{2,1,3,0:T(8,128)} %fusion.72, f32[4,8,128,192]{2,3,1,0:T(8,128)} %get-tuple-element.29, f32[4,8,128]{2,1,0:T(8,128)S(1)} %get-tuple-element.28), kind=kOutput, calls=%fused_computation.65 | convolution fusion | flops 206934208 | bytes 7553024 | tf_op jit(solution)/shard_map/hgln,lhgd->nhd/dot_general | solution.py:48
  140.9 2.4 fusion.71
  143.2 2.7 fusion.121
  146.0 2.7 fusion.65
  148.7 5.7 %fusion.64 = bf16[192,4,128]{2,0,1:T(8,128)(2,1)S(1)} fusion(bf16[128,4,8,128]{0,3,2,1:T(8,128)(2,1)S(1)} %bitcast.213, f32[4,192,128,8]{2,1,3,0:T(8,128)} %fusion.71, f32[4,8,128,192]{2,3,1,0:T(8,128)} %get-tuple-element.31, f32[4,8,128]{2,1,0:T(8,128)S(1)} %get-tuple-element.30), kind=kOutput, calls=%fused_computation.66 | convolution fusion | flops 206934208 | bytes 7553024 | tf_op jit(solution)/shard_map/hgln,lhgd->nhd/dot_general | solution.py:48
  155.1 11.8 %fusion.7 = f32[2,192,8192]{2,1,0:T(8,128)} fusion(bf16[2,192,512]{2,1,0:T(8,128)(2,1)S(1)} %constant_dynamic-update-slice_fusion, bf16[1,8192,512]{2,1,0:T(8,128)(2,1)} %param.9), kind=kOutput, calls=%fused_computation.10 | convolution fusion | flops 3221225472 | bytes 21364736 | tf_op jit(solution)/shard_map/stk,dk->std/dot_general | solution.py:93
  166.9 12.6 %add_convert_fusion = bf16[2,192,8192]{2,1,0:T(8,128)(2,1)} fusion(f32[2,192,8192]{2,1,0:T(8,128)} %fusion.7, bf16[2,192,512]{2,1,0:T(8,128)(2,1)S(1)} %constant_dynamic-update-slice_fusion.2, bf16[1,8192,512]{2,1,0:T(8,128)(2,1)} %param.10), kind=kOutput, calls=%fused_computation.6 | convolution fusion | flops 3227516928 | bytes 27656192 | tf_op jit(solution)/shard_map/stk,dk->std/dot_general | solution.py:94
  179.5 11.1 %copy.93 = bf16[2,192,8192]{2,0,1:T(2,128)(2,1)S(1)} copy(bf16[2,192,8192]{2,1,0:T(8,128)(2,1)} %add_convert_fusion) | data formatting | bytes 12582912
  190.6 6.9 %copy.99 = bf16[24,8,2,8192]{3,1,2,0:T(8,128)(2,1)} copy(bf16[24,8,2,8192]{3,2,1,0:T(2,128)(2,1)S(1)} %bitcast.206) | data formatting | bytes 12582912
  197.6 9.5 %fusion.4 = bf16[8192,512]{0,1:T(8,128)(2,1)} fusion(bf16[2,192,512]{2,1,0:T(8,128)(2,1)S(1)} %constant_dynamic-update-slice_fusion, bf16[2,192,8192]{2,1,0:T(8,128)(2,1)} %all-gather.2.cloned.1.call-done), kind=kOutput, calls=%fused_computation.7 | convolution fusion | flops 3225419776 | bytes 15073280 | tf_op jit(solution)/shard_map/std,stk->dk/dot_general | solution.py:100
  207.2 9.7 %fusion.5 = bf16[8192,512]{0,1:T(8,128)(2,1)} fusion(bf16[2,192,512]{2,1,0:T(8,128)(2,1)S(1)} %constant_dynamic-update-slice_fusion.2, bf16[2,192,8192]{2,1,0:T(8,128)(2,1)} %all-gather.2.cloned.1.call-done), kind=kOutput, calls=%fused_computation.8 | convolution fusion | flops 3225419776 | bytes 15073280 | tf_op jit(solution)/shard_map/std,stk->dk/dot_general | solution.py:101
  217.8 6.1 %convolution_convert_fusion = bf16[4,128,8,128]{3,1,2,0:T(8,128)(2,1)S(1)} fusion(f32[4,192,128,8]{2,1,3,0:T(8,128)} %fusion.72, bf16[192,4,128,1]{2,1,0,3:T(4,128)(2,1)S(1)} %bitcast.225, f32[4,8,128,192]{2,3,1,0:T(8,128)} %get-tuple-element.29, f32[4,8,128]{2,1,0:T(8,128)S(1)} %copy-done.7), kind=kOutput, calls=%fused_computation.49 | convolution fusion | flops 207360192 | bytes 7553024 | tf_op jit(solution)/shard_map/hgln,nhd->lhgd/dot_general | solution.py:45
  224.4 6.4 %convolution_convert_fusion.1 = bf16[4,128,8,128]{3,1,2,0:T(8,128)(2,1)S(1)} fusion(f32[4,192,128,8]{2,1,3,0:T(8,128)} %fusion.71, bf16[192,4,128,1]{2,1,0,3:T(4,128)(2,1)S(1)} %bitcast.223, f32[4,8,128,192]{2,3,1,0:T(8,128)} %get-tuple-element.31, f32[4,8,128]{2,1,0:T(8,128)S(1)} %get-tuple-element.30), kind=kOutput, calls=%fused_computation.50 | convolution fusion | flops 207360192 | bytes 7553024 | tf_op jit(solution)/shard_map/hgln,nhd->lhgd/dot_general | solution.py:45
  232.9 62.0 %reduce-scatter.10.cloned.1.call-done = bf16[24,16384]{1,0:T(8,128)(2,1)} async-done(((bf16[192,16384]{1,0:T(8,128)(2,1)}), bf16[24,16384]{1,0:T(8,128)(2,1)}) %reduce-scatter.10.cloned.1.call-update) | async-done | bytes 786448
  294.9 2.6 reshape.77
  298.8 68.0 %reduce-scatter.6.cloned.1.call-done = bf16[512,512]{0,1:T(8,128)(2,1)} async-done(((bf16[8192,512]{0,1:T(8,128)(2,1)}), bf16[512,512]{0,1:T(8,128)(2,1)}) %reduce-scatter.6.cloned.1.call-update) | async-done | bytes 524304 | tf_op jit(solution)/shard_map/reduce_scatter | solution.py:105
  366.8 2.0 copy.65
  368.8 73.7 %reduce-scatter.8.cloned.1.call-done = bf16[512,512]{0,1:T(8,128)(2,1)} async-done(((bf16[8192,512]{0,1:T(8,128)(2,1)}), bf16[512,512]{0,1:T(8,128)(2,1)}) %reduce-scatter.8.cloned.1.call-update) | async-done | bytes 524304 | tf_op jit(solution)/shard_map/reduce_scatter | solution.py:108
  (59 shorter events, 24.0 us)
Async XLA Ops:
  7.2 93.9 %all-gather.2.cloned.1.call-start = ((), (), s32[]{:S(2)}) async-start(), calls=%async_computation.3 | async-start | bytes 7077888 | tf_op jit(solution)/shard_map/all_gather | solution.py:63
  7.9 287.0 %reduce-scatter.10.cloned.1.call-start = ((), (), s32[]{:S(2)}) async-start(), calls=%async_computation.6 | async-start | bytes 7077888
  13.6 2.0 copy-start
  15.7 0.7 copy-start.5
  118.4 6.4 %copy-start.2 = (bf16[1,1,128,4096]{2,3,1,0:T(8,128)(2,1)S(1)}, bf16[1,1,128,4096]{2,3,1,0:T(8,128)(2,1)}, u32[]{:S(2)}) copy-start(bf16[1,1,128,4096]{2,3,1,0:T(8,128)(2,1)} %copy.96) | copy-start | bytes 3145732
  128.5 3.4 copy-start.6
  138.4 4.8 %copy-start.1 = (bf16[1,1,128,4096]{2,3,1,0:T(8,128)(2,1)S(1)}, bf16[1,1,128,4096]{2,3,1,0:T(8,128)(2,1)}, u32[]{:S(2)}) copy-start(bf16[1,1,128,4096]{2,3,1,0:T(8,128)(2,1)} %copy.95) | copy-start | bytes 3145732
  138.4 4.8 %copy-start.3 = (bf16[192,4,128]{2,1,0:T(4,128)(2,1)S(1)}, bf16[192,4,128]{2,1,0:T(4,128)(2,1)}, u32[]{:S(2)}) copy-start(bf16[192,4,128]{2,1,0:T(4,128)(2,1)} %reshape_squeeze.18) | copy-start | bytes 589828
  197.5 169.3 %reduce-scatter.6.cloned.1.call-start = ((), (), s32[]{:S(2)}) async-start(), calls=%async_computation.4 | async-start | bytes 8912896 | tf_op jit(solution)/shard_map/reduce_scatter | solution.py:105
  207.1 235.4 %reduce-scatter.8.cloned.1.call-start = ((), (), s32[]{:S(2)}) async-start(), calls=%async_computation.5 | async-start | bytes 8912896 | tf_op jit(solution)/shard_map/reduce_scatter | solution.py:108
  216.9 0.9 copy-start.4
  216.9 0.9 copy-start.7
Sparse Core Ops, SparseCore 0:
  10.3 90.7 all-gather.1
  197.6 97.2 reduce-scatter.9
  297.4 69.2 reduce-scatter.5
  369.2 73.3 reduce-scatter.7
where the time goes:
time: 457 us; the launch traced here: 451 us
  waiting for transfers between devices  287 us (63%)
  matrix products  103 us (23%)
  local copies, waits for them, and re-layouts  42.9 us (9%)
  between operations  15.3 us (3%)
    all_gather x1, waiting for transfers between devices, shards(): gathered = lax.all_gather(image_tokens, 'section', axis=1, tiled=True)  82.8 us
    reduce_scatter x1, waiting for transfers between devices, shards(): lax.psum_scatter(value_term.astype(jnp.bfloat16), 'dp', scatter_dimension...  73.7 us
    reduce_scatter x1, waiting for transfers between devices, shards(): lax.psum_scatter(key_term.astype(jnp.bfloat16), 'dp', scatter_dimension=0...  68 us
    unnamed x5, waiting for transfers between devices  62.7 us
    unnamed x29, local copies, waits for them, and re-layouts  30.9 us
    dot_general x2, matrix products, project(): jnp.dot(tokens, weight, preferred_element_type=jnp.float32)  17.2 us
    dot_general x1, matrix products, shards(): jnp.einsum('stk,dk->std', value_grads, w_value, preferred_element_type=jn...  12.6 us
    dot_general x2, matrix products, attend_one(): jnp.einsum('hgln,nhd->lhgd', score_grad, heads_of_keys, preferred_element...  12.5 us
  transfers between devices with their start and end apart: 4, of which 4 were waited for; matrix products, arithmetic and copies ran while one was open for 11% of the time, Pallas kernels for 0%

commit v1 on v0

--- a/solution.py
+++ b/solution.py
@@ -1,14 +1,18 @@
+import functools
 import math
 
 import jax
 import jax.numpy as jnp
 from jax import lax
+from jax.experimental import pallas as pl
+from jax.experimental.pallas import tpu as pltpu
 from jax.sharding import PartitionSpec as P
 
 QUERY_HEADS = 32
 KEY_VALUE_HEADS = 4
 HEAD_SIZE = 128
 MAX_TILES = 4
+MESH_ID = pl.DeviceIdType.MESH
 
 
 def attend_one(queries, key_rows, value_rows, cotangent, key_limit, row_limit):
@@ -55,15 +59,61 @@
     )
 
 
-def project(tokens, weight):
-    return jnp.dot(tokens, weight, preferred_element_type=jnp.float32).astype(jnp.bfloat16)
+def exchange_kernel(n, scatter, x_ref, o_ref, send_sems, recv_sems, local_sem):
+    me = lax.axis_index("section")
+    row = lax.axis_index("dp")
+    barrier = pltpu.get_barrier_semaphore()
+    for k in range(1, n):
+        pl.semaphore_signal(
+            barrier, inc=1, device_id=(lax.rem(me + k, n), row), device_id_type=MESH_ID
+        )
+    pl.semaphore_wait(barrier, n - 1)
+    own = x_ref.at[:, me] if scatter else x_ref
+    local = pltpu.make_async_copy(own, o_ref.at[:, me], local_sem)
+    local.start()
+    copies = []
+    for k in range(1, n):
+        peer = lax.rem(me + k, n)
+        src = x_ref.at[:, peer] if scatter else x_ref
+        copy = pltpu.make_async_remote_copy(
+            src_ref=src,
+            dst_ref=o_ref.at[:, me],
+            send_sem=send_sems.at[k],
+            recv_sem=recv_sems.at[k],
+            device_id=(peer, row),
+            device_id_type=MESH_ID,
+        )
+        copy.start()
+        copies.append(copy)
+    for copy in copies:
+        copy.wait()
+    local.wait()
+
+
+def exchange(x, n, scatter, collective_id):
+    if scatter:
+        out_shape = x.shape
+    else:
+        out_shape = (x.shape[0], n) + x.shape[1:]
+    return pl.pallas_call(
+        functools.partial(exchange_kernel, n, scatter),
+        out_shape=jax.ShapeDtypeStruct(out_shape, x.dtype),
+        in_specs=[pl.BlockSpec(memory_space=pl.ANY)],
+        out_specs=pl.BlockSpec(memory_space=pl.ANY),
+        scratch_shapes=[
+            pltpu.SemaphoreType.DMA((n,)),
+            pltpu.SemaphoreType.DMA((n,)),
+            pltpu.SemaphoreType.DMA(()),
+        ],
+        compiler_params=pltpu.CompilerParams(collective_id=collective_id, has_side_effects=True),
+    )(x)
 
 
 def shards(queries, image_tokens, key_weight, value_weight, cotangent, tile_counts, text_lengths):
-    gathered = lax.all_gather(image_tokens, "section", axis=1, tiled=True)
-    samples_here = gathered.shape[0]
-    image_len = gathered.shape[1]
-    model_width = gathered.shape[2]
+    n_section = lax.axis_size("section")
+    samples_here, chunk, model_width = image_tokens.shape
+    gathered = exchange(image_tokens, n_section, False, 0)
+    image_len = n_section * chunk
     tile_len = image_len // MAX_TILES
     w_key = key_weight[0]
     w_value = value_weight[0]
@@ -72,9 +122,12 @@
     query_list = []
     key_list = []
     value_list = []
-    flat_tokens = gathered.reshape(samples_here * image_len, model_width)
-    keys_all = project(flat_tokens, w_key).reshape(samples_here, image_len, -1)
-    values_all = project(flat_tokens, w_value).reshape(samples_here, image_len, -1)
+    keys_all = jnp.einsum(
+        "bjtd,dk->bjtk", gathered, w_key, preferred_element_type=jnp.float32
+    ).astype(jnp.bfloat16).reshape(samples_here, image_len, -1)
+    values_all = jnp.einsum(
+        "bjtd,dk->bjtk", gathered, w_value, preferred_element_type=jnp.float32
+    ).astype(jnp.bfloat16).reshape(samples_here, image_len, -1)
     for sample_index in range(samples_here):
         query_gradient, key_gradient, value_gradient = attend_one(
             query_local[sample_index],
@@ -88,32 +141,27 @@
         key_list.append(key_gradient)
         value_list.append(value_gradient)
     query_out = jnp.stack(query_list)[None]
-    key_grads = jnp.stack(key_list)
-    value_grads = jnp.stack(value_list)
-    image_term = jnp.einsum("stk,dk->std", key_grads, w_key, preferred_element_type=jnp.float32)
+    key_grads = jnp.stack(key_list).reshape(samples_here, n_section, chunk, -1)
+    value_grads = jnp.stack(value_list).reshape(samples_here, n_section, chunk, -1)
+    kv_grads = jnp.concatenate([key_grads, value_grads], axis=-1)
+    kv_term = jnp.einsum(
+        "bjtd,bjtk->dk", gathered, kv_grads, preferred_element_type=jnp.float32
+    )
+    kv_sum = lax.psum_scatter(kv_term.astype(jnp.bfloat16), "dp", scatter_dimension=0, tiled=True)
+    kv_width = key_grads.shape[-1]
+    image_term = jnp.einsum(
+        "bjtk,dk->bjtd", key_grads, w_key, preferred_element_type=jnp.float32
+    )
     image_term = image_term + jnp.einsum(
-        "stk,dk->std", value_grads, w_value, preferred_element_type=jnp.float32
+        "bjtk,dk->bjtd", value_grads, w_value, preferred_element_type=jnp.float32
     )
-    image_out = lax.psum_scatter(
-        image_term.astype(jnp.bfloat16), "section", scatter_dimension=1, tiled=True
-    )
-    key_term = jnp.einsum("std,stk->dk", gathered, key_grads, preferred_element_type=jnp.float32)
-    value_term = jnp.einsum(
-        "std,stk->dk", gathered, value_grads, preferred_element_type=jnp.float32
-    )
-    key_sum, value_sum = (
-        lax.psum_scatter(
-            key_term.astype(jnp.bfloat16), "dp", scatter_dimension=0, tiled=True
-        ).astype(jnp.float32),
-        lax.psum_scatter(
-            value_term.astype(jnp.bfloat16), "dp", scatter_dimension=0, tiled=True
-        ).astype(jnp.float32),
-    )
+    received = exchange(image_term.astype(jnp.bfloat16), n_section, True, 1)
+    image_out = jnp.sum(received.astype(jnp.float32), axis=1).astype(jnp.bfloat16)
     return (
         query_out,
         image_out,
-        key_sum.astype(jnp.bfloat16)[None],
-        value_sum.astype(jnp.bfloat16)[None],
+        kv_sum[:, :kv_width][None],
+        kv_sum[:, kv_width:][None],
     )
 
 

time: 457 us -> 376 us (0.82)
  waiting for transfers between devices: 287 us -> 0.02 us
  Pallas kernels: 0 us -> 229 us
  local copies, waits for them, and re-layouts: 42.9 us -> 20.5 us
  other arithmetic: 2.82 us -> 7.57 us
    pallas_call x0 -> x2, Pallas kernels: none -> 229 us  [exchange(): pl.pallas_call(functools.partial(exchange_kernel, n, scatter), out_shape=...]
    reduce_scatter x2 -> x1, waiting for transfers between devices: 142 us -> 0.01 us  [shards(): lax.psum_scatter(kv_term.astype(jnp.bfloat16), 'dp', scatter_dimension=0,...]
    all_gather x1 -> x0, waiting for transfers between devices: 82.8 us -> none  [shards(): gathered = lax.all_gather(image_tokens, 'section', axis=1, tiled=True)]
    unnamed x5 -> x1, waiting for transfers between devices: 62.7 us -> 0.02 us
    unnamed x29 -> x27, local copies, waits for them, and re-layouts: 30.9 us -> 7.63 us
    reduce_sum x0 -> x1, other arithmetic: none -> 4.75 us  [shards(): jnp.sum(received.astype(jnp.float32), axis=1).astype(jnp.bfloat16)]
    dot_general x6 -> x5, matrix products: 60.8 us -> 57 us  [the longest x1 15.2 us: shards(): jnp.einsum('bjtd,bjtk->dk', gathered, kv_grads, preferred_element_type=jn...]
  transfers between devices with their start and end apart: 4 -> 1, of which waited for: 4 -> 0; matrix products, arithmetic and copies ran while one was open for 11% -> 12% of each run, Pallas kernels for 0% -> 33%
where the time goes in v1:
time: 376 us; the launch traced here: 371 us
  Pallas kernels  229 us (61%)
  matrix products  98.5 us (26%)
  local copies, waits for them, and re-layouts  20.5 us (5%)
  between operations  15.6 us (4%)
  other arithmetic  7.57 us (2%)
    pallas_call x2, Pallas kernels, exchange(): pl.pallas_call(functools.partial(exchange_kernel, n, scatter), out_shape=...  229 us
    dot_general x1, matrix products, shards(): jnp.einsum('bjtd,bjtk->dk', gathered, kv_grads, preferred_element_type=jn...  15.2 us
    dot_general x1, matrix products, shards(): jnp.einsum('bjtk,dk->bjtd', value_grads, w_value, preferred_element_type=...  12.9 us
    dot_general x2, matrix products, attend_one(): jnp.einsum('hgln,lhgd->nhd', score_grad, heads_of_queries, preferred_elem...  12.4 us
    dot_general x2, matrix products, attend_one(): jnp.einsum('hgln,nhd->lhgd', score_grad, heads_of_keys, preferred_element...  11.9 us
    dot_general x1, matrix products, shards(): jnp.einsum('bjtk,dk->bjtd', key_grads, w_key, preferred_element_type=jnp....  11.7 us
    dot_general x1, matrix products, shards(): jnp.einsum('bjtd,dk->bjtk', gathered, w_key, preferred_element_type=jnp.f...  8.62 us
    dot_general x1, matrix products, shards(): jnp.einsum('bjtd,dk->bjtk', gathered, w_value, preferred_element_type=jnp...  8.61 us
  transfers between devices with their start and end apart: 1, of which 0 were waited for; matrix products, arithmetic and copies ran while one was open for 12% of the time, Pallas kernels for 33%

profile of v1, /device:TPU:38, one launch (start us, length us, event | category | flops | bytes accessed | tf_op | source)
XLA Modules:
  0.0 371.5 jit_solution(9881685545965908826)
XLA Ops:
  9.9 1.3 fusion.118
  12.5 1.7 fusion.114
  14.2 1.3 copy.76
  18.1 106.6 %shard_map.102 = bf16[2,8,24,8192]{3,2,1,0:T(8,128)(2,1)} custom-call(bf16[2,24,8192]{2,1,0:T(8,128)(2,1)} %x_ref.1), custom_call_target="tpu_custom_call" | custom-call | tf_op jit(solution)/shard_map/pallas_call | solution.py:98
  124.7 8.6 %fusion.43 = bf16[2,8,24,512]{3,2,1,0:T(8,128)(2,1)S(1)} fusion(bf16[2,8,24,8192]{3,2,1,0:T(8,128)(2,1)} %shard_map.102, bf16[1,8192,512]{2,1,0:T(8,128)(2,1)} %param.10), kind=kOutput, calls=%fused_computation.54 | convolution fusion | flops 3221422080 | bytes 15073280 | tf_op jit(solution)/shard_map/bjtd,dk->bjtk/dot_general | solution.py:128
  133.4 8.6 %fusion.40 = bf16[2,8,24,512]{3,2,1,0:T(8,128)(2,1)S(1)} fusion(bf16[2,8,24,8192]{3,2,1,0:T(8,128)(2,1)} %shard_map.102, bf16[1,8192,512]{2,1,0:T(8,128)(2,1)} %param.9), kind=kOutput, calls=%fused_computation.53 | convolution fusion | flops 3221422080 | bytes 15073280 | tf_op jit(solution)/shard_map/bjtd,dk->bjtk/dot_general | solution.py:125
  142.9 1.6 reshape_squeeze.18
  144.5 1.7 reshape_squeeze.21
  146.2 2.3 fusion.74
  148.4 4.3 %fusion.119 = (f32[4,8,128]{2,1,0:T(8,128)}, f32[4,8,128,192]{2,3,1,0:T(8,128)}) fusion(pred[192]{0:T(512)(128)(4,1)S(1)} %iota_compare_fusion, bf16[128,4,8,128]{0,3,2,1:T(8,128)(2,1)S(1)} %bitcast.213, bf16[192,4,128,1]{2,1,0,3:T(4,128)(2,1)} %bitcast.221), kind=kOutput, calls=%fused_computation.120 | convolution fusion | flops 204472512 | bytes 4407488 | tf_op jit(solution)/shard_map/sub | solution.py:38
  152.7 2.7 fusion.67
  155.4 6.5 %fusion.62 = bf16[192,4,128]{2,0,1:T(8,128)(2,1)} fusion(bf16[128,4,8,128]{0,3,2,1:T(8,128)(2,1)S(1)} %bitcast.214, f32[4,192,128,8]{2,1,3,0:T(8,128)} %fusion.74, f32[4,8,128,192]{2,3,1,0:T(8,128)} %get-tuple-element.27, f32[4,8,128]{2,1,0:T(8,128)} %get-tuple-element.26), kind=kOutput, calls=%fused_computation.63 | convolution fusion | flops 206934208 | bytes 7553024 | tf_op jit(solution)/shard_map/hgln,lhgd->nhd/dot_general | solution.py:52
  163.5 2.4 fusion.73
  165.8 2.8 fusion.124
  168.6 2.9 fusion.64
  171.5 5.9 %fusion.63 = bf16[192,4,128]{2,0,1:T(8,128)(2,1)S(1)} fusion(bf16[128,4,8,128]{0,3,2,1:T(8,128)(2,1)S(1)} %bitcast.212, f32[4,192,128,8]{2,1,3,0:T(8,128)} %fusion.73, f32[4,8,128,192]{2,3,1,0:T(8,128)} %get-tuple-element.29, f32[4,8,128]{2,1,0:T(8,128)S(1)} %get-tuple-element.28), kind=kOutput, calls=%fused_computation.64 | convolution fusion | flops 206934208 | bytes 7553024 | tf_op jit(solution)/shard_map/hgln,lhgd->nhd/dot_general | solution.py:52
  178.7 15.2 %fusion.4 = bf16[8192,1024]{0,1:T(8,128)(2,1)} fusion(bf16[2,8,24,8192]{3,2,1,0:T(8,128)(2,1)} %shard_map.102, bf16[2,8,24,512]{3,2,1,0:T(8,128)(2,1)S(1)} %get-tuple-element.31, bf16[2,8,24,512]{3,2,1,0:T(8,128)(2,1)S(1)} %get-tuple-element.30), kind=kOutput, calls=%fused_computation.5 | convolution fusion | flops 6452412416 | bytes 23855104 | tf_op jit(solution)/shard_map/bjtd,bjtk->dk/dot_general | solution.py:147
  194.8 5.9 %convolution_convert_fusion = bf16[4,128,8,128]{3,1,2,0:T(8,128)(2,1)S(1)} fusion(f32[4,192,128,8]{2,1,3,0:T(8,128)} %fusion.74, bf16[192,4,128,1]{2,1,0,3:T(4,128)(2,1)S(1)} %bitcast.222, f32[4,8,128,192]{2,3,1,0:T(8,128)} %get-tuple-element.27, f32[4,8,128]{2,1,0:T(8,128)S(1)} %copy-done.6), kind=kOutput, calls=%fused_computation.47 | convolution fusion | flops 207360192 | bytes 7553024 | tf_op jit(solution)/shard_map/hgln,nhd->lhgd/dot_general | solution.py:49
  201.2 6.0 %convolution_convert_fusion.1 = bf16[4,128,8,128]{3,1,2,0:T(8,128)(2,1)S(1)} fusion(f32[4,192,128,8]{2,1,3,0:T(8,128)} %fusion.73, bf16[192,4,128,1]{2,1,0,3:T(4,128)(2,1)} %bitcast.219, f32[4,8,128,192]{2,3,1,0:T(8,128)} %get-tuple-element.29, f32[4,8,128]{2,1,0:T(8,128)S(1)} %copy-done.8), kind=kOutput, calls=%fused_computation.48 | convolution fusion | flops 207360192 | bytes 7553024 | tf_op jit(solution)/shard_map/hgln,nhd->lhgd/dot_general | solution.py:49
  207.8 11.7 %fusion.8 = f32[2,8,24,8192]{3,2,1,0:T(8,128)} fusion(bf16[2,8,24,512]{3,2,1,0:T(8,128)(2,1)} %copy-done.3, bf16[1,8192,512]{2,1,0:T(8,128)(2,1)} %param.9), kind=kOutput, calls=%fused_computation.10 | convolution fusion | flops 3221225472 | bytes 21364736 | tf_op jit(solution)/shard_map/bjtk,dk->bjtd/dot_general | solution.py:152
  219.5 12.9 %add_convert_fusion.x_ref = bf16[2,8,24,8192]{3,2,1,0:T(8,128)(2,1)} fusion(f32[2,8,24,8192]{3,2,1,0:T(8,128)} %fusion.8, bf16[2,8,24,512]{3,2,1,0:T(8,128)(2,1)S(1)} %get-tuple-element.31, bf16[1,8192,512]{2,1,0:T(8,128)(2,1)} %param.10), kind=kOutput, calls=%fused_computation.6 | convolution fusion | flops 3227516928 | bytes 27656192 | tf_op jit(solution)/shard_map/bjtk,dk->bjtd/dot_general | solution.py:155
  232.4 122.7 %shard_map.103 = bf16[2,8,24,8192]{3,2,1,0:T(8,128)(2,1)} custom-call(bf16[2,8,24,8192]{3,2,1,0:T(8,128)(2,1)} %add_convert_fusion.x_ref), custom_call_target="tpu_custom_call" | custom-call | tf_op jit(solution)/shard_map/pallas_call | solution.py:98
  355.1 4.8 %reduce_sum.52 = bf16[2,24,8192]{2,1,0:T(8,128)(2,1)} reduce(bf16[2,8,24,8192]{3,2,1,0:T(8,128)(2,1)} %shard_map.103, bf16[]{:T(256)} %constant.12.clone.1), dimensions={1}, to_apply=%region_6.7 | reduce | flops 2752512 | bytes 7077890 | tf_op jit(solution)/shard_map/reduce_sum | solution.py:159
  359.8 1.5 maximum_bitcast_fusion
  (50 shorter events, 14.2 us)
Async XLA Ops:
  7.2 354.2 %reduce-scatter.2.cloned.1.call-start = ((), (), s32[]{:S(2)}) async-start(), calls=%async_computation.1 | async-start | bytes 17825792 | tf_op jit(solution)/shard_map/reduce_scatter | solution.py:150
  15.5 2.0 copy-start
  142.1 6.4 %copy-start.2 = (bf16[1,1,128,4096]{2,3,1,0:T(8,128)(2,1)S(1)}, bf16[1,1,128,4096]{2,3,1,0:T(8,128)(2,1)}, u32[]{:S(2)}) copy-start(bf16[1,1,128,4096]{2,3,1,0:T(8,128)(2,1)} %copy.77) | copy-start | bytes 3145732
  161.9 3.9 %copy-start.1 = (bf16[1,1,128,4096]{2,3,1,0:T(8,128)(2,1)S(1)}, bf16[1,1,128,4096]{2,3,1,0:T(8,128)(2,1)}, u32[]{:S(2)}) copy-start(bf16[1,1,128,4096]{2,3,1,0:T(8,128)(2,1)} %copy.76) | copy-start | bytes 3145732
  161.9 3.9 %copy-start.4 = (bf16[192,4,128]{2,1,0:T(4,128)(2,1)S(1)}, bf16[192,4,128]{2,1,0:T(4,128)(2,1)}, u32[]{:S(2)}) copy-start(bf16[192,4,128]{2,1,0:T(4,128)(2,1)} %reshape_squeeze.18) | copy-start | bytes 589828
  168.6 2.9 copy-start.7
  177.9 0.7 copy-start.3
  193.8 0.9 copy-start.5
  193.8 0.9 copy-start.6
  194.8 6.4 %copy-start.8 = (f32[4,8,128]{2,1,0:T(8,128)S(1)}, f32[4,8,128]{2,1,0:T(8,128)}, u32[]{:S(2)}) copy-start(f32[4,8,128]{2,1,0:T(8,128)} %copy-done.7) | copy-start | bytes 49156
Sparse Core Ops, SparseCore 0:
  194.0 140.1 reduce-scatter.1

commit v2 on v1

--- a/solution.py
+++ b/solution.py
@@ -107,6 +107,27 @@
         ],
         compiler_params=pltpu.CompilerParams(collective_id=collective_id, has_side_effects=True),
     )(x)
+
+
+def chip_then_core_scatter(term):
+    n_dp = lax.axis_size("dp")
+    rows, width = term.shape
+    me = lax.axis_index("dp")
+    core = lax.rem(me, 2)
+    chunks = term.reshape(n_dp // 2, 2, rows // n_dp, width)
+    mine = jnp.where(core == 0, chunks[:, 0], chunks[:, 1])
+    theirs = jnp.where(core == 0, chunks[:, 1], chunks[:, 0])
+    pairs = [(i, i ^ 1) for i in range(n_dp)]
+    arrived = lax.ppermute(theirs, "dp", perm=pairs)
+    paired = (mine.astype(jnp.float32) + arrived.astype(jnp.float32)).astype(jnp.bfloat16)
+    groups = [list(range(c, n_dp, 2)) for c in range(2)]
+    return lax.psum_scatter(
+        paired.reshape(rows // 2, width),
+        "dp",
+        scatter_dimension=0,
+        axis_index_groups=groups,
+        tiled=True,
+    )
 
 
 def shards(queries, image_tokens, key_weight, value_weight, cotangent, tile_counts, text_lengths):
@@ -147,7 +168,7 @@
     kv_term = jnp.einsum(
         "bjtd,bjtk->dk", gathered, kv_grads, preferred_element_type=jnp.float32
     )
-    kv_sum = lax.psum_scatter(kv_term.astype(jnp.bfloat16), "dp", scatter_dimension=0, tiled=True)
+    kv_sum = chip_then_core_scatter(kv_term.astype(jnp.bfloat16))
     kv_width = key_grads.shape[-1]
     image_term = jnp.einsum(
         "bjtk,dk->bjtd", key_grads, w_key, preferred_element_type=jnp.float32

time: 376 us -> 545 us (1.45)
  local copies, waits for them, and re-layouts: 20.5 us -> 163 us
  waiting for transfers between devices: 0.02 us -> 13.2 us
  other arithmetic: 7.57 us -> 19.6 us
    unnamed x27 -> x23, local copies, waits for them, and re-layouts: 7.63 us -> 82.8 us
    slice x0 -> x1, local copies, waits for them, and re-layouts: none -> 38.7 us  [chip_then_core_scatter(): mine = jnp.where(core == 0, chunks[:, 0], chunks[:, 1])]
    reshape x0 -> x1, local copies, waits for them, and re-layouts: none -> 27.7 us  [chip_then_core_scatter(): chunks = term.reshape(n_dp // 2, 2, rows // n_dp, width)]
    ppermute x0 -> x1, waiting for transfers between devices: none -> 13.1 us  [chip_then_core_scatter(): arrived = lax.ppermute(theirs, 'dp', perm=pairs)]
    convert_element_type x0 -> x1, other arithmetic: none -> 7.39 us  [chip_then_core_scatter(): (mine.astype(jnp.float32) + arrived.astype(jnp.float32)).astype(jnp.bfloa...]
  transfers between devices with their start and end apart: 1 -> 2, of which waited for: 0 -> 1; matrix products, arithmetic and copies ran while one was open for 12% -> 8% of each run, Pallas kernels for 33% -> 23%
where the time goes in v2:
time: 545 us; the launch traced here: 539 us
  Pallas kernels  228 us (42%)
  local copies, waits for them, and re-layouts  163 us (30%)
  matrix products  98.7 us (18%)
  other arithmetic  19.6 us (4%)
  between operations  15.5 us (3%)
  waiting for transfers between devices  13.2 us (2%)
    pallas_call x2, Pallas kernels, exchange(): pl.pallas_call(functools.partial(exchange_kernel, n, scatter), out_shape=...  228 us
    unnamed x23, local copies, waits for them, and re-layouts  82.8 us
    slice x1, local copies, waits for them, and re-layouts, chip_then_core_scatter(): mine = jnp.where(core == 0, chunks[:, 0], chunks[:, 1])  38.7 us
    reshape x1, local copies, waits for them, and re-layouts, chip_then_core_scatter(): chunks = term.reshape(n_dp // 2, 2, rows // n_dp, width)  27.7 us
    dot_general x1, matrix products, shards(): jnp.einsum('bjtd,bjtk->dk', gathered, kv_grads, preferred_element_type=jn...  15.4 us
    ppermute x1, waiting for transfers between devices, chip_then_core_scatter(): arrived = lax.ppermute(theirs, 'dp', perm=pairs)  13.1 us
    dot_general x1, matrix products, shards(): jnp.einsum('bjtk,dk->bjtd', value_grads, w_value, preferred_element_type=...  12.9 us
    dot_general x2, matrix products, attend_one(): jnp.einsum('hgln,nhd->lhgd', score_grad, heads_of_keys, preferred_element...  12.5 us
  transfers between devices with their start and end apart: 2, of which 1 were waited for; matrix products, arithmetic and copies ran while one was open for 8% of the time, Pallas kernels for 23%

profile of v2, /device:TPU:38, one launch (start us, length us, event | category | flops | bytes accessed | tf_op | source)
XLA Modules:
  0.0 538.6 jit_solution(1098009872220900466)
XLA Ops:
  10.4 106.6 %shard_map.102 = bf16[2,8,24,8192]{3,2,1,0:T(8,128)(2,1)} custom-call(bf16[2,24,8192]{2,1,0:T(8,128)(2,1)} %x_ref.1), custom_call_target="tpu_custom_call" | custom-call | tf_op jit(solution)/shard_map/pallas_call | solution.py:98
  117.0 8.6 %fusion.44 = bf16[2,8,24,512]{3,2,1,0:T(8,128)(2,1)S(1)} fusion(bf16[2,8,24,8192]{3,2,1,0:T(8,128)(2,1)} %shard_map.102, bf16[1,8192,512]{2,1,0:T(8,128)(2,1)} %param.10), kind=kOutput, calls=%fused_computation.57 | convolution fusion | flops 3221422080 | bytes 15073280 | tf_op jit(solution)/shard_map/bjtd,dk->bjtk/dot_general | solution.py:149
  126.4 8.6 %fusion.41 = bf16[2,8,24,512]{3,2,1,0:T(8,128)(2,1)S(1)} fusion(bf16[2,8,24,8192]{3,2,1,0:T(8,128)(2,1)} %shard_map.102, bf16[1,8192,512]{2,1,0:T(8,128)(2,1)} %param.9), kind=kOutput, calls=%fused_computation.56 | convolution fusion | flops 3221422080 | bytes 15073280 | tf_op jit(solution)/shard_map/bjtd,dk->bjtk/dot_general | solution.py:146
  137.7 2.7 fusion.116
  149.8 4.3 fusion.126
  154.0 2.7 fusion.65
  156.7 6.4 %fusion.64 = bf16[192,4,128]{2,0,1:T(8,128)(2,1)} fusion(bf16[128,4,8,128]{0,3,2,1:T(8,128)(2,1)S(1)} %bitcast.223, f32[4,192,128,8]{2,1,3,0:T(8,128)} %fusion.74, f32[4,8,128,192]{2,3,1,0:T(8,128)} %get-tuple-element.23, f32[4,8,128]{2,1,0:T(8,128)} %get-tuple-element.22), kind=kOutput, calls=%fused_computation.67 | convolution fusion | flops 206934208 | bytes 7553024 | tf_op jit(solution)/shard_map/hgln,lhgd->nhd/dot_general | solution.py:52
  166.8 2.7 fusion.121
  169.5 2.7 fusion.68
  172.2 5.7 %fusion.63 = bf16[192,4,128]{2,0,1:T(8,128)(2,1)S(1)} fusion(bf16[128,4,8,128]{0,3,2,1:T(8,128)(2,1)S(1)} %bitcast.221, f32[4,192,128,8]{2,1,3,0:T(8,128)} %fusion.75, f32[4,8,128,192]{2,3,1,0:T(8,128)} %get-tuple-element.21, f32[4,8,128]{2,1,0:T(8,128)S(1)} %get-tuple-element.20), kind=kOutput, calls=%fused_computation.66 | convolution fusion | flops 206934208 | bytes 7553024 | tf_op jit(solution)/shard_map/hgln,lhgd->nhd/dot_general | solution.py:52
  178.7 15.4 %fusion.5 = bf16[8192,1024]{0,1:T(8,128)(2,1)} fusion(bf16[2,8,24,8192]{3,2,1,0:T(8,128)(2,1)} %shard_map.102, bf16[2,8,24,512]{3,2,1,0:T(8,128)(2,1)S(1)} %get-tuple-element.25, bf16[2,8,24,512]{3,2,1,0:T(8,128)(2,1)S(1)} %get-tuple-element.24), kind=kOutput, calls=%fused_computation.7 | convolution fusion | flops 6452412416 | bytes 23855104 | tf_op jit(solution)/shard_map/bjtd,bjtk->dk/dot_general | solution.py:168
  194.2 27.7 %reshape.80 = bf16[8,2,512,1024]{2,1,0,3:T(2,128)(2,1)} reshape(bf16[8192,1024]{0,1:T(8,128)(2,1)} %fusion.5) | data formatting | bytes 33554432 | tf_op jit(solution)/shard_map/reshape | solution.py:117
  221.9 38.7 %fusion.115 = (bf16[8,1,512,1024]{2,1,0,3:T(2,128)(2,1)}, bf16[8,1,512,1024]{2,1,0,3:T(2,128)(2,1)}) fusion(bf16[8,2,512,1024]{2,1,0,3:T(2,128)(2,1)} %reshape.80), kind=kLoop, calls=%fused_computation.118 | loop fusion | bytes 33554432 | tf_op jit(solution)/shard_map/slice | solution.py:118
  260.5 38.9 %copy.82 = bf16[8,1,512,1024]{3,2,0,1:T(8,128)(2,1)} copy(bf16[8,1,512,1024]{2,1,0,3:T(2,128)(2,1)} %get-tuple-element.5) | data formatting | bytes 16777216
  299.4 38.7 %copy.81 = bf16[8,1,512,1024]{3,2,0,1:T(8,128)(2,1)} copy(bf16[8,1,512,1024]{2,1,0,3:T(2,128)(2,1)} %get-tuple-element.4) | data formatting | bytes 16777216
  338.2 4.6 select_bitcast_fusion
  342.9 13.1 %collective-permute-done = bf16[8,512,1024]{2,1,0:T(8,128)(2,1)S(1)} collective-permute-done((bf16[8,512,1024]{2,1,0:T(8,128)(2,1)S(1)}, bf16[8,512,1024]{2,1,0:T(8,128)(2,1)S(1)}, u32[]{:S(2)}, u32[]{:S(2)}) %collective-permute-start) | collective-permute-done | bytes 8388640 | tf_op jit(solution)/shard_map/ppermute | solution.py:121
  356.0 7.4 %fusion.4 = bf16[8,512,1024]{2,1,0:T(8,128)(2,1)} fusion(bf16[8,512,1024]{2,1,0:T(8,128)(2,1)S(1)} %collective-permute-done, bf16[8,1,512,1024]{3,2,0,1:T(8,128)(2,1)S(1)} %copy-done, bf16[8,1,512,1024]{3,2,0,1:T(8,128)(2,1)} %copy.82, pred[]{:T(512)S(6)} %eq.4), kind=kLoop, calls=%fused_computation.6 | loop fusion | flops 20971520 | bytes 33554432 | tf_op jit(solution)/shard_map/convert_element_type | solution.py:122
  363.5 5.8 %convolution_convert_fusion = bf16[4,128,8,128]{3,1,2,0:T(8,128)(2,1)S(1)} fusion(f32[4,192,128,8]{2,1,3,0:T(8,128)} %fusion.75, bf16[192,4,128,1]{2,1,0,3:T(4,128)(2,1)S(1)} %bitcast.229, f32[4,8,128,192]{2,3,1,0:T(8,128)} %get-tuple-element.21, f32[4,8,128]{2,1,0:T(8,128)S(1)} %get-tuple-element.20), kind=kOutput, calls=%fused_computation.50 | convolution fusion | flops 207360192 | bytes 7553024 | tf_op jit(solution)/shard_map/hgln,nhd->lhgd/dot_general | solution.py:49
  369.9 6.7 %convolution_convert_fusion.1 = bf16[4,128,8,128]{3,1,2,0:T(8,128)(2,1)S(1)} fusion(f32[4,192,128,8]{2,1,3,0:T(8,128)} %fusion.74, bf16[192,4,128,1]{2,1,0,3:T(4,128)(2,1)} %bitcast.231, f32[4,8,128,192]{2,3,1,0:T(8,128)} %get-tuple-element.23, f32[4,8,128]{2,1,0:T(8,128)S(1)} %copy-done.6), kind=kOutput, calls=%fused_computation.51 | convolution fusion | flops 207360192 | bytes 7553024 | tf_op jit(solution)/shard_map/hgln,nhd->lhgd/dot_general | solution.py:49
  377.1 11.6 %fusion.9 = f32[2,8,24,8192]{3,2,1,0:T(8,128)} fusion(bf16[2,8,24,512]{3,2,1,0:T(8,128)(2,1)} %copy-done.2, bf16[1,8192,512]{2,1,0:T(8,128)(2,1)} %param.9), kind=kOutput, calls=%fused_computation.12 | convolution fusion | flops 3221225472 | bytes 21364736 | tf_op jit(solution)/shard_map/bjtk,dk->bjtd/dot_general | solution.py:173
  388.7 12.9 %add_convert_fusion.x_ref = bf16[2,8,24,8192]{3,2,1,0:T(8,128)(2,1)} fusion(f32[2,8,24,8192]{3,2,1,0:T(8,128)} %fusion.9, bf16[2,8,24,512]{3,2,1,0:T(8,128)(2,1)S(1)} %get-tuple-element.25, bf16[1,8192,512]{2,1,0:T(8,128)(2,1)} %param.10), kind=kOutput, calls=%fused_computation.8 | convolution fusion | flops 3227516928 | bytes 27656192 | tf_op jit(solution)/shard_map/bjtk,dk->bjtd/dot_general | solution.py:176
  401.6 121.7 %shard_map.103 = bf16[2,8,24,8192]{3,2,1,0:T(8,128)(2,1)} custom-call(bf16[2,8,24,8192]{3,2,1,0:T(8,128)(2,1)} %add_convert_fusion.x_ref), custom_call_target="tpu_custom_call" | custom-call | tf_op jit(solution)/shard_map/pallas_call | solution.py:98
  523.3 4.8 reduce_sum.52
  (52 shorter events, 24.1 us)
Async XLA Ops:
  7.2 522.4 %reduce-scatter.2.cloned.1.call-start = ((), (), s32[]{:S(2)}) async-start(), calls=%async_computation.1 | async-start | bytes 9437184 | tf_op jit(solution)/shard_map/reduce_scatter | solution.py:124
  7.2 2.0 copy-start.4
  126.4 10.1 %copy-start.5 = (s32[2]{0:T(128)S(1)}, s32[2]{0:T(128)}, u32[]{:S(2)}) copy-start(s32[2]{0:T(128)} %param.12) | copy-start | bytes 28
  163.2 3.6 copy-start.1
  163.2 3.6 copy-start.3
  178.7 15.4 %copy-start.2 = (bf16[2,8,24,512]{3,2,1,0:T(8,128)(2,1)}, bf16[2,8,24,512]{3,2,1,0:T(8,128)(2,1)S(1)}, u32[]{:S(2)}) copy-start(bf16[2,8,24,512]{3,2,1,0:T(8,128)(2,1)S(1)} %get-tuple-element.24) | copy-start | bytes 1179652
  338.2 17.9 %copy-start = (bf16[8,1,512,1024]{3,2,0,1:T(8,128)(2,1)S(1)}, bf16[8,1,512,1024]{3,2,0,1:T(8,128)(2,1)}, u32[]{:S(2)}) copy-start(bf16[8,1,512,1024]{3,2,0,1:T(8,128)(2,1)} %copy.81) | copy-start | bytes 25165828
  342.8 13.2 %collective-permute-start = (bf16[8,512,1024]{2,1,0:T(8,128)(2,1)S(1)}, bf16[8,512,1024]{2,1,0:T(8,128)(2,1)S(1)}, u32[]{:S(2)}, u32[]{:S(2)}) collective-permute-start(bf16[8,512,1024]{2,1,0:T(8,128)(2,1)S(1)} %select_bitcast_fusion), channel_id=1, source_target_pairs={{0,1},{1,0},{2,3},{3,2},{4,5},{5,4},{6,7},{7,6},{8,9},{9,8},{10,11... | collective-permute-start | bytes 25165832 | tf_op jit(solution)/shard_map/ppermute | solution.py:121
  363.5 6.4 %copy-start.6 = (f32[4,8,128]{2,1,0:T(8,128)S(1)}, f32[4,8,128]{2,1,0:T(8,128)}, u32[]{:S(2)}) copy-start(f32[4,8,128]{2,1,0:T(8,128)} %get-tuple-element.22) | copy-start | bytes 49156
Sparse Core Ops, SparseCore 0:
  363.6 139.4 reduce-scatter.1

commit v3 on v1

--- a/solution.py
+++ b/solution.py
@@ -112,7 +112,6 @@
 def shards(queries, image_tokens, key_weight, value_weight, cotangent, tile_counts, text_lengths):
     n_section = lax.axis_size("section")
     samples_here, chunk, model_width = image_tokens.shape
-    gathered = exchange(image_tokens, n_section, False, 0)
     image_len = n_section * chunk
     tile_len = image_len // MAX_TILES
     w_key = key_weight[0]
@@ -120,42 +119,31 @@
     query_local = queries[0]
     cotan_local = cotangent[0]
     query_list = []
-    key_list = []
-    value_list = []
-    keys_all = jnp.einsum(
-        "bjtd,dk->bjtk", gathered, w_key, preferred_element_type=jnp.float32
-    ).astype(jnp.bfloat16).reshape(samples_here, image_len, -1)
-    values_all = jnp.einsum(
-        "bjtd,dk->bjtk", gathered, w_value, preferred_element_type=jnp.float32
-    ).astype(jnp.bfloat16).reshape(samples_here, image_len, -1)
+    kv_term = None
+    image_list = []
     for sample_index in range(samples_here):
+        tokens = lax.all_gather(image_tokens[sample_index], "section", axis=0, tiled=True)
+        keys = jnp.dot(tokens, w_key, preferred_element_type=jnp.float32).astype(jnp.bfloat16)
+        values = jnp.dot(tokens, w_value, preferred_element_type=jnp.float32).astype(jnp.bfloat16)
         query_gradient, key_gradient, value_gradient = attend_one(
             query_local[sample_index],
-            keys_all[sample_index],
-            values_all[sample_index],
+            keys,
+            values,
             cotan_local[sample_index],
             tile_counts[sample_index] * tile_len,
             text_lengths[sample_index],
         )
         query_list.append(query_gradient)
-        key_list.append(key_gradient)
-        value_list.append(value_gradient)
+        kv_grads = jnp.concatenate([key_gradient, value_gradient], axis=-1)
+        part = jnp.einsum("td,tk->dk", tokens, kv_grads, preferred_element_type=jnp.float32)
+        kv_term = part if kv_term is None else kv_term + part
+        term = jnp.einsum("tk,dk->td", key_gradient, w_key, preferred_element_type=jnp.float32)
+        term = term + jnp.einsum("tk,dk->td", value_gradient, w_value, preferred_element_type=jnp.float32)
+        image_list.append(term.astype(jnp.bfloat16).reshape(n_section, chunk, model_width))
     query_out = jnp.stack(query_list)[None]
-    key_grads = jnp.stack(key_list).reshape(samples_here, n_section, chunk, -1)
-    value_grads = jnp.stack(value_list).reshape(samples_here, n_section, chunk, -1)
-    kv_grads = jnp.concatenate([key_grads, value_grads], axis=-1)
-    kv_term = jnp.einsum(
-        "bjtd,bjtk->dk", gathered, kv_grads, preferred_element_type=jnp.float32
-    )
     kv_sum = lax.psum_scatter(kv_term.astype(jnp.bfloat16), "dp", scatter_dimension=0, tiled=True)
-    kv_width = key_grads.shape[-1]
-    image_term = jnp.einsum(
-        "bjtk,dk->bjtd", key_grads, w_key, preferred_element_type=jnp.float32
-    )
-    image_term = image_term + jnp.einsum(
-        "bjtk,dk->bjtd", value_grads, w_value, preferred_element_type=jnp.float32
-    )
-    received = exchange(image_term.astype(jnp.bfloat16), n_section, True, 1)
+    kv_width = kv_sum.shape[-1] // 2
+    received = exchange(jnp.stack(image_list), n_section, True, 1)
     image_out = jnp.sum(received.astype(jnp.float32), axis=1).astype(jnp.bfloat16)
     return (
         query_out,

time: 376 us -> 405 us (1.077)
  Pallas kernels: 229 us -> 122 us
  waiting for transfers between devices: 0.02 us -> 107 us
  matrix products: 98.5 us -> 128 us
    pallas_call x2 -> x1, Pallas kernels: 229 us -> 122 us  [exchange(): pl.pallas_call(functools.partial(exchange_kernel, n, scatter), out_shape=...]
    all_gather x0 -> x2, waiting for transfers between devices: none -> 106 us  [shards(): lax.all_gather(image_tokens[sample_index], 'section', axis=0, tiled=True)]
    dot_general x5 -> x10, matrix products: 57 us -> 84.7 us  [the longest x2 32 us: shards(): jnp.einsum('td,tk->dk', tokens, kv_grads, preferred_element_type=jnp.floa...]
    reshape x0 -> x6, local copies, waits for them, and re-layouts: none -> 5.25 us  [the longest x2 2.68 us: attend_one(): value_gradient.reshape(total_keys, KEY_VALUE_HEADS * HEAD_SIZE)]
  transfers between devices with their start and end apart: 1 -> 3, of which waited for: 0 -> 2; matrix products, arithmetic and copies ran while one was open for 12% -> 18% of each run, Pallas kernels for 33% -> 30%
where the time goes in v3:
time: 405 us; the launch traced here: 404 us
  matrix products  128 us (32%)
  Pallas kernels  122 us (30%)
  waiting for transfers between devices  107 us (26%)
  local copies, waits for them, and re-layouts  21.5 us (5%)
  between operations  15.3 us (4%)
  other arithmetic  10.7 us (3%)
    pallas_call x1, Pallas kernels, exchange(): pl.pallas_call(functools.partial(exchange_kernel, n, scatter), out_shape=...  122 us
    all_gather x2, waiting for transfers between devices, shards(): lax.all_gather(image_tokens[sample_index], 'section', axis=0, tiled=True)  106 us
    dot_general x2, matrix products, shards(): jnp.einsum('td,tk->dk', tokens, kv_grads, preferred_element_type=jnp.floa...  32 us
    dot_general x2, matrix products, shards(): jnp.einsum('tk,dk->td', value_gradient, w_value, preferred_element_type=j...  14.6 us
    dot_general x2, matrix products, attend_one(): jnp.einsum('hgln,lhgd->nhd', score_grad, heads_of_queries, preferred_elem...  13.5 us
    dot_general x2, matrix products, shards(): jnp.dot(tokens, w_key, preferred_element_type=jnp.float32)  12.9 us
    dot_general x2, matrix products, shards(): jnp.einsum('tk,dk->td', key_gradient, w_key, preferred_element_type=jnp.f...  12.8 us
    dot_general x2, matrix products, attend_one(): jnp.einsum('hgln,nhd->lhgd', score_grad, heads_of_keys, preferred_element...  12.4 us
  transfers between devices with their start and end apart: 3, of which 2 were waited for; matrix products, arithmetic and copies ran while one was open for 18% of the time, Pallas kernels for 30%

profile of v3, /device:TPU:38, one launch (start us, length us, event | category | flops | bytes accessed | tf_op | source)
XLA Modules:
  0.0 403.7 jit_solution(1156837915392046009)
XLA Ops:
  20.3 54.9 %all-gather.7.cloned.1.call-done = bf16[1,192,8192]{2,1,0:T(8,128)(2,1)} async-done(((bf16[1,24,8192]{2,1,0:T(8,128)(2,1)}), bf16[1,192,8192]{2,1,0:T(8,128)(2,1)}) %all-gather.7.cloned.1.call-update) | async-done | bytes 3145744 | tf_op jit(solution)/shard_map/all_gather | solution.py:125
  75.1 6.1 %fusion.87 = bf16[192,512]{1,0:T(8,128)(2,1)S(1)} fusion(bf16[1,8192,512]{2,1,0:T(8,128)(2,1)} %param.10, bf16[1,192,8192]{2,1,0:T(8,128)(2,1)} %all-gather.7.cloned.1.call-done), kind=kOutput, calls=%fused_computation.82 | convolution fusion | flops 1610711040 | bytes 11730944 | tf_op jit(solution)/shard_map/dot_general | solution.py:127
  81.3 6.1 %fusion.77 = bf16[192,512]{1,0:T(8,128)(2,1)S(1)} fusion(bf16[1,8192,512]{2,1,0:T(8,128)(2,1)} %param.9, bf16[1,192,8192]{2,1,0:T(8,128)(2,1)} %all-gather.7.cloned.1.call-done), kind=kOutput, calls=%fused_computation.80 | convolution fusion | flops 1610711040 | bytes 11730944 | tf_op jit(solution)/shard_map/dot_general | solution.py:126
  88.2 51.3 %all-gather.5.cloned.1.call-done = bf16[1,192,8192]{2,1,0:T(8,128)(2,1)} async-done(((bf16[1,24,8192]{2,1,0:T(8,128)(2,1)}), bf16[1,192,8192]{2,1,0:T(8,128)(2,1)}) %all-gather.5.cloned.1.call-update) | async-done | bytes 3145744 | tf_op jit(solution)/shard_map/all_gather | solution.py:125
  139.5 6.1 %fusion.82 = bf16[192,512]{1,0:T(8,128)(2,1)S(1)} fusion(bf16[1,8192,512]{2,1,0:T(8,128)(2,1)} %param.10, bf16[1,192,8192]{2,1,0:T(8,128)(2,1)} %all-gather.5.cloned.1.call-done), kind=kOutput, calls=%fused_computation.81 | convolution fusion | flops 1610711040 | bytes 11730944 | tf_op jit(solution)/shard_map/dot_general | solution.py:127
  145.7 6.8 %fusion.72 = bf16[192,512]{1,0:T(8,128)(2,1)} fusion(bf16[1,8192,512]{2,1,0:T(8,128)(2,1)} %param.9, bf16[1,192,8192]{2,1,0:T(8,128)(2,1)} %all-gather.5.cloned.1.call-done), kind=kOutput, calls=%fused_computation.79 | convolution fusion | flops 1610711040 | bytes 11730944 | tf_op jit(solution)/shard_map/dot_general | solution.py:126
  154.2 2.3 fusion.107
  156.5 4.3 %fusion.152 = (f32[4,8,128]{2,1,0:T(8,128)}, f32[4,8,128,192]{2,3,1,0:T(8,128)}) fusion(pred[192]{0:T(512)(128)(4,1)S(1)} %iota_compare_fusion, bf16[128,4,8,128]{0,3,2,1:T(8,128)(2,1)S(1)} %bitcast.240, bf16[192,4,128,1]{2,1,0,3:T(4,128)(2,1)} %bitcast.246), kind=kOutput, calls=%fused_computation.143 | convolution fusion | flops 204472512 | bytes 4407488 | tf_op jit(solution)/shard_map/sub | solution.py:38
  160.8 2.7 fusion.97
  163.4 6.4 %fusion.92 = bf16[4,24,8,128]{3,2,1,0:T(8,128)(2,1)} fusion(bf16[128,4,8,128]{0,3,2,1:T(8,128)(2,1)S(1)} %bitcast.241, f32[4,192,128,8]{2,1,3,0:T(8,128)} %fusion.107, f32[4,8,128,192]{2,3,1,0:T(8,128)} %get-tuple-element.25, f32[4,8,128]{2,1,0:T(8,128)} %get-tuple-element.24), kind=kOutput, calls=%fused_computation.83 | convolution fusion | flops 206934208 | bytes 7553024 | tf_op jit(solution)/shard_map/hgln,lhgd->nhd/dot_general | solution.py:52
  172.2 2.8 fusion.157
  175.5 2.7 fusion.94
  178.2 7.0 %fusion.93 = bf16[4,24,8,128]{3,2,1,0:T(8,128)(2,1)} fusion(bf16[128,4,8,128]{0,3,2,1:T(8,128)(2,1)} %bitcast.238, f32[4,192,128,8]{2,1,3,0:T(8,128)} %fusion.106, f32[4,8,128,192]{2,3,1,0:T(8,128)} %get-tuple-element.27, f32[4,8,128]{2,1,0:T(8,128)} %copy-done.14), kind=kOutput, calls=%fused_computation.84 | convolution fusion | flops 206934208 | bytes 7553024 | tf_op jit(solution)/shard_map/hgln,lhgd->nhd/dot_general | solution.py:52
  188.0 13.2 %fusion.34 = f32[1024,8192]{1,0:T(8,128)} fusion(bf16[1,192,8192]{2,1,0:T(8,128)(2,1)S(1)} %copy-done.3, bf16[192,512]{1,0:T(8,128)(2,1)S(1)} %get-tuple-element.28, bf16[192,512]{1,0:T(8,128)(2,1)S(1)} %get-tuple-element.29), kind=kOutput, calls=%fused_computation.46 | convolution fusion | flops 3222011904 | bytes 37093376 | tf_op jit(solution)/shard_map/td,tk->dk/dot_general | solution.py:138
  201.1 18.9 %fusion.4 = bf16[8192,1024]{0,1:T(8,128)(2,1)} fusion(f32[1024,8192]{1,0:T(8,128)} %fusion.34, bf16[1,192,8192]{2,1,0:T(8,128)(2,1)S(1)} %copy-done.2, bf16[192,512]{1,0:T(8,128)(2,1)} %get-tuple-element.30, bf16[192,512]{1,0:T(8,128)(2,1)} %get-tuple-element.31), kind=kOutput, calls=%fused_computation.5 | convolution fusion | flops 3238789120 | bytes 53870592 | tf_op jit(solution)/shard_map/td,tk->dk/dot_general | solution.py:138
  220.9 5.9 %convolution_convert_fusion = bf16[4,128,8,128]{3,1,2,0:T(8,128)(2,1)S(1)} fusion(f32[4,192,128,8]{2,1,3,0:T(8,128)} %fusion.107, bf16[192,4,128,1]{2,1,0,3:T(4,128)(2,1)S(1)} %bitcast.247, f32[4,8,128,192]{2,3,1,0:T(8,128)} %get-tuple-element.25, f32[4,8,128]{2,1,0:T(8,128)S(1)} %copy-done.13), kind=kOutput, calls=%fused_computation.65 | convolution fusion | flops 207360192 | bytes 7553024 | tf_op jit(solution)/shard_map/hgln,nhd->lhgd/dot_general | solution.py:49
  227.3 6.6 %convolution_convert_fusion.1 = bf16[4,128,8,128]{3,1,2,0:T(8,128)(2,1)S(1)} fusion(f32[4,192,128,8]{2,1,3,0:T(8,128)} %fusion.106, bf16[192,4,128,1]{2,1,0,3:T(4,128)(2,1)S(1)} %bitcast.249, f32[4,8,128,192]{2,3,1,0:T(8,128)} %get-tuple-element.27, f32[4,8,128]{2,1,0:T(8,128)S(1)} %copy-done.15), kind=kOutput, calls=%fused_computation.66 | convolution fusion | flops 207360192 | bytes 7553024 | tf_op jit(solution)/shard_map/hgln,nhd->lhgd/dot_general | solution.py:49
  235.2 6.5 %fusion.15 = f32[192,8192]{1,0:T(8,128)S(1)} fusion(bf16[1,8192,512]{2,1,0:T(8,128)(2,1)} %param.9, bf16[4,24,8,128]{3,2,1,0:T(8,128)(2,1)S(1)} %copy-done.8), kind=kOutput, calls=%fused_computation.18 | convolution fusion | flops 1610612736 | bytes 14876672 | tf_op jit(solution)/shard_map/tk,dk->td/dot_general | solution.py:140
  241.7 6.4 %fusion.13 = f32[192,8192]{1,0:T(8,128)S(1)} fusion(bf16[1,8192,512]{2,1,0:T(8,128)(2,1)} %param.9, bf16[4,24,8,128]{3,2,1,0:T(8,128)(2,1)S(1)} %copy-done.7), kind=kOutput, calls=%fused_computation.16 | convolution fusion | flops 1610612736 | bytes 14876672 | tf_op jit(solution)/shard_map/tk,dk->td/dot_general | solution.py:140
  248.1 8.1 %fusion.5 = bf16[192,8192]{1,0:T(8,128)(2,1)} fusion(f32[192,8192]{1,0:T(8,128)S(1)} %fusion.15, bf16[1,8192,512]{2,1,0:T(8,128)(2,1)} %param.10, bf16[4,24,8,128]{3,2,1,0:T(8,128)(2,1)S(1)} %fusion.94), kind=kOutput, calls=%fused_computation.8 | convolution fusion | flops 1613758464 | bytes 18022400 | tf_op jit(solution)/shard_map/tk,dk->td/dot_general | solution.py:141
  256.2 6.6 %fusion.6 = bf16[192,8192]{1,0:T(8,128)(2,1)S(1)} fusion(f32[192,8192]{1,0:T(8,128)S(1)} %fusion.13, bf16[1,8192,512]{2,1,0:T(8,128)(2,1)} %param.10, bf16[4,24,8,128]{3,2,1,0:T(8,128)(2,1)S(1)} %fusion.97), kind=kOutput, calls=%fused_computation.9 | convolution fusion | flops 1613758464 | bytes 18022400 | tf_op jit(solution)/shard_map/tk,dk->td/dot_general | solution.py:141
  262.8 3.2 pad_maximum_fusion.x_ref
  265.9 121.6 %shard_map.102 = bf16[2,8,24,8192]{3,2,1,0:T(8,128)(2,1)} custom-call(bf16[2,8,24,8192]{3,2,1,0:T(8,128)(2,1)} %pad_maximum_fusion.x_ref), custom_call_target="tpu_custom_call" | custom-call | tf_op jit(solution)/shard_map/pallas_call | solution.py:98
  387.6 4.8 %reduce_sum.52 = bf16[2,24,8192]{2,1,0:T(8,128)(2,1)} reduce(bf16[2,8,24,8192]{3,2,1,0:T(8,128)(2,1)} %shard_map.102, bf16[]{:T(256)} %constant.12.clone.1), dimensions={1}, to_apply=%region_6.7 | reduce | flops 2752512 | bytes 7077890 | tf_op jit(solution)/shard_map/reduce_sum | solution.py:147
  (65 shorter events, 27.4 us)
Async XLA Ops:
  7.2 68.0 %all-gather.7.cloned.1.call-start = ((), (), s32[]{:S(2)}) async-start(), calls=%async_computation.3 | async-start | bytes 3538944 | tf_op jit(solution)/shard_map/all_gather | solution.py:125
  9.3 130.2 %all-gather.5.cloned.1.call-start = ((), (), s32[]{:S(2)}) async-start(), calls=%async_computation.2 | async-start | bytes 3538944 | tf_op jit(solution)/shard_map/all_gather | solution.py:125
  10.0 383.9 %reduce-scatter.2.cloned.1.call-start = ((), (), s32[]{:S(2)}) async-start(), calls=%async_computation.1 | async-start | bytes 17825792 | tf_op jit(solution)/shard_map/reduce_scatter | solution.py:144
  15.7 2.0 copy-start.4
  17.8 0.7 copy-start.12
  152.5 4.0 copy-start.6
  169.9 2.3 copy-start.5
  169.9 2.3 copy-start.10
  174.9 0.6 copy-start.14
  178.2 9.7 %copy-start.3 = (bf16[1,192,8192]{2,1,0:T(8,128)(2,1)S(1)}, bf16[1,192,8192]{2,1,0:T(8,128)(2,1)}, u32[]{:S(2)}) copy-start(bf16[1,192,8192]{2,1,0:T(8,128)(2,1)} %all-gather.5.cloned.1.call-done) | copy-start | bytes 9437188
  187.9 13.2 %copy-start.2 = (bf16[1,192,8192]{2,1,0:T(8,128)(2,1)S(1)}, bf16[1,192,8192]{2,1,0:T(8,128)(2,1)}, u32[]{:S(2)}) copy-start(bf16[1,192,8192]{2,1,0:T(8,128)(2,1)} %all-gather.7.cloned.1.call-done) | copy-start | bytes 9437188
  220.0 0.9 copy-start.9
  220.0 0.9 copy-start.13
  220.9 6.4 %copy-start.11 = (bf16[192,4,128]{2,1,0:T(4,128)(2,1)S(1)}, bf16[192,4,128]{2,1,0:T(4,128)(2,1)}, u32[]{:S(2)}) copy-start(bf16[192,4,128]{2,1,0:T(4,128)(2,1)} %reshape.72) | copy-start | bytes 589828
  220.9 6.4 %copy-start.15 = (f32[4,8,128]{2,1,0:T(8,128)S(1)}, f32[4,8,128]{2,1,0:T(8,128)}, u32[]{:S(2)}) copy-start(f32[4,8,128]{2,1,0:T(8,128)} %copy-done.14) | copy-start | bytes 49156
  227.3 7.9 %copy-start.8 = (bf16[4,24,8,128]{3,2,1,0:T(8,128)(2,1)S(1)}, bf16[4,24,8,128]{3,2,1,0:T(8,128)(2,1)}, u32[]{:S(2)}) copy-start(bf16[4,24,8,128]{3,2,1,0:T(8,128)(2,1)} %fusion.93) | copy-start | bytes 589828
  235.2 6.5 %copy-start.7 = (bf16[4,24,8,128]{3,2,1,0:T(8,128)(2,1)S(1)}, bf16[4,24,8,128]{3,2,1,0:T(8,128)(2,1)}, u32[]{:S(2)}) copy-start(bf16[4,24,8,128]{3,2,1,0:T(8,128)(2,1)} %fusion.92) | copy-start | bytes 589828
  256.2 6.6 %copy-start = (bf16[192,8192]{1,0:T(8,128)(2,1)S(1)}, bf16[192,8192]{1,0:T(8,128)(2,1)}, u32[]{:S(2)}) copy-start(bf16[192,8192]{1,0:T(8,128)(2,1)} %fusion.5) | copy-start | bytes 9437188
  387.6 4.8 %copy-start.1 = (bf16[1,128,4096]{2,1,0:T(8,128)(2,1)S(1)}, bf16[1,128,4096]{2,1,0:T(8,128)(2,1)}, u32[]{:S(2)}) copy-start(bf16[1,128,4096]{2,1,0:T(8,128)(2,1)} %copy.35) | copy-start | bytes 3145732
Sparse Core Ops, SparseCore 0:
  10.9 64.2 all-gather.6
  78.0 61.4 all-gather.4
  220.1 141.8 reduce-scatter.1

commit v4 on v1

--- a/solution.py
+++ b/solution.py
@@ -88,6 +88,115 @@
     for copy in copies:
         copy.wait()
     local.wait()
+
+
+def relay_gather_kernel(x_ref, o_ref, stage, local_sem, direct_send, direct_recv,
+                        hop_send, hop_recv, fwd_send, fwd_recv):
+    s = lax.axis_index("section")
+    r = lax.axis_index("dp")
+    y = lax.rem(s, 4)
+    z = (s // 4) * 2 + r // 8
+    xc = lax.rem(r, 8)
+    half = x_ref.shape[-1] // 2
+
+    def sec(zz, yy):
+        return (lax.rem(zz, 4) // 2) * 4 + yy
+
+    def dpi(zz):
+        return lax.rem(zz, 2) * 8 + xc
+
+    up, down = z + 1, z + 3
+    peers = [(sec(z, lax.rem(y + j, 4)), r) for j in range(1, 4)]
+    for yy in range(4):
+        peers.append((sec(up, yy), dpi(up)))
+        peers.append((sec(down, yy), dpi(down)))
+    barrier = pltpu.get_barrier_semaphore()
+    for peer in peers:
+        pl.semaphore_signal(barrier, inc=1, device_id=peer, device_id_type=MESH_ID)
+    pl.semaphore_wait(barrier, len(peers))
+
+    local = pltpu.make_async_copy(x_ref, o_ref.at[:, s], local_sem)
+    local.start()
+    sends = []
+    for j in range(1, 4):
+        copy = pltpu.make_async_remote_copy(
+            src_ref=x_ref,
+            dst_ref=o_ref.at[:, s],
+            send_sem=direct_send.at[j],
+            recv_sem=direct_recv.at[j],
+            device_id=peers[j - 1],
+            device_id_type=MESH_ID,
+        )
+        copy.start()
+        sends.append(copy)
+    hops = []
+    for side, (target, lanes) in enumerate(((up, pl.ds(0, half)), (down, pl.ds(half, half)))):
+        copy = pltpu.make_async_remote_copy(
+            src_ref=x_ref.at[:, :, lanes],
+            dst_ref=stage.at[side],
+            send_sem=hop_send.at[side],
+            recv_sem=hop_recv.at[side],
+            device_id=(sec(target, y), dpi(target)),
+            device_id_type=MESH_ID,
+        )
+        copy.start()
+        hops.append(copy)
+    forwards = []
+    for side, (origin, target, lanes) in enumerate(
+        ((down, up, pl.ds(0, half)), (up, down, pl.ds(half, half)))
+    ):
+        hops[side].wait_recv()
+        for yy in range(4):
+            copy = pltpu.make_async_remote_copy(
+                src_ref=stage.at[side],
+                dst_ref=o_ref.at[:, sec(origin, y), :, lanes],
+                send_sem=fwd_send.at[side, yy],
+                recv_sem=fwd_recv.at[side, y],
+                device_id=(sec(target, yy), dpi(target)),
+                device_id_type=MESH_ID,
+            )
+            copy.start()
+            forwards.append(copy)
+    for copy in sends:
+        copy.wait()
+    for copy in hops:
+        copy.wait_send()
+    for copy in forwards:
+        copy.wait_send()
+    for side, (origin, target, lanes) in enumerate(
+        ((down, up, pl.ds(0, half)), (up, down, pl.ds(half, half)))
+    ):
+        for yy in range(4):
+            pltpu.make_async_remote_copy(
+                src_ref=stage.at[side],
+                dst_ref=o_ref.at[:, sec(origin, y), :, lanes],
+                send_sem=fwd_send.at[side, yy],
+                recv_sem=fwd_recv.at[side, yy],
+                device_id=(sec(target, yy), dpi(target)),
+                device_id_type=MESH_ID,
+            ).wait_recv()
+    local.wait()
+
+
+def relay_gather(x, n):
+    samples, chunk, width = x.shape
+    return pl.pallas_call(
+        relay_gather_kernel,
+        out_shape=jax.ShapeDtypeStruct((samples, n, chunk, width), x.dtype),
+        in_specs=[pl.BlockSpec(memory_space=pl.ANY)],
+        out_specs=pl.BlockSpec(memory_space=pl.ANY),
+        scratch_shapes=[
+            pltpu.VMEM((2, samples, chunk, width // 2), x.dtype),
+            pltpu.SemaphoreType.DMA(()),
+            pltpu.SemaphoreType.DMA((4,)),
+            pltpu.SemaphoreType.DMA((4,)),
+            pltpu.SemaphoreType.DMA((2,)),
+            pltpu.SemaphoreType.DMA((2,)),
+            pltpu.SemaphoreType.DMA((2, 4)),
+            pltpu.SemaphoreType.DMA((2, 4)),
+        ],
+        compiler_params=pltpu.CompilerParams(collective_id=2, has_side_effects=True),
+    )(x)
 
 
 def exchange(x, n, scatter, collective_id):
@@ -112,7 +221,10 @@
 def shards(queries, image_tokens, key_weight, value_weight, cotangent, tile_counts, text_lengths):
     n_section = lax.axis_size("section")
     samples_here, chunk, model_width = image_tokens.shape
-    gathered = exchange(image_tokens, n_section, False, 0)
+    if n_section == 8 and lax.axis_size("dp") == 16:
+        gathered = relay_gather(image_tokens, n_section)
+    else:
+        gathered = exchange(image_tokens, n_section, False, 0)
     image_len = n_section * chunk
     tile_len = image_len // MAX_TILES
     w_key = key_weight[0]

time: 376 us -> 370 us (0.984)
  Pallas kernels: 229 us -> 224 us
    pallas_call x2 -> x1, Pallas kernels: 229 us -> 129 us  [exchange(): pl.pallas_call(functools.partial(exchange_kernel, n, scatter), out_shape=...]
    pallas_call x0 -> x1, Pallas kernels: none -> 94.9 us  [relay_gather(): pl.pallas_call(relay_gather_kernel, out_shape=jax.ShapeDtypeStruct((sampl...]
  transfers between devices with their start and end apart: 1 -> 1, of which waited for: 0 -> 0; matrix products, arithmetic and copies ran while one was open for 12% -> 12% of each run, Pallas kernels for 33% -> 35%
where the time goes in v4:
time: 370 us; the launch traced here: 366 us
  Pallas kernels  224 us (61%)
  matrix products  98.5 us (27%)
  local copies, waits for them, and re-layouts  20.5 us (6%)
  between operations  15.6 us (4%)
  other arithmetic  7.57 us (2%)
    pallas_call x1, Pallas kernels, exchange(): pl.pallas_call(functools.partial(exchange_kernel, n, scatter), out_shape=...  129 us
    pallas_call x1, Pallas kernels, relay_gather(): pl.pallas_call(relay_gather_kernel, out_shape=jax.ShapeDtypeStruct((sampl...  94.9 us
    dot_general x1, matrix products, shards(): jnp.einsum('bjtd,bjtk->dk', gathered, kv_grads, preferred_element_type=jn...  15.2 us
    dot_general x1, matrix products, shards(): jnp.einsum('bjtk,dk->bjtd', value_grads, w_value, preferred_element_type=...  12.9 us
    dot_general x2, matrix products, attend_one(): jnp.einsum('hgln,lhgd->nhd', score_grad, heads_of_queries, preferred_elem...  12.4 us
    dot_general x2, matrix products, attend_one(): jnp.einsum('hgln,nhd->lhgd', score_grad, heads_of_keys, preferred_element...  11.9 us
    dot_general x1, matrix products, shards(): jnp.einsum('bjtk,dk->bjtd', key_grads, w_key, preferred_element_type=jnp....  11.7 us
    dot_general x1, matrix products, shards(): jnp.einsum('bjtd,dk->bjtk', gathered, w_value, preferred_element_type=jnp...  8.61 us
  transfers between devices with their start and end apart: 1, of which 0 were waited for; matrix products, arithmetic and copies ran while one was open for 12% of the time, Pallas kernels for 35%

profile of v4, /device:TPU:38, one launch (start us, length us, event | category | flops | bytes accessed | tf_op | source)
XLA Modules:
  0.0 366.2 jit_solution(8211605470825050128)
XLA Ops:
  9.9 1.3 fusion.118
  12.5 1.7 fusion.114
  14.2 1.3 copy.76
  18.1 94.9 %shard_map.102 = bf16[2,8,24,8192]{3,2,1,0:T(8,128)(2,1)} custom-call(bf16[2,24,8192]{2,1,0:T(8,128)(2,1)} %x_ref.1), custom_call_target="tpu_custom_call" | custom-call | tf_op jit(solution)/shard_map/pallas_call | solution.py:183
  113.0 8.6 %fusion.43 = bf16[2,8,24,512]{3,2,1,0:T(8,128)(2,1)S(1)} fusion(bf16[2,8,24,8192]{3,2,1,0:T(8,128)(2,1)} %shard_map.102, bf16[1,8192,512]{2,1,0:T(8,128)(2,1)} %param.10), kind=kOutput, calls=%fused_computation.54 | convolution fusion | flops 3221422080 | bytes 15073280 | tf_op jit(solution)/shard_map/bjtd,dk->bjtk/dot_general | solution.py:240
  121.8 8.6 %fusion.40 = bf16[2,8,24,512]{3,2,1,0:T(8,128)(2,1)S(1)} fusion(bf16[2,8,24,8192]{3,2,1,0:T(8,128)(2,1)} %shard_map.102, bf16[1,8192,512]{2,1,0:T(8,128)(2,1)} %param.9), kind=kOutput, calls=%fused_computation.53 | convolution fusion | flops 3221422080 | bytes 15073280 | tf_op jit(solution)/shard_map/bjtd,dk->bjtk/dot_general | solution.py:237
  131.2 1.6 reshape_squeeze.18
  132.8 1.7 reshape_squeeze.21
  134.5 2.3 fusion.74
  136.7 4.3 %fusion.119 = (f32[4,8,128]{2,1,0:T(8,128)}, f32[4,8,128,192]{2,3,1,0:T(8,128)}) fusion(pred[192]{0:T(512)(128)(4,1)S(1)} %iota_compare_fusion, bf16[128,4,8,128]{0,3,2,1:T(8,128)(2,1)S(1)} %bitcast.213, bf16[192,4,128,1]{2,1,0,3:T(4,128)(2,1)} %bitcast.221), kind=kOutput, calls=%fused_computation.120 | convolution fusion | flops 204472512 | bytes 4407488 | tf_op jit(solution)/shard_map/sub | solution.py:38
  141.0 2.7 fusion.67
  143.7 6.5 %fusion.62 = bf16[192,4,128]{2,0,1:T(8,128)(2,1)} fusion(bf16[128,4,8,128]{0,3,2,1:T(8,128)(2,1)S(1)} %bitcast.214, f32[4,192,128,8]{2,1,3,0:T(8,128)} %fusion.74, f32[4,8,128,192]{2,3,1,0:T(8,128)} %get-tuple-element.27, f32[4,8,128]{2,1,0:T(8,128)} %get-tuple-element.26), kind=kOutput, calls=%fused_computation.63 | convolution fusion | flops 206934208 | bytes 7553024 | tf_op jit(solution)/shard_map/hgln,lhgd->nhd/dot_general | solution.py:52
  151.8 2.4 fusion.73
  154.1 2.8 fusion.124
  156.9 2.9 fusion.64
  159.8 5.9 %fusion.63 = bf16[192,4,128]{2,0,1:T(8,128)(2,1)S(1)} fusion(bf16[128,4,8,128]{0,3,2,1:T(8,128)(2,1)S(1)} %bitcast.212, f32[4,192,128,8]{2,1,3,0:T(8,128)} %fusion.73, f32[4,8,128,192]{2,3,1,0:T(8,128)} %get-tuple-element.29, f32[4,8,128]{2,1,0:T(8,128)S(1)} %get-tuple-element.28), kind=kOutput, calls=%fused_computation.64 | convolution fusion | flops 206934208 | bytes 7553024 | tf_op jit(solution)/shard_map/hgln,lhgd->nhd/dot_general | solution.py:52
  167.0 15.2 %fusion.4 = bf16[8192,1024]{0,1:T(8,128)(2,1)} fusion(bf16[2,8,24,8192]{3,2,1,0:T(8,128)(2,1)} %shard_map.102, bf16[2,8,24,512]{3,2,1,0:T(8,128)(2,1)S(1)} %get-tuple-element.31, bf16[2,8,24,512]{3,2,1,0:T(8,128)(2,1)S(1)} %get-tuple-element.30), kind=kOutput, calls=%fused_computation.5 | convolution fusion | flops 6452412416 | bytes 23855104 | tf_op jit(solution)/shard_map/bjtd,bjtk->dk/dot_general | solution.py:259
  183.1 5.9 %convolution_convert_fusion = bf16[4,128,8,128]{3,1,2,0:T(8,128)(2,1)S(1)} fusion(f32[4,192,128,8]{2,1,3,0:T(8,128)} %fusion.74, bf16[192,4,128,1]{2,1,0,3:T(4,128)(2,1)S(1)} %bitcast.222, f32[4,8,128,192]{2,3,1,0:T(8,128)} %get-tuple-element.27, f32[4,8,128]{2,1,0:T(8,128)S(1)} %copy-done.6), kind=kOutput, calls=%fused_computation.47 | convolution fusion | flops 207360192 | bytes 7553024 | tf_op jit(solution)/shard_map/hgln,nhd->lhgd/dot_general | solution.py:49
  189.5 6.0 %convolution_convert_fusion.1 = bf16[4,128,8,128]{3,1,2,0:T(8,128)(2,1)S(1)} fusion(f32[4,192,128,8]{2,1,3,0:T(8,128)} %fusion.73, bf16[192,4,128,1]{2,1,0,3:T(4,128)(2,1)} %bitcast.219, f32[4,8,128,192]{2,3,1,0:T(8,128)} %get-tuple-element.29, f32[4,8,128]{2,1,0:T(8,128)S(1)} %copy-done.8), kind=kOutput, calls=%fused_computation.48 | convolution fusion | flops 207360192 | bytes 7553024 | tf_op jit(solution)/shard_map/hgln,nhd->lhgd/dot_general | solution.py:49
  196.1 11.7 %fusion.8 = f32[2,8,24,8192]{3,2,1,0:T(8,128)} fusion(bf16[2,8,24,512]{3,2,1,0:T(8,128)(2,1)} %copy-done.3, bf16[1,8192,512]{2,1,0:T(8,128)(2,1)} %param.9), kind=kOutput, calls=%fused_computation.10 | convolution fusion | flops 3221225472 | bytes 21364736 | tf_op jit(solution)/shard_map/bjtk,dk->bjtd/dot_general | solution.py:264
  207.8 12.9 %add_convert_fusion.x_ref = bf16[2,8,24,8192]{3,2,1,0:T(8,128)(2,1)} fusion(f32[2,8,24,8192]{3,2,1,0:T(8,128)} %fusion.8, bf16[2,8,24,512]{3,2,1,0:T(8,128)(2,1)S(1)} %get-tuple-element.31, bf16[1,8192,512]{2,1,0:T(8,128)(2,1)} %param.10), kind=kOutput, calls=%fused_computation.6 | convolution fusion | flops 3227516928 | bytes 27656192 | tf_op jit(solution)/shard_map/bjtk,dk->bjtd/dot_general | solution.py:267
  220.7 129.1 %shard_map.103 = bf16[2,8,24,8192]{3,2,1,0:T(8,128)(2,1)} custom-call(bf16[2,8,24,8192]{3,2,1,0:T(8,128)(2,1)} %add_convert_fusion.x_ref), custom_call_target="tpu_custom_call" | custom-call | tf_op jit(solution)/shard_map/pallas_call | solution.py:207
  349.8 4.8 %reduce_sum.52 = bf16[2,24,8192]{2,1,0:T(8,128)(2,1)} reduce(bf16[2,8,24,8192]{3,2,1,0:T(8,128)(2,1)} %shard_map.103, bf16[]{:T(256)} %constant.12.clone.1), dimensions={1}, to_apply=%region_6.7 | reduce | flops 2752512 | bytes 7077890 | tf_op jit(solution)/shard_map/reduce_sum | solution.py:271
  354.5 1.5 maximum_bitcast_fusion
  (50 shorter events, 14.2 us)
Async XLA Ops:
  7.2 348.9 %reduce-scatter.2.cloned.1.call-start = ((), (), s32[]{:S(2)}) async-start(), calls=%async_computation.1 | async-start | bytes 17825792 | tf_op jit(solution)/shard_map/reduce_scatter | solution.py:262
  15.5 2.0 copy-start
  130.4 6.4 %copy-start.2 = (bf16[1,1,128,4096]{2,3,1,0:T(8,128)(2,1)S(1)}, bf16[1,1,128,4096]{2,3,1,0:T(8,128)(2,1)}, u32[]{:S(2)}) copy-start(bf16[1,1,128,4096]{2,3,1,0:T(8,128)(2,1)} %copy.77) | copy-start | bytes 3145732
  150.2 3.9 %copy-start.1 = (bf16[1,1,128,4096]{2,3,1,0:T(8,128)(2,1)S(1)}, bf16[1,1,128,4096]{2,3,1,0:T(8,128)(2,1)}, u32[]{:S(2)}) copy-start(bf16[1,1,128,4096]{2,3,1,0:T(8,128)(2,1)} %copy.76) | copy-start | bytes 3145732
  150.2 3.9 %copy-start.4 = (bf16[192,4,128]{2,1,0:T(4,128)(2,1)S(1)}, bf16[192,4,128]{2,1,0:T(4,128)(2,1)}, u32[]{:S(2)}) copy-start(bf16[192,4,128]{2,1,0:T(4,128)(2,1)} %reshape_squeeze.18) | copy-start | bytes 589828
  156.9 2.9 copy-start.7
  166.2 0.7 copy-start.3
  182.2 0.9 copy-start.5
  182.2 0.9 copy-start.6
  183.1 6.4 %copy-start.8 = (f32[4,8,128]{2,1,0:T(8,128)S(1)}, f32[4,8,128]{2,1,0:T(8,128)}, u32[]{:S(2)}) copy-start(f32[4,8,128]{2,1,0:T(8,128)} %copy-done.7) | copy-start | bytes 49156
Sparse Core Ops, SparseCore 0:
  182.3 146.5 reduce-scatter.1

commit v5 on v4

--- a/solution.py
+++ b/solution.py
@@ -221,53 +221,47 @@
 def shards(queries, image_tokens, key_weight, value_weight, cotangent, tile_counts, text_lengths):
     n_section = lax.axis_size("section")
     samples_here, chunk, model_width = image_tokens.shape
-    if n_section == 8 and lax.axis_size("dp") == 16:
-        gathered = relay_gather(image_tokens, n_section)
-    else:
-        gathered = exchange(image_tokens, n_section, False, 0)
     image_len = n_section * chunk
     tile_len = image_len // MAX_TILES
     w_key = key_weight[0]
     w_value = value_weight[0]
     query_local = queries[0]
     cotan_local = cotangent[0]
+    late = [
+        lax.all_gather(image_tokens[i], "section", axis=0, tiled=True)
+        for i in range(1, samples_here)
+    ]
+    if n_section == 8 and lax.axis_size("dp") == 16:
+        first = relay_gather(image_tokens[:1], n_section)
+    else:
+        first = exchange(image_tokens[:1], n_section, False, 0)
+    token_list = [first.reshape(image_len, model_width)] + late
     query_list = []
-    key_list = []
-    value_list = []
-    keys_all = jnp.einsum(
-        "bjtd,dk->bjtk", gathered, w_key, preferred_element_type=jnp.float32
-    ).astype(jnp.bfloat16).reshape(samples_here, image_len, -1)
-    values_all = jnp.einsum(
-        "bjtd,dk->bjtk", gathered, w_value, preferred_element_type=jnp.float32
-    ).astype(jnp.bfloat16).reshape(samples_here, image_len, -1)
+    kv_term = None
+    image_list = []
     for sample_index in range(samples_here):
+        tokens = token_list[sample_index]
+        keys = jnp.dot(tokens, w_key, preferred_element_type=jnp.float32).astype(jnp.bfloat16)
+        values = jnp.dot(tokens, w_value, preferred_element_type=jnp.float32).astype(jnp.bfloat16)
         query_gradient, key_gradient, value_gradient = attend_one(
             query_local[sample_index],
-            keys_all[sample_index],
-            values_all[sample_index],
+            keys,
+            values,
             cotan_local[sample_index],
             tile_counts[sample_index] * tile_len,
             text_lengths[sample_index],
         )
         query_list.append(query_gradient)
-        key_list.append(key_gradient)
-        value_list.append(value_gradient)
+        kv_grads = jnp.concatenate([key_gradient, value_gradient], axis=-1)
+        part = jnp.einsum("td,tk->dk", tokens, kv_grads, preferred_element_type=jnp.float32)
+        kv_term = part if kv_term is None else kv_term + part
+        term = jnp.einsum("tk,dk->td", key_gradient, w_key, preferred_element_type=jnp.float32)
+        term = term + jnp.einsum("tk,dk->td", value_gradient, w_value, preferred_element_type=jnp.float32)
+        image_list.append(term.astype(jnp.bfloat16).reshape(n_section, chunk, model_width))
     query_out = jnp.stack(query_list)[None]
-    key_grads = jnp.stack(key_list).reshape(samples_here, n_section, chunk, -1)
-    value_grads = jnp.stack(value_list).reshape(samples_here, n_section, chunk, -1)
-    kv_grads = jnp.concatenate([key_grads, value_grads], axis=-1)
-    kv_term = jnp.einsum(
-        "bjtd,bjtk->dk", gathered, kv_grads, preferred_element_type=jnp.float32
-    )
     kv_sum = lax.psum_scatter(kv_term.astype(jnp.bfloat16), "dp", scatter_dimension=0, tiled=True)
-    kv_width = key_grads.shape[-1]
-    image_term = jnp.einsum(
-        "bjtk,dk->bjtd", key_grads, w_key, preferred_element_type=jnp.float32
-    )
-    image_term = image_term + jnp.einsum(
-        "bjtk,dk->bjtd", value_grads, w_value, preferred_element_type=jnp.float32
-    )
-    received = exchange(image_term.astype(jnp.bfloat16), n_section, True, 1)
+    kv_width = kv_sum.shape[-1] // 2
+    received = exchange(jnp.stack(image_list), n_section, True, 1)
     image_out = jnp.sum(received.astype(jnp.float32), axis=1).astype(jnp.bfloat16)
     return (
         query_out,

time: 370 us -> 362 us (0.978)
  Pallas kernels: 224 us -> 185 us
  matrix products: 98.5 us -> 126 us
    pallas_call x1, Pallas kernels: 94.9 us -> 56.5 us  [relay_gather(): pl.pallas_call(relay_gather_kernel, out_shape=jax.ShapeDtypeStruct((sampl...]
    dot_general x5 -> x10, matrix products: 56.9 us -> 81.9 us  [the longest x2 32.2 us: shards(): jnp.einsum('td,tk->dk', tokens, kv_grads, preferred_element_type=jnp.floa...]
    another operation x9 -> x0, local copies, waits for them, and re-layouts: 3.75 us -> none  [the longest x2 3.29 us: attend_one(): heads_of_keys = key_rows.reshape(total_keys, KEY_VALUE_HEADS, HEAD_SIZE)]
    unnamed x27 -> x45, local copies, waits for them, and re-layouts: 7.63 us -> 10 us
  transfers between devices with their start and end apart: 1 -> 2, of which waited for: 0 -> 0; matrix products, arithmetic and copies ran while one was open for 12% -> 29% of each run, Pallas kernels for 35% -> 51%
where the time goes in v5:
time: 362 us; the launch traced here: 359 us
  Pallas kernels  185 us (51%)
  matrix products  126 us (35%)
  local copies, waits for them, and re-layouts  21.9 us (6%)
  between operations  15.7 us (4%)
  other arithmetic  10.8 us (3%)
    pallas_call x1, Pallas kernels, exchange(): pl.pallas_call(functools.partial(exchange_kernel, n, scatter), out_shape=...  129 us
    pallas_call x1, Pallas kernels, relay_gather(): pl.pallas_call(relay_gather_kernel, out_shape=jax.ShapeDtypeStruct((sampl...  56.5 us
    dot_general x2, matrix products, shards(): jnp.einsum('td,tk->dk', tokens, kv_grads, preferred_element_type=jnp.floa...  32.2 us
    dot_general x2, matrix products, attend_one(): jnp.einsum('hgln,nhd->lhgd', score_grad, heads_of_keys, preferred_element...  13 us
    dot_general x2, matrix products, attend_one(): jnp.einsum('hgln,lhgd->nhd', score_grad, heads_of_queries, preferred_elem...  12.8 us
    dot_general x2, matrix products, shards(): jnp.einsum('tk,dk->td', value_gradient, w_value, preferred_element_type=j...  12.7 us
    dot_general x2, matrix products, shards(): jnp.einsum('tk,dk->td', key_gradient, w_key, preferred_element_type=jnp.f...  12.6 us
    dot_general x2, matrix products, shards(): jnp.dot(tokens, w_value, preferred_element_type=jnp.float32)  12.4 us
  transfers between devices with their start and end apart: 2, of which 0 were waited for; matrix products, arithmetic and copies ran while one was open for 29% of the time, Pallas kernels for 51%

profile of v5, /device:TPU:38, one launch (start us, length us, event | category | flops | bytes accessed | tf_op | source)
XLA Modules:
  0.0 359.4 jit_solution(7158230705175860924)
XLA Ops:
  18.7 56.5 %shard_map.102 = bf16[1,8,24,8192]{3,2,1,0:T(8,128)(2,1)} custom-call(bf16[1,24,8192]{2,1,0:T(8,128)(2,1)} %get-tuple-element.18.x_ref), custom_call_target="tpu_custom_call" | custom-call | tf_op jit(solution)/shard_map/pallas_call | solution.py:183
  75.3 6.3 %fusion.76 = bf16[192,512]{1,0:T(8,128)(2,1)S(1)} fusion(bf16[192,8192]{1,0:T(8,128)(2,1)} %bitcast.227, bf16[1,8192,512]{2,1,0:T(8,128)(2,1)} %param.10), kind=kOutput, calls=%fused_computation.77 | convolution fusion | flops 1610711040 | bytes 11730944 | tf_op jit(solution)/shard_map/dot_general | solution.py:245
  81.6 5.9 %fusion.68 = bf16[192,512]{1,0:T(8,128)(2,1)} fusion(bf16[192,8192]{1,0:T(8,128)(2,1)S(1)} %bitcast.228, bf16[1,8192,512]{2,1,0:T(8,128)(2,1)} %param.9), kind=kOutput, calls=%fused_computation.75 | convolution fusion | flops 1610711040 | bytes 11730944 | tf_op jit(solution)/shard_map/dot_general | solution.py:244
  90.4 3.5 fusion.99
  93.9 3.9 %fusion.150 = (f32[4,8,128]{2,1,0:T(8,128)S(1)}, f32[4,8,128,192]{2,3,1,0:T(8,128)}) fusion(pred[192]{0:T(512)(128)(4,1)S(1)} %iota_compare_fusion.1, bf16[128,4,8,128]{0,3,2,1:T(8,128)(2,1)} %bitcast.236, bf16[192,4,128,1]{2,1,0,3:T(4,128)(2,1)S(1)} %bitcast.242), kind=kOutput, calls=%fused_computation.141 | convolution fusion | flops 204472512 | bytes 4407488 | tf_op jit(solution)/shard_map/sub | solution.py:38
  98.4 5.9 %fusion.85 = bf16[4,24,8,128]{3,2,1,0:T(8,128)(2,1)S(1)} fusion(bf16[128,4,8,128]{0,3,2,1:T(8,128)(2,1)} %bitcast.237, f32[4,192,128,8]{2,1,3,0:T(8,128)} %fusion.99, f32[4,8,128,192]{2,3,1,0:T(8,128)} %get-tuple-element.27, f32[4,8,128]{2,1,0:T(8,128)S(1)} %get-tuple-element.26), kind=kOutput, calls=%fused_computation.80 | convolution fusion | flops 206934208 | bytes 7553024 | tf_op jit(solution)/shard_map/hgln,lhgd->nhd/dot_general | solution.py:52
  104.4 3.1 fusion.86
  107.5 13.2 %fusion.92 = f32[1024,8192]{1,0:T(8,128)} fusion(bf16[192,8192]{1,0:T(8,128)(2,1)S(1)} %bitcast.229, bf16[192,512]{1,0:T(8,128)(2,1)S(1)} %get-tuple-element.28, bf16[192,512]{1,0:T(8,128)(2,1)S(1)} %get-tuple-element.29), kind=kOutput, calls=%fused_computation.89 | convolution fusion | flops 3222011904 | bytes 37093376 | tf_op jit(solution)/shard_map/td,tk->dk/dot_general | solution.py:256
  120.7 6.1 %fusion.79 = bf16[192,512]{1,0:T(8,128)(2,1)S(1)} fusion(bf16[1,8192,512]{2,1,0:T(8,128)(2,1)} %param.10, bf16[1,192,8192]{2,1,0:T(8,128)(2,1)} %all-gather.3.cloned.1.call-done), kind=kOutput, calls=%fused_computation.78 | convolution fusion | flops 1610711040 | bytes 11730944 | tf_op jit(solution)/shard_map/dot_general | solution.py:245
  126.9 6.2 %fusion.71 = bf16[192,512]{1,0:T(8,128)(2,1)S(1)} fusion(bf16[1,8192,512]{2,1,0:T(8,128)(2,1)} %param.9, bf16[1,192,8192]{2,1,0:T(8,128)(2,1)} %all-gather.3.cloned.1.call-done), kind=kOutput, calls=%fused_computation.76 | convolution fusion | flops 1610711040 | bytes 11730944 | tf_op jit(solution)/shard_map/dot_general | solution.py:244
  133.2 2.3 fusion.100
  135.5 2.7 fusion.145
  138.8 2.7 fusion.89
  141.5 6.8 %fusion.84 = bf16[4,24,8,128]{3,2,1,0:T(8,128)(2,1)} fusion(bf16[128,4,8,128]{0,3,2,1:T(8,128)(2,1)} %bitcast.234, f32[4,192,128,8]{2,1,3,0:T(8,128)} %fusion.100, f32[4,8,128,192]{2,3,1,0:T(8,128)} %get-tuple-element.25, f32[4,8,128]{2,1,0:T(8,128)} %copy-done.17), kind=kOutput, calls=%fused_computation.79 | convolution fusion | flops 206934208 | bytes 7553024 | tf_op jit(solution)/shard_map/hgln,lhgd->nhd/dot_general | solution.py:52
  149.3 19.0 %fusion.4 = bf16[8192,1024]{0,1:T(8,128)(2,1)} fusion(f32[1024,8192]{1,0:T(8,128)} %fusion.92, bf16[1,192,8192]{2,1,0:T(8,128)(2,1)S(1)} %copy-done.4, bf16[192,512]{1,0:T(8,128)(2,1)S(1)} %get-tuple-element.30, bf16[192,512]{1,0:T(8,128)(2,1)S(1)} %get-tuple-element.31), kind=kOutput, calls=%fused_computation.5 | convolution fusion | flops 3238789120 | bytes 53870592 | tf_op jit(solution)/shard_map/td,tk->dk/dot_general | solution.py:256
  169.3 5.9 %convolution_convert_fusion.1 = bf16[4,128,8,128]{3,1,2,0:T(8,128)(2,1)S(1)} fusion(f32[4,192,128,8]{2,1,3,0:T(8,128)} %fusion.99, bf16[192,4,128,1]{2,1,0,3:T(4,128)(2,1)S(1)} %bitcast.243, f32[4,8,128,192]{2,3,1,0:T(8,128)} %get-tuple-element.27, f32[4,8,128]{2,1,0:T(8,128)S(1)} %copy-done.16), kind=kOutput, calls=%fused_computation.62 | convolution fusion | flops 207360192 | bytes 7553024 | tf_op jit(solution)/shard_map/hgln,nhd->lhgd/dot_general | solution.py:49
  176.4 6.2 %fusion.15 = f32[192,8192]{1,0:T(8,128)S(1)} fusion(bf16[1,8192,512]{2,1,0:T(8,128)(2,1)} %param.9, bf16[4,24,8,128]{3,2,1,0:T(8,128)(2,1)S(1)} %copy-done.8), kind=kOutput, calls=%fused_computation.18 | convolution fusion | flops 1610612736 | bytes 14876672 | tf_op jit(solution)/shard_map/tk,dk->td/dot_general | solution.py:258
  182.7 6.2 %fusion.5 = bf16[192,8192]{1,0:T(8,128)(2,1)S(1)} fusion(f32[192,8192]{1,0:T(8,128)S(1)} %fusion.15, bf16[1,8192,512]{2,1,0:T(8,128)(2,1)} %param.10, bf16[4,24,8,128]{3,2,1,0:T(8,128)(2,1)S(1)} %fusion.86), kind=kOutput, calls=%fused_computation.8 | convolution fusion | flops 1613758464 | bytes 18022400 | tf_op jit(solution)/shard_map/tk,dk->td/dot_general | solution.py:259
  189.0 7.1 %convolution_convert_fusion = bf16[4,128,8,128]{3,1,2,0:T(8,128)(2,1)} fusion(f32[4,192,128,8]{2,1,3,0:T(8,128)} %fusion.100, bf16[192,4,128,1]{2,1,0,3:T(4,128)(2,1)} %bitcast.245, f32[4,8,128,192]{2,3,1,0:T(8,128)} %get-tuple-element.25, f32[4,8,128]{2,1,0:T(8,128)S(1)} %copy-done.18), kind=kOutput, calls=%fused_computation.61 | convolution fusion | flops 207360192 | bytes 7553024 | tf_op jit(solution)/shard_map/hgln,nhd->lhgd/dot_general | solution.py:49
  198.4 6.4 %fusion.13 = f32[192,8192]{1,0:T(8,128)S(1)} fusion(bf16[1,8192,512]{2,1,0:T(8,128)(2,1)} %param.9, bf16[4,24,8,128]{3,2,1,0:T(8,128)(2,1)S(1)} %copy-done.9), kind=kOutput, calls=%fused_computation.16 | convolution fusion | flops 1610612736 | bytes 14876672 | tf_op jit(solution)/shard_map/tk,dk->td/dot_general | solution.py:258
  204.8 6.4 %fusion.6 = bf16[192,8192]{1,0:T(8,128)(2,1)S(1)} fusion(f32[192,8192]{1,0:T(8,128)S(1)} %fusion.13, bf16[1,8192,512]{2,1,0:T(8,128)(2,1)} %param.10, bf16[4,24,8,128]{3,2,1,0:T(8,128)(2,1)S(1)} %fusion.89), kind=kOutput, calls=%fused_computation.9 | convolution fusion | flops 1613758464 | bytes 18022400 | tf_op jit(solution)/shard_map/tk,dk->td/dot_general | solution.py:259
  211.2 3.2 pad_maximum_fusion.x_ref
  214.4 128.5 %shard_map.103 = bf16[2,8,24,8192]{3,2,1,0:T(8,128)(2,1)} custom-call(bf16[2,8,24,8192]{3,2,1,0:T(8,128)(2,1)} %pad_maximum_fusion.x_ref), custom_call_target="tpu_custom_call" | custom-call | tf_op jit(solution)/shard_map/pallas_call | solution.py:207
  342.9 4.9 %reduce_sum.52 = bf16[2,24,8192]{2,1,0:T(8,128)(2,1)} reduce(bf16[2,8,24,8192]{3,2,1,0:T(8,128)(2,1)} %shard_map.103, bf16[]{:T(256)} %constant.12.clone.1), dimensions={1}, to_apply=%region_6.7 | reduce | flops 2752512 | bytes 7077890 | tf_op jit(solution)/shard_map/reduce_sum | solution.py:265
  (69 shorter events, 24.7 us)
Async XLA Ops:
  7.2 3.9 %copy-start.13 = (s32[2]{0:T(128)S(1)}, s32[2]{0:T(128)}, u32[]{:S(2)}) copy-start(s32[2]{0:T(128)} %param.12) | copy-start | bytes 28
  7.2 113.5 %all-gather.3.cloned.1.call-start = ((), (), s32[]{:S(2)}) async-start(), calls=%async_computation.2 | async-start | bytes 3538944 | tf_op jit(solution)/shard_map/all_gather | solution.py:231
  9.3 340.0 %reduce-scatter.2.cloned.1.call-start = ((), (), s32[]{:S(2)}) async-start(), calls=%async_computation.1 | async-start | bytes 17825792 | tf_op jit(solution)/shard_map/reduce_scatter | solution.py:262
  14.2 2.0 copy-start.5
  75.3 6.3 %copy-start = (bf16[1,8,24,8192]{3,2,1,0:T(8,128)(2,1)S(1)}, bf16[1,8,24,8192]{3,2,1,0:T(8,128)(2,1)}, u32[]{:S(2)}) copy-start(bf16[1,8,24,8192]{3,2,1,0:T(8,128)(2,1)} %shard_map.102) | copy-start | bytes 9437188
  81.6 6.9 %copy-start.14 = (s32[2]{0:T(128)S(1)}, s32[2]{0:T(128)}, u32[]{:S(2)}) copy-start(s32[2]{0:T(128)} %param.13) | copy-start | bytes 28
  88.5 9.3 %copy-start.10 = (bf16[192,4,128]{2,1,0:T(4,128)(2,1)}, bf16[192,4,128]{2,1,0:T(4,128)(2,1)S(1)}, u32[]{:S(2)}) copy-start(bf16[192,4,128]{2,1,0:T(4,128)(2,1)S(1)} %reshape.76) | copy-start | bytes 589828
  97.8 0.6 copy-start.15
  104.4 3.1 copy-start.7
  126.9 6.3 %copy-start.1 = (bf16[16,8,32,128]{3,2,1,0:T(8,128)(2,1)S(1)}, bf16[16,8,32,128]{3,2,1,0:T(8,128)(2,1)}, u32[]{:S(2)}) copy-start(bf16[16,8,32,128]{3,2,1,0:T(8,128)(2,1)} %copy.78) | copy-start | bytes 3145732
  133.1 2.4 copy-start.6
  133.1 5.1 %copy-start.12 = (bf16[192,4,128]{2,1,0:T(4,128)(2,1)}, bf16[192,4,128]{2,1,0:T(4,128)(2,1)S(1)}, u32[]{:S(2)}) copy-start(bf16[192,4,128]{2,1,0:T(4,128)(2,1)S(1)} %reshape.78) | copy-start | bytes 589828
  138.2 0.6 copy-start.17
  141.5 7.8 %copy-start.4 = (bf16[1,192,8192]{2,1,0:T(8,128)(2,1)S(1)}, bf16[1,192,8192]{2,1,0:T(8,128)(2,1)}, u32[]{:S(2)}) copy-start(bf16[1,192,8192]{2,1,0:T(8,128)(2,1)} %all-gather.3.cloned.1.call-done) | copy-start | bytes 9437188
  168.3 0.9 copy-start.11
  168.3 0.9 copy-start.16
  169.3 7.2 %copy-start.8 = (bf16[4,24,8,128]{3,2,1,0:T(8,128)(2,1)S(1)}, bf16[4,24,8,128]{3,2,1,0:T(8,128)(2,1)}, u32[]{:S(2)}) copy-start(bf16[4,24,8,128]{3,2,1,0:T(8,128)(2,1)} %copy-done.7) | copy-start | bytes 589828
  182.7 6.3 %copy-start.18 = (f32[4,8,128]{2,1,0:T(8,128)S(1)}, f32[4,8,128]{2,1,0:T(8,128)}, u32[]{:S(2)}) copy-start(f32[4,8,128]{2,1,0:T(8,128)} %copy-done.17) | copy-start | bytes 49156
  189.0 9.4 %copy-start.9 = (bf16[4,24,8,128]{3,2,1,0:T(8,128)(2,1)S(1)}, bf16[4,24,8,128]{3,2,1,0:T(8,128)(2,1)}, u32[]{:S(2)}) copy-start(bf16[4,24,8,128]{3,2,1,0:T(8,128)(2,1)} %fusion.84) | copy-start | bytes 589828
  342.9 4.9 %copy-start.2 = (bf16[1,128,4096]{2,1,0:T(8,128)(2,1)S(1)}, bf16[1,128,4096]{2,1,0:T(8,128)(2,1)}, u32[]{:S(2)}) copy-start(bf16[1,128,4096]{2,1,0:T(8,128)(2,1)} %copy.35) | copy-start | bytes 3145732
  342.9 4.9 %copy-start.3 = (bf16[1,128,4096]{2,1,0:T(8,128)(2,1)S(1)}, bf16[1,128,4096]{2,1,0:T(8,128)(2,1)}, u32[]{:S(2)}) copy-start(bf16[1,128,4096]{2,1,0:T(8,128)(2,1)} %copy.36) | copy-start | bytes 3145732
Sparse Core Ops, SparseCore 0:
  10.9 87.6 all-gather.2
  168.5 151.8 reduce-scatter.1

commit v6 on v5

--- a/solution.py
+++ b/solution.py
@@ -237,7 +237,8 @@
         first = exchange(image_tokens[:1], n_section, False, 0)
     token_list = [first.reshape(image_len, model_width)] + late
     query_list = []
-    kv_term = None
+    key_list = []
+    value_list = []
     image_list = []
     for sample_index in range(samples_here):
         tokens = token_list[sample_index]
@@ -252,22 +253,30 @@
             text_lengths[sample_index],
         )
         query_list.append(query_gradient)
-        kv_grads = jnp.concatenate([key_gradient, value_gradient], axis=-1)
-        part = jnp.einsum("td,tk->dk", tokens, kv_grads, preferred_element_type=jnp.float32)
-        kv_term = part if kv_term is None else kv_term + part
+        key_list.append(key_gradient)
+        value_list.append(value_gradient)
         term = jnp.einsum("tk,dk->td", key_gradient, w_key, preferred_element_type=jnp.float32)
         term = term + jnp.einsum("tk,dk->td", value_gradient, w_value, preferred_element_type=jnp.float32)
         image_list.append(term.astype(jnp.bfloat16).reshape(n_section, chunk, model_width))
+    all_tokens = jnp.concatenate(token_list, axis=0)
+    value_term = jnp.einsum(
+        "td,tk->dk", all_tokens, jnp.concatenate(value_list, axis=0),
+        preferred_element_type=jnp.float32,
+    ).astype(jnp.bfloat16)
+    value_sum = lax.psum_scatter(value_term, "dp", scatter_dimension=0, tiled=True)
+    key_term = jnp.einsum(
+        "td,tk->dk", all_tokens, jnp.concatenate(key_list, axis=0),
+        preferred_element_type=jnp.float32,
+    ).astype(jnp.bfloat16)
+    key_sum = lax.psum_scatter(key_term, "dp", scatter_dimension=0, tiled=True)
     query_out = jnp.stack(query_list)[None]
-    kv_sum = lax.psum_scatter(kv_term.astype(jnp.bfloat16), "dp", scatter_dimension=0, tiled=True)
-    kv_width = kv_sum.shape[-1] // 2
     received = exchange(jnp.stack(image_list), n_section, True, 1)
     image_out = jnp.sum(received.astype(jnp.float32), axis=1).astype(jnp.bfloat16)
     return (
         query_out,
         image_out,
-        kv_sum[:, :kv_width][None],
-        kv_sum[:, kv_width:][None],
+        key_sum[None],
+        value_sum[None],
     )
 
 

time: 362 us -> 347 us (0.959)
  matrix products: 126 us -> 111 us
  waiting for transfers between devices: 0.04 us -> 9.77 us
  Pallas kernels: 185 us -> 179 us
    dot_general x2, matrix products: 32.2 us -> 16.4 us  [the longest x1 9.69 us: shards(): jnp.einsum('td,tk->dk', all_tokens, jnp.concatenate(key_list, axis=0), pr...]
    all_gather x1, waiting for transfers between devices: 0.01 us -> 9.72 us  [shards(): lax.all_gather(image_tokens[i], 'section', axis=0, tiled=True)]
    pallas_call x1, Pallas kernels: 129 us -> 123 us  [exchange(): pl.pallas_call(functools.partial(exchange_kernel, n, scatter), out_shape=...]
    unnamed x45, local copies, waits for them, and re-layouts: 10 us -> 5.83 us
  transfers between devices with their start and end apart: 2 -> 3, of which waited for: 0 -> 1; matrix products, arithmetic and copies ran while one was open for 29% -> 34% of each run, Pallas kernels for 51% -> 52%
where the time goes in v6:
time: 347 us
  Pallas kernels  179 us (52%)
  matrix products  111 us (32%)
  local copies, waits for them, and re-layouts  20.6 us (6%)
  between operations  15.4 us (4%)
  other arithmetic  10.9 us (3%)
  waiting for transfers between devices  9.77 us (3%)
    pallas_call x1, Pallas kernels, exchange(): pl.pallas_call(functools.partial(exchange_kernel, n, scatter), out_shape=...  123 us
    pallas_call x1, Pallas kernels, relay_gather(): pl.pallas_call(relay_gather_kernel, out_shape=jax.ShapeDtypeStruct((sampl...  55.3 us
    dot_general x2, matrix products, shards(): jnp.dot(tokens, w_value, preferred_element_type=jnp.float32)  13.2 us
    dot_general x2, matrix products, attend_one(): jnp.einsum('hgln,nhd->lhgd', score_grad, heads_of_keys, preferred_element...  13.1 us
    dot_general x2, matrix products, shards(): jnp.dot(tokens, w_key, preferred_element_type=jnp.float32)  13 us
    dot_general x2, matrix products, attend_one(): jnp.einsum('hgln,lhgd->nhd', score_grad, heads_of_queries, preferred_elem...  13 us
    dot_general x2, matrix products, shards(): jnp.einsum('tk,dk->td', key_gradient, w_key, preferred_element_type=jnp.f...  12.6 us
    dot_general x2, matrix products, shards(): jnp.einsum('tk,dk->td', value_gradient, w_value, preferred_element_type=j...  12.6 us
  transfers between devices with their start and end apart: 3, of which 1 were waited for; matrix products, arithmetic and copies ran while one was open for 34% of the time, Pallas kernels for 52%

profile of v6, /device:TPU:38, one launch (start us, length us, event | category | flops | bytes accessed | tf_op | source)
XLA Modules:
  0.0 346.6 jit_solution(3184333591908375182)
XLA Ops:
  17.5 55.3 %shard_map.102 = bf16[1,8,24,8192]{3,2,1,0:T(8,128)(2,1)} custom-call(bf16[1,24,8192]{2,1,0:T(8,128)(2,1)} %get-tuple-element.8.x_ref), custom_call_target="tpu_custom_call" | custom-call | tf_op jit(solution)/shard_map/pallas_call | solution.py:183
  72.8 6.2 %fusion.64 = bf16[192,512]{1,0:T(8,128)(2,1)S(1)} fusion(bf16[192,8192]{1,0:T(8,128)(2,1)} %bitcast.224, bf16[1,8192,512]{2,1,0:T(8,128)(2,1)} %param.9), kind=kOutput, calls=%fused_computation.73 | convolution fusion | flops 1610711040 | bytes 11730944 | tf_op jit(solution)/shard_map/dot_general | solution.py:245
  80.4 2.8 fusion.143
  83.2 2.7 fusion.78
  87.3 9.7 %all-gather.3.cloned.1.call-done = bf16[1,192,8192]{2,1,0:T(8,128)(2,1)} async-done(((bf16[1,24,8192]{2,1,0:T(8,128)(2,1)}), bf16[1,192,8192]{2,1,0:T(8,128)(2,1)}) %all-gather.3.cloned.1.call-update) | async-done | bytes 3145744 | tf_op jit(solution)/shard_map/all_gather | solution.py:231
  97.0 6.8 %fusion.67 = bf16[192,512]{1,0:T(8,128)(2,1)} fusion(bf16[1,8192,512]{2,1,0:T(8,128)(2,1)} %param.9, bf16[1,192,8192]{2,1,0:T(8,128)(2,1)} %all-gather.3.cloned.1.call-done), kind=kOutput, calls=%fused_computation.74 | convolution fusion | flops 1610711040 | bytes 11730944 | tf_op jit(solution)/shard_map/dot_general | solution.py:245
  104.8 3.4 fusion.138
  108.2 2.8 fusion.81
  112.1 6.7 %convolution_convert_fusion = bf16[8192,512]{1,0:T(8,128)(2,1)} fusion(bf16[192,8192]{1,0:T(8,128)(2,1)S(1)} %bitcast.245, bf16[192,8192]{1,0:T(8,128)(2,1)S(1)} %bitcast.226, bf16[192,512]{1,0:T(8,128)(2,1)S(1)} %bitcast.243, bf16[192,512]{1,0:T(8,128)(2,1)S(1)} %bitcast.240), kind=kOutput, calls=%fused_computation.4 | convolution fusion | flops 3238789120 | bytes 15073280 | tf_op jit(solution)/shard_map/td,tk->dk/dot_general | solution.py:262
  119.1 6.8 %fusion.70 = bf16[192,512]{1,0:T(8,128)(2,1)} fusion(bf16[192,8192]{1,0:T(8,128)(2,1)} %bitcast.225, bf16[1,8192,512]{2,1,0:T(8,128)(2,1)} %param.10), kind=kOutput, calls=%fused_computation.75 | convolution fusion | flops 1610711040 | bytes 11730944 | tf_op jit(solution)/shard_map/dot_general | solution.py:246
  127.6 3.2 fusion.90
  130.9 5.9 %fusion.77 = bf16[4,24,8,128]{3,2,1,0:T(8,128)(2,1)S(1)} fusion(bf16[128,4,8,128]{0,3,2,1:T(8,128)(2,1)S(1)} %bitcast.231, f32[4,192,128,8]{2,1,3,0:T(8,128)} %fusion.90, f32[4,8,128,192]{2,3,1,0:T(8,128)} %get-tuple-element.17, f32[4,8,128]{2,1,0:T(8,128)} %copy-done.17), kind=kOutput, calls=%fused_computation.78 | convolution fusion | flops 206934208 | bytes 7553024 | tf_op jit(solution)/shard_map/hgln,lhgd->nhd/dot_general | solution.py:52
  137.5 6.4 %fusion.73 = bf16[192,512]{1,0:T(8,128)(2,1)S(1)} fusion(bf16[1,8192,512]{2,1,0:T(8,128)(2,1)} %param.10, bf16[1,192,8192]{2,1,0:T(8,128)(2,1)} %all-gather.3.cloned.1.call-done), kind=kOutput, calls=%fused_computation.76 | convolution fusion | flops 1610711040 | bytes 11730944 | tf_op jit(solution)/shard_map/dot_general | solution.py:246
  146.3 7.1 %fusion.76 = bf16[4,24,8,128]{3,2,1,0:T(8,128)(2,1)} fusion(bf16[128,4,8,128]{0,3,2,1:T(8,128)(2,1)} %bitcast.228, f32[4,192,128,8]{2,1,3,0:T(8,128)} %fusion.91, f32[4,8,128,192]{2,3,1,0:T(8,128)} %get-tuple-element.15, f32[4,8,128]{2,1,0:T(8,128)} %get-tuple-element.14), kind=kOutput, calls=%fused_computation.77 | convolution fusion | flops 206934208 | bytes 7553024 | tf_op jit(solution)/shard_map/hgln,lhgd->nhd/dot_general | solution.py:52
  154.3 9.7 %convolution_convert_fusion.1 = bf16[8192,512]{1,0:T(8,128)(2,1)} fusion(bf16[192,8192]{1,0:T(8,128)(2,1)} %bitcast.244, bf16[192,8192]{1,0:T(8,128)(2,1)S(1)} %bitcast.227, bf16[192,512]{1,0:T(8,128)(2,1)S(1)} %bitcast.242, bf16[192,512]{1,0:T(8,128)(2,1)} %bitcast.241), kind=kOutput, calls=%fused_computation.5 | convolution fusion | flops 3238789120 | bytes 15073280 | tf_op jit(solution)/shard_map/td,tk->dk/dot_general | solution.py:267
  164.9 6.1 %convolution_convert_fusion.3 = bf16[4,128,8,128]{3,1,2,0:T(8,128)(2,1)S(1)} fusion(f32[4,192,128,8]{2,1,3,0:T(8,128)} %fusion.90, bf16[192,4,128,1]{2,1,0,3:T(4,128)(2,1)S(1)} %bitcast.237, f32[4,8,128,192]{2,3,1,0:T(8,128)} %get-tuple-element.17, f32[4,8,128]{2,1,0:T(8,128)S(1)} %copy-done.18), kind=kOutput, calls=%fused_computation.60 | convolution fusion | flops 207360192 | bytes 7553024 | tf_op jit(solution)/shard_map/hgln,nhd->lhgd/dot_general | solution.py:49
  172.7 6.4 %fusion.14 = f32[192,8192]{1,0:T(8,128)S(1)} fusion(bf16[1,8192,512]{2,1,0:T(8,128)(2,1)} %param.9, bf16[4,24,8,128]{3,2,1,0:T(8,128)(2,1)S(1)} %copy-done.10), kind=kOutput, calls=%fused_computation.18 | convolution fusion | flops 1610612736 | bytes 14876672 | tf_op jit(solution)/shard_map/tk,dk->td/dot_general | solution.py:258
  179.1 6.3 %fusion.4 = bf16[192,8192]{1,0:T(8,128)(2,1)S(1)} fusion(f32[192,8192]{1,0:T(8,128)S(1)} %fusion.14, bf16[1,8192,512]{2,1,0:T(8,128)(2,1)} %param.10, bf16[4,24,8,128]{3,2,1,0:T(8,128)(2,1)S(1)} %fusion.78), kind=kOutput, calls=%fused_computation.8 | convolution fusion | flops 1613758464 | bytes 18022400 | tf_op jit(solution)/shard_map/tk,dk->td/dot_general | solution.py:259
  185.4 6.9 %convolution_convert_fusion.2 = bf16[4,128,8,128]{3,1,2,0:T(8,128)(2,1)} fusion(f32[4,192,128,8]{2,1,3,0:T(8,128)} %fusion.91, bf16[192,4,128,1]{2,1,0,3:T(4,128)(2,1)} %bitcast.239, f32[4,8,128,192]{2,3,1,0:T(8,128)} %get-tuple-element.15, f32[4,8,128]{2,1,0:T(8,128)S(1)} %copy-done.19), kind=kOutput, calls=%fused_computation.59 | convolution fusion | flops 207360192 | bytes 7553024 | tf_op jit(solution)/shard_map/hgln,nhd->lhgd/dot_general | solution.py:49
  194.7 6.2 %fusion.12 = f32[192,8192]{1,0:T(8,128)S(1)} fusion(bf16[1,8192,512]{2,1,0:T(8,128)(2,1)} %param.9, bf16[4,24,8,128]{3,2,1,0:T(8,128)(2,1)S(1)} %copy-done.8), kind=kOutput, calls=%fused_computation.16 | convolution fusion | flops 1610612736 | bytes 14876672 | tf_op jit(solution)/shard_map/tk,dk->td/dot_general | solution.py:258
  200.9 6.2 %fusion.5 = bf16[192,8192]{1,0:T(8,128)(2,1)S(1)} fusion(f32[192,8192]{1,0:T(8,128)S(1)} %fusion.12, bf16[1,8192,512]{2,1,0:T(8,128)(2,1)} %param.10, bf16[4,24,8,128]{3,2,1,0:T(8,128)(2,1)S(1)} %fusion.81), kind=kOutput, calls=%fused_computation.9 | convolution fusion | flops 1613758464 | bytes 18022400 | tf_op jit(solution)/shard_map/tk,dk->td/dot_general | solution.py:259
  207.1 3.2 pad_maximum_fusion.x_ref
  210.3 123.3 %shard_map.103 = bf16[2,8,24,8192]{3,2,1,0:T(8,128)(2,1)} custom-call(bf16[2,8,24,8192]{3,2,1,0:T(8,128)(2,1)} %pad_maximum_fusion.x_ref), custom_call_target="tpu_custom_call" | custom-call | tf_op jit(solution)/shard_map/pallas_call | solution.py:207
  333.7 4.9 %reduce_sum.52 = bf16[2,24,8192]{2,1,0:T(8,128)(2,1)} reduce(bf16[2,8,24,8192]{3,2,1,0:T(8,128)(2,1)} %shard_map.103, bf16[]{:T(256)} %constant.12.clone.1), dimensions={1}, to_apply=%region_6.7 | reduce | flops 2752512 | bytes 7077890 | tf_op jit(solution)/shard_map/reduce_sum | solution.py:274
  (73 shorter events, 26.0 us)
Async XLA Ops:
  7.2 89.9 %all-gather.3.cloned.1.call-start = ((), (), s32[]{:S(2)}) async-start(), calls=%async_computation.4 | async-start | bytes 3538944 | tf_op jit(solution)/shard_map/all_gather | solution.py:231
  9.3 330.8 %reduce-scatter.5.cloned.1.call-start = ((), (), s32[]{:S(2)}) async-start(), calls=%async_computation.3 | async-start | bytes 8912896 | tf_op jit(solution)/shard_map/reduce_scatter | solution.py:266
  14.9 2.0 copy-start.4
  72.8 6.4 %copy-start.15 = (s32[2]{0:T(128)S(1)}, s32[2]{0:T(128)}, u32[]{:S(2)}) copy-start(s32[2]{0:T(128)} %param.13) | copy-start | bytes 28
  72.8 7.6 %copy-start.6 = (bf16[1,1,128,4096]{2,3,1,0:T(8,128)(2,1)S(1)}, bf16[1,1,128,4096]{2,3,1,0:T(8,128)(2,1)}, u32[]{:S(2)}) copy-start(bf16[1,1,128,4096]{2,3,1,0:T(8,128)(2,1)} %copy.67) | copy-start | bytes 3145732
  79.1 4.1 %copy-start.11 = (bf16[192,4,128]{2,1,0:T(4,128)(2,1)}, bf16[192,4,128]{2,1,0:T(4,128)(2,1)S(1)}, u32[]{:S(2)}) copy-start(bf16[192,4,128]{2,1,0:T(4,128)(2,1)S(1)} %reshape.76) | copy-start | bytes 589828
  83.2 2.7 copy-start.17
  87.3 17.5 %copy-start.5 = (bf16[1,1,128,4096]{2,3,1,0:T(8,128)(2,1)S(1)}, bf16[1,1,128,4096]{2,3,1,0:T(8,128)(2,1)}, u32[]{:S(2)}) copy-start(bf16[1,1,128,4096]{2,3,1,0:T(8,128)(2,1)} %copy.68) | copy-start | bytes 3145732
  104.8 3.4 copy-start.13
  108.2 2.9 copy-start.2
  108.2 2.9 copy-start.14
  108.2 3.9 %copy-start.16 = (bf16[1,192,8192]{2,1,0:T(8,128)(2,1)S(1)}, bf16[1,192,8192]{2,1,0:T(8,128)(2,1)}, u32[]{:S(2)}) copy-start(bf16[1,192,8192]{2,1,0:T(8,128)(2,1)} %all-gather.3.cloned.1.call-done) | copy-start | bytes 9437188
  118.9 221.2 %reduce-scatter.3.cloned.1.call-start = ((), (), s32[]{:S(2)}) async-start(), calls=%async_computation.2 | async-start | bytes 8912896 | tf_op jit(solution)/shard_map/reduce_scatter | solution.py:271
  125.9 5.0 %copy-start.7 = (bf16[1,1,128,4096]{2,3,1,0:T(8,128)(2,1)S(1)}, bf16[1,1,128,4096]{2,3,1,0:T(8,128)(2,1)}, u32[]{:S(2)}) copy-start(bf16[1,1,128,4096]{2,3,1,0:T(8,128)(2,1)} %copy.67) | copy-start | bytes 3145732
  136.8 7.1 %copy-start.9 = (bf16[4,24,8,128]{3,2,1,0:T(8,128)(2,1)}, bf16[4,24,8,128]{3,2,1,0:T(8,128)(2,1)S(1)}, u32[]{:S(2)}) copy-start(bf16[4,24,8,128]{3,2,1,0:T(8,128)(2,1)S(1)} %fusion.77) | copy-start | bytes 589828
  146.3 8.0 %copy-start.3 = (bf16[1,8,24,8192]{3,2,1,0:T(8,128)(2,1)S(1)}, bf16[1,8,24,8192]{3,2,1,0:T(8,128)(2,1)}, u32[]{:S(2)}) copy-start(bf16[1,8,24,8192]{3,2,1,0:T(8,128)(2,1)} %shard_map.102) | copy-start | bytes 9437188
  164.0 0.9 copy-start.12
  164.0 0.9 copy-start.18
  164.9 7.7 %copy-start.10 = (bf16[4,24,8,128]{3,2,1,0:T(8,128)(2,1)S(1)}, bf16[4,24,8,128]{3,2,1,0:T(8,128)(2,1)}, u32[]{:S(2)}) copy-start(bf16[4,24,8,128]{3,2,1,0:T(8,128)(2,1)} %copy-done.9) | copy-start | bytes 589828
  179.1 6.4 %copy-start.19 = (f32[4,8,128]{2,1,0:T(8,128)S(1)}, f32[4,8,128]{2,1,0:T(8,128)}, u32[]{:S(2)}) copy-start(f32[4,8,128]{2,1,0:T(8,128)} %get-tuple-element.14) | copy-start | bytes 49156
  185.4 9.2 %copy-start.8 = (bf16[4,24,8,128]{3,2,1,0:T(8,128)(2,1)S(1)}, bf16[4,24,8,128]{3,2,1,0:T(8,128)(2,1)}, u32[]{:S(2)}) copy-start(bf16[4,24,8,128]{3,2,1,0:T(8,128)(2,1)} %fusion.76) | copy-start | bytes 589828
  333.7 4.9 %copy-start = (bf16[1,128,4096]{2,1,0:T(8,128)(2,1)S(1)}, bf16[1,128,4096]{2,1,0:T(8,128)(2,1)}, u32[]{:S(2)}) copy-start(bf16[1,128,4096]{2,1,0:T(8,128)(2,1)} %copy.33) | copy-start | bytes 3145732
  333.7 4.9 %copy-start.1 = (bf16[1,128,4096]{2,1,0:T(8,128)(2,1)S(1)}, bf16[1,128,4096]{2,1,0:T(8,128)(2,1)}, u32[]{:S(2)}) copy-start(bf16[1,128,4096]{2,1,0:T(8,128)(2,1)} %copy.34) | copy-start | bytes 3145732
Sparse Core Ops, SparseCore 0:
  10.9 86.1 all-gather.2
  119.0 72.6 reduce-scatter.4
  194.6 110.0 reduce-scatter.2

commit v7 on v6

--- a/solution.py
+++ b/solution.py
@@ -218,6 +218,16 @@
     )(x)
 
 
+def scatter_by_permutes(blocks, n):
+    me = lax.axis_index("section")
+    total = lax.dynamic_index_in_dim(blocks, me, axis=0, keepdims=False).astype(jnp.float32)
+    for k in range(1, n):
+        outgoing = lax.dynamic_index_in_dim(blocks, lax.rem(me + k, n), axis=0, keepdims=False)
+        incoming = lax.ppermute(outgoing, "section", perm=[(i, (i + k) % n) for i in range(n)])
+        total = total + incoming.astype(jnp.float32)
+    return total.astype(jnp.bfloat16)
+
+
 def shards(queries, image_tokens, key_weight, value_weight, cotangent, tile_counts, text_lengths):
     n_section = lax.axis_size("section")
     samples_here, chunk, model_width = image_tokens.shape
@@ -258,6 +268,9 @@
         term = jnp.einsum("tk,dk->td", key_gradient, w_key, preferred_element_type=jnp.float32)
         term = term + jnp.einsum("tk,dk->td", value_gradient, w_value, preferred_element_type=jnp.float32)
         image_list.append(term.astype(jnp.bfloat16).reshape(n_section, chunk, model_width))
+        if sample_index == 0 and samples_here > 1:
+            image_list[0], token_list[1] = lax.optimization_barrier((image_list[0], token_list[1]))
+            image_list[0] = scatter_by_permutes(image_list[0], n_section)
     all_tokens = jnp.concatenate(token_list, axis=0)
     value_term = jnp.einsum(
         "td,tk->dk", all_tokens, jnp.concatenate(value_list, axis=0),
@@ -270,8 +283,9 @@
     ).astype(jnp.bfloat16)
     key_sum = lax.psum_scatter(key_term, "dp", scatter_dimension=0, tiled=True)
     query_out = jnp.stack(query_list)[None]
-    received = exchange(jnp.stack(image_list), n_section, True, 1)
-    image_out = jnp.sum(received.astype(jnp.float32), axis=1).astype(jnp.bfloat16)
+    received = exchange(jnp.stack(image_list[1:]), n_section, True, 1)
+    late_sums = jnp.sum(received.astype(jnp.float32), axis=1).astype(jnp.bfloat16)
+    image_out = jnp.concatenate([image_list[0][None], late_sums], axis=0)
     return (
         query_out,
         image_out,

time: 347 us -> 350 us (level); the launches traced: 347 us -> 343 us
  Pallas kernels: 179 us -> 116 us
  starting transfers between devices: 0.3 us -> 51.6 us
  waiting for transfers between devices: 9.77 us -> 14.3 us
  matrix products: 111 us -> 115 us
    pallas_call x1, Pallas kernels: 123 us -> 59 us  [exchange(): pl.pallas_call(functools.partial(exchange_kernel, n, scatter), out_shape=...]
    ppermute x0 -> x7, starting transfers between devices: none -> 51.5 us  [scatter_by_permutes(): lax.ppermute(outgoing, 'section', perm=[(i, (i + k) % n) for i in range(n)])]
    ppermute x0 -> x7, waiting for transfers between devices: none -> 14.3 us  [scatter_by_permutes(): lax.ppermute(outgoing, 'section', perm=[(i, (i + k) % n) for i in range(n)])]
    all_gather x1, waiting for transfers between devices: 9.72 us -> 0.02 us  [shards(): lax.all_gather(image_tokens[i], 'section', axis=0, tiled=True)]
    unnamed x45 -> x29, local copies, waits for them, and re-layouts: 5.83 us -> 7.47 us
  transfers between devices with their start and end apart: 3 -> 10, of which waited for: 1 -> 1; matrix products, arithmetic and copies ran while one was open for 34% -> 35% of each run, Pallas kernels for 52% -> 34%
where the time goes in v7:
time: 350 us; the launch traced here: 343 us
  Pallas kernels  116 us (33%)
  matrix products  115 us (33%)
  starting transfers between devices  51.6 us (15%)
  local copies, waits for them, and re-layouts  21.7 us (6%)
  between operations  15.4 us (4%)
  waiting for transfers between devices  14.3 us (4%)
  other arithmetic  9.66 us (3%)
    pallas_call x1, Pallas kernels, exchange(): pl.pallas_call(functools.partial(exchange_kernel, n, scatter), out_shape=...  59 us
    pallas_call x1, Pallas kernels, relay_gather(): pl.pallas_call(relay_gather_kernel, out_shape=jax.ShapeDtypeStruct((sampl...  56.5 us
    ppermute x7, starting transfers between devices, scatter_by_permutes(): lax.ppermute(outgoing, 'section', perm=[(i, (i + k) % n) for i in range(n)])  51.5 us
    dot_general x2, matrix products, shards(): jnp.einsum('tk,dk->td', value_gradient, w_value, preferred_element_type=j...  14.4 us
    ppermute x7, waiting for transfers between devices, scatter_by_permutes(): lax.ppermute(outgoing, 'section', perm=[(i, (i + k) % n) for i in range(n)])  14.3 us
    dot_general x2, matrix products, attend_one(): jnp.einsum('hgln,nhd->lhgd', score_grad, heads_of_keys, preferred_element...  14.1 us
    dot_general x2, matrix products, shards(): jnp.dot(tokens, w_key, preferred_element_type=jnp.float32)  13 us
    dot_general x2, matrix products, shards(): jnp.dot(tokens, w_value, preferred_element_type=jnp.float32)  13 us
  transfers between devices with their start and end apart: 10, of which 1 were waited for; matrix products, arithmetic and copies ran while one was open for 35% of the time, Pallas kernels for 34%

profile of v7, /device:TPU:38, one launch (start us, length us, event | category | flops | bytes accessed | tf_op | source)
XLA Modules:
  0.0 342.8 jit_solution(5424996533015317536)
XLA Ops:
  18.9 56.5 %shard_map.102 = bf16[1,8,24,8192]{3,2,1,0:T(8,128)(2,1)} custom-call(bf16[1,24,8192]{2,1,0:T(8,128)(2,1)} %get-tuple-element.20.x_ref), custom_call_target="tpu_custom_call" | custom-call | tf_op jit(solution)/shard_map/pallas_call | solution.py:183
  75.4 6.1 %fusion.70 = bf16[192,512]{1,0:T(8,128)(2,1)S(1)} fusion(bf16[192,8192]{1,0:T(8,128)(2,1)} %bitcast.239, bf16[1,8192,512]{2,1,0:T(8,128)(2,1)} %param.10), kind=kOutput, calls=%fused_computation.74 | convolution fusion | flops 1610711040 | bytes 11730944 | tf_op jit(solution)/shard_map/dot_general | solution.py:256
  81.6 6.2 %fusion.64 = bf16[192,512]{1,0:T(8,128)(2,1)S(1)} fusion(bf16[192,8192]{1,0:T(8,128)(2,1)} %bitcast.240, bf16[1,8192,512]{2,1,0:T(8,128)(2,1)} %param.9), kind=kOutput, calls=%fused_computation.72 | convolution fusion | flops 1610711040 | bytes 11730944 | tf_op jit(solution)/shard_map/dot_general | solution.py:255
  94.8 5.9 %fusion.77 = bf16[4,24,8,128]{3,2,1,0:T(8,128)(2,1)S(1)} fusion(bf16[128,4,8,128]{0,3,2,1:T(8,128)(2,1)S(1)} %bitcast.247, f32[4,192,128,8]{2,1,3,0:T(8,128)} %fusion.98, f32[4,8,128,192]{2,3,1,0:T(8,128)} %get-tuple-element.26, f32[4,8,128]{2,1,0:T(8,128)S(1)} %get-tuple-element.25), kind=kOutput, calls=%fused_computation.77 | convolution fusion | flops 206934208 | bytes 7553024 | tf_op jit(solution)/shard_map/hgln,lhgd->nhd/dot_general | solution.py:52
  103.5 6.2 %fusion.16 = f32[192,8192]{1,0:T(8,128)S(1)} fusion(bf16[1,8192,512]{2,1,0:T(8,128)(2,1)} %param.9, bf16[4,24,8,128]{3,2,1,0:T(8,128)(2,1)S(1)} %fusion.77), kind=kOutput, calls=%fused_computation.20 | convolution fusion | flops 1610612736 | bytes 14876672 | tf_op jit(solution)/shard_map/tk,dk->td/dot_general | solution.py:268
  109.8 6.2 %fusion.4 = bf16[192,8192]{1,0:T(8,128)(2,1)S(1)} fusion(f32[192,8192]{1,0:T(8,128)S(1)} %fusion.16, bf16[1,8192,512]{2,1,0:T(8,128)(2,1)} %param.10, bf16[4,24,8,128]{3,2,1,0:T(8,128)(2,1)S(1)} %fusion.78), kind=kOutput, calls=%fused_computation.8 | convolution fusion | flops 1613758464 | bytes 18022400 | tf_op jit(solution)/shard_map/tk,dk->td/dot_general | solution.py:269
  116.0 6.8 %fusion.67 = bf16[192,512]{1,0:T(8,128)(2,1)} fusion(bf16[192,8192]{1,0:T(8,128)(2,1)} %bitcast.256, bf16[1,8192,512]{2,1,0:T(8,128)(2,1)} %param.9), kind=kOutput, calls=%fused_computation.73 | convolution fusion | flops 1610711040 | bytes 11730944 | tf_op jit(solution)/shard_map/dot_general | solution.py:255
  123.8 4.8 %fusion.149 = (f32[4,8,128]{2,1,0:T(8,128)}, f32[4,8,128,192]{2,3,1,0:T(8,128)}) fusion(pred[192]{0:T(512)(128)(4,1)S(1)} %iota_compare_fusion, bf16[128,4,8,128]{0,3,2,1:T(8,128)(2,1)} %bitcast.244, bf16[192,4,128,1]{2,1,0,3:T(4,128)(2,1)S(1)} %bitcast.252), kind=kOutput, calls=%fused_computation.152 | convolution fusion | flops 204472512 | bytes 4407488 | tf_op jit(solution)/shard_map/sub | solution.py:38
  128.7 3.1 fusion.81
  132.8 6.8 %convolution_convert_fusion = bf16[8192,512]{1,0:T(8,128)(2,1)} fusion(bf16[192,8192]{1,0:T(8,128)(2,1)S(1)} %bitcast.259, bf16[192,8192]{1,0:T(8,128)(2,1)S(1)} %bitcast.242, bf16[192,512]{1,0:T(8,128)(2,1)S(1)} %get-tuple-element.31, bf16[192,512]{1,0:T(8,128)(2,1)S(1)} %get-tuple-element.32), kind=kOutput, calls=%fused_computation.4 | convolution fusion | flops 3238789120 | bytes 15073280 | tf_op jit(solution)/shard_map/td,tk->dk/dot_general | solution.py:275
  139.6 6.8 %fusion.73 = bf16[192,512]{1,0:T(8,128)(2,1)} fusion(bf16[192,8192]{1,0:T(8,128)(2,1)} %bitcast.257, bf16[1,8192,512]{2,1,0:T(8,128)(2,1)} %param.10), kind=kOutput, calls=%fused_computation.75 | convolution fusion | flops 1610711040 | bytes 11730944 | tf_op jit(solution)/shard_map/dot_general | solution.py:256
  147.4 3.6 %fusion.99 = f32[4,192,128,8]{2,1,3,0:T(8,128)} fusion(bf16[128,4,8,128]{3,2,1,0:T(8,128)(2,1)} %bitcast.236, pred[128]{0:T(512)(128)(4,1)S(1)} %iota_compare_fusion.2, bf16[192,4,128,1]{2,1,0,3:T(4,128)(2,1)S(1)} %bitcast.251), kind=kOutput, calls=%fused_computation.108 | convolution fusion | flops 201850880 | bytes 4391040 | tf_op jit(solution)/shard_map/lhgd,nhd->hgln/dot_general | solution.py:44
  151.0 6.0 %fusion.76 = bf16[4,24,8,128]{3,2,1,0:T(8,128)(2,1)S(1)} fusion(bf16[128,4,8,128]{0,3,2,1:T(8,128)(2,1)} %bitcast.245, f32[4,192,128,8]{2,1,3,0:T(8,128)} %fusion.99, f32[4,8,128,192]{2,3,1,0:T(8,128)} %get-tuple-element.28, f32[4,8,128]{2,1,0:T(8,128)} %get-tuple-element.27), kind=kOutput, calls=%fused_computation.76 | convolution fusion | flops 206934208 | bytes 7553024 | tf_op jit(solution)/shard_map/hgln,lhgd->nhd/dot_general | solution.py:52
  158.0 9.7 %convolution_convert_fusion.1 = bf16[8192,512]{1,0:T(8,128)(2,1)} fusion(bf16[192,8192]{1,0:T(8,128)(2,1)} %bitcast.258, bf16[192,8192]{1,0:T(8,128)(2,1)} %bitcast.241, bf16[192,512]{1,0:T(8,128)(2,1)S(1)} %get-tuple-element.29, bf16[192,512]{1,0:T(8,128)(2,1)S(1)} %get-tuple-element.30), kind=kOutput, calls=%fused_computation.5 | convolution fusion | flops 3238789120 | bytes 15073280 | tf_op jit(solution)/shard_map/td,tk->dk/dot_general | solution.py:280
  168.4 7.1 %convolution_convert_fusion.3 = bf16[4,128,8,128]{3,1,2,0:T(8,128)(2,1)} fusion(f32[4,192,128,8]{2,1,3,0:T(8,128)} %fusion.98, bf16[192,4,128,1]{2,1,0,3:T(4,128)(2,1)} %bitcast.255, f32[4,8,128,192]{2,3,1,0:T(8,128)} %get-tuple-element.26, f32[4,8,128]{2,1,0:T(8,128)S(1)} %copy-done.11), kind=kOutput, calls=%fused_computation.59 | convolution fusion | flops 207360192 | bytes 7553024 | tf_op jit(solution)/shard_map/hgln,nhd->lhgd/dot_general | solution.py:49
  179.4 6.1 %collective-permute-start.6 = (bf16[24,8192]{1,0:T(8,128)(2,1)}, bf16[24,8192]{1,0:T(8,128)(2,1)}, u32[]{:S(2)}, u32[]{:S(2)}) collective-permute-start(bf16[24,8192]{1,0:T(8,128)(2,1)} %get-tuple-element.9), channel_id=1, source_target_pairs={{0,112},{16,0},{32,16},{48,32},{64,48},{80,64},{96,80},{112,96},{1... | collective-permute-start | bytes 1179656 | tf_op jit(solution)/shard_map/ppermute | solution.py:226
  185.4 8.3 %collective-permute-start.5 = (bf16[24,8192]{1,0:T(8,128)(2,1)}, bf16[24,8192]{1,0:T(8,128)(2,1)}, u32[]{:S(2)}, u32[]{:S(2)}) collective-permute-start(bf16[24,8192]{1,0:T(8,128)(2,1)} %get-tuple-element.10), channel_id=1, source_target_pairs={{0,96},{16,112},{32,0},{48,16},{64,32},{80,48},{96,64},{112,80},{1... | collective-permute-start | bytes 1179656 | tf_op jit(solution)/shard_map/ppermute | solution.py:226
  196.1 6.3 %fusion.12 = f32[192,8192]{1,0:T(8,128)S(1)} fusion(bf16[1,8192,512]{2,1,0:T(8,128)(2,1)} %param.9, bf16[4,24,8,128]{3,2,1,0:T(8,128)(2,1)S(1)} %fusion.76), kind=kOutput, calls=%fused_computation.16 | convolution fusion | flops 1610612736 | bytes 14876672 | tf_op jit(solution)/shard_map/tk,dk->td/dot_general | solution.py:268
  202.4 8.1 %fusion.5 = bf16[192,8192]{1,0:T(8,128)(2,1)} fusion(f32[192,8192]{1,0:T(8,128)S(1)} %fusion.12, bf16[1,8192,512]{2,1,0:T(8,128)(2,1)} %param.10, bf16[4,24,8,128]{3,2,1,0:T(8,128)(2,1)S(1)} %fusion.81), kind=kOutput, calls=%fused_computation.9 | convolution fusion | flops 1613758464 | bytes 18022400 | tf_op jit(solution)/shard_map/tk,dk->td/dot_general | solution.py:269
  210.5 7.0 %convolution_convert_fusion.2 = bf16[4,128,8,128]{3,1,2,0:T(8,128)(2,1)} fusion(f32[4,192,128,8]{2,1,3,0:T(8,128)} %fusion.99, bf16[192,4,128,1]{2,1,0,3:T(4,128)(2,1)S(1)} %bitcast.253, f32[4,8,128,192]{2,3,1,0:T(8,128)} %get-tuple-element.28, f32[4,8,128]{2,1,0:T(8,128)S(1)} %copy-done.9), kind=kOutput, calls=%fused_computation.58 | convolution fusion | flops 207360192 | bytes 7553024 | tf_op jit(solution)/shard_map/hgln,nhd->lhgd/dot_general | solution.py:49
  219.9 59.0 %shard_map.103 = bf16[1,8,24,8192]{3,2,1,0:T(8,128)(2,1)} custom-call(bf16[1,8,24,8192]{3,2,1,0:T(8,128)(2,1)} %bitcast.232), custom_call_target="tpu_custom_call" | custom-call | tf_op jit(solution)/shard_map/pallas_call | solution.py:207
  281.4 34.8 %collective-permute-start.2 = (bf16[24,8192]{1,0:T(8,128)(2,1)}, bf16[24,8192]{1,0:T(8,128)(2,1)S(1)}, u32[]{:S(2)}, u32[]{:S(2)}) collective-permute-start(bf16[24,8192]{1,0:T(8,128)(2,1)} %get-tuple-element.13), channel_id=1, source_target_pairs={{0,48},{16,64},{32,80},{48,96},{64,112},{80,0},{96,16},{112,32},{1... | collective-permute-start | bytes 1179656 | tf_op jit(solution)/shard_map/ppermute | solution.py:226
  316.2 3.1 maximum_bitcast_fusion
  319.2 14.2 %collective-permute-done.2 = bf16[24,8192]{1,0:T(8,128)(2,1)S(1)} collective-permute-done((bf16[24,8192]{1,0:T(8,128)(2,1)}, bf16[24,8192]{1,0:T(8,128)(2,1)S(1)}, u32[]{:S(2)}, u32[]{:S(2)}) %collective-permute-start.2) | collective-permute-done | bytes 393248 | tf_op jit(solution)/shard_map/ppermute | solution.py:226
  (71 shorter events, 38.7 us)
Async XLA Ops:
  7.2 3.9 %copy-start.6 = (s32[2]{0:T(128)S(1)}, s32[2]{0:T(128)}, u32[]{:S(2)}) copy-start(s32[2]{0:T(128)} %param.12) | copy-start | bytes 28
  7.2 108.9 %all-gather.3.cloned.1.call-start = ((), (), s32[]{:S(2)}) async-start(), calls=%async_computation.4 | async-start | bytes 3538944 | tf_op jit(solution)/shard_map/all_gather | solution.py:241
  9.3 327.0 %reduce-scatter.5.cloned.1.call-start = ((), (), s32[]{:S(2)}) async-start(), calls=%async_computation.3 | async-start | bytes 8912896 | tf_op jit(solution)/shard_map/reduce_scatter | solution.py:279
  81.6 6.3 %copy-start.7 = (s32[2]{0:T(128)S(1)}, s32[2]{0:T(128)}, u32[]{:S(2)}) copy-start(s32[2]{0:T(128)} %param.13) | copy-start | bytes 28
  87.7 4.4 %copy-start.1 = (bf16[1,1,128,4096]{2,3,1,0:T(8,128)(2,1)S(1)}, bf16[1,1,128,4096]{2,3,1,0:T(8,128)(2,1)}, u32[]{:S(2)}) copy-start(bf16[1,1,128,4096]{2,3,1,0:T(8,128)(2,1)} %copy.67) | copy-start | bytes 3145732
  87.8 7.0 %copy-start.5 = (bf16[192,4,128]{2,1,0:T(4,128)(2,1)}, bf16[192,4,128]{2,1,0:T(4,128)(2,1)S(1)}, u32[]{:S(2)}) copy-start(bf16[192,4,128]{2,1,0:T(4,128)(2,1)S(1)} %reshape.82) | copy-start | bytes 589828
  94.8 5.9 %copy-start.10 = (f32[4,8,128]{2,1,0:T(8,128)}, f32[4,8,128]{2,1,0:T(8,128)S(1)}, u32[]{:S(2)}) copy-start(f32[4,8,128]{2,1,0:T(8,128)S(1)} %get-tuple-element.25) | copy-start | bytes 49156
  100.7 2.8 copy-start.2
  123.8 4.9 %copy-start.3 = (bf16[192,4,128]{2,1,0:T(4,128)(2,1)}, bf16[192,4,128]{2,1,0:T(4,128)(2,1)S(1)}, u32[]{:S(2)}) copy-start(bf16[192,4,128]{2,1,0:T(4,128)(2,1)S(1)} %reshape.87) | copy-start | bytes 589828
  128.7 3.2 copy-start
  128.7 4.1 %copy-start.8 = (bf16[1,192,8192]{2,1,0:T(8,128)(2,1)S(1)}, bf16[1,192,8192]{2,1,0:T(8,128)(2,1)}, u32[]{:S(2)}) copy-start(bf16[1,192,8192]{2,1,0:T(8,128)(2,1)} %all-gather.3.cloned.1.call-done) | copy-start | bytes 9437188
  139.6 196.7 %reduce-scatter.3.cloned.1.call-start = ((), (), s32[]{:S(2)}) async-start(), calls=%async_computation.2 | async-start | bytes 8912896 | tf_op jit(solution)/shard_map/reduce_scatter | solution.py:284
  167.7 0.7 copy-start.11
  179.4 102.0 %collective-permute-start = (bf16[24,8192]{1,0:T(8,128)(2,1)}, bf16[24,8192]{1,0:T(8,128)(2,1)}, u32[]{:S(2)}, u32[]{:S(2)}) collective-permute-start(bf16[24,8192]{1,0:T(8,128)(2,1)} %get-tuple-element.8), channel_id=1, source_target_pairs={{0,16},{16,32},{32,48},{48,64},{64,80},{80,96},{96,112},{112,0},{1... | collective-permute-start | bytes 1179656 | tf_op jit(solution)/shard_map/ppermute | solution.py:226
  179.4 136.8 %collective-permute-start.6 = (bf16[24,8192]{1,0:T(8,128)(2,1)}, bf16[24,8192]{1,0:T(8,128)(2,1)}, u32[]{:S(2)}, u32[]{:S(2)}) collective-permute-start(bf16[24,8192]{1,0:T(8,128)(2,1)} %get-tuple-element.9), channel_id=1, source_target_pairs={{0,112},{16,0},{32,16},{48,32},{64,48},{80,64},{96,80},{112,96},{1... | collective-permute-start | bytes 1179656 | tf_op jit(solution)/shard_map/ppermute | solution.py:226
  185.4 133.8 %collective-permute-start.5 = (bf16[24,8192]{1,0:T(8,128)(2,1)}, bf16[24,8192]{1,0:T(8,128)(2,1)}, u32[]{:S(2)}, u32[]{:S(2)}) collective-permute-start(bf16[24,8192]{1,0:T(8,128)(2,1)} %get-tuple-element.10), channel_id=1, source_target_pairs={{0,96},{16,112},{32,0},{48,16},{64,32},{80,48},{96,64},{112,80},{1... | collective-permute-start | bytes 1179656 | tf_op jit(solution)/shard_map/ppermute | solution.py:226
  193.7 125.5 %collective-permute-start.4 = (bf16[24,8192]{1,0:T(8,128)(2,1)}, bf16[24,8192]{1,0:T(8,128)(2,1)}, u32[]{:S(2)}, u32[]{:S(2)}) collective-permute-start(bf16[24,8192]{1,0:T(8,128)(2,1)} %get-tuple-element.11), channel_id=1, source_target_pairs={{0,80},{16,96},{32,112},{48,0},{64,16},{80,32},{96,48},{112,64},{1... | collective-permute-start | bytes 1179656 | tf_op jit(solution)/shard_map/ppermute | solution.py:226
  193.7 125.5 %collective-permute-start.3 = (bf16[24,8192]{1,0:T(8,128)(2,1)}, bf16[24,8192]{1,0:T(8,128)(2,1)}, u32[]{:S(2)}, u32[]{:S(2)}) collective-permute-start(bf16[24,8192]{1,0:T(8,128)(2,1)} %get-tuple-element.12), channel_id=1, source_target_pairs={{0,64},{16,80},{32,96},{48,112},{64,0},{80,16},{96,32},{112,48},{1... | collective-permute-start | bytes 1179656 | tf_op jit(solution)/shard_map/ppermute | solution.py:226
  202.4 8.2 %copy-start.4 = (bf16[192,4,128]{2,1,0:T(4,128)(2,1)S(1)}, bf16[192,4,128]{2,1,0:T(4,128)(2,1)}, u32[]{:S(2)}) copy-start(bf16[192,4,128]{2,1,0:T(4,128)(2,1)} %copy-done.3) | copy-start | bytes 589828
  202.4 8.1 %copy-start.9 = (f32[4,8,128]{2,1,0:T(8,128)S(1)}, f32[4,8,128]{2,1,0:T(8,128)}, u32[]{:S(2)}) copy-start(f32[4,8,128]{2,1,0:T(8,128)} %get-tuple-element.27) | copy-start | bytes 49156
  281.4 52.1 %collective-permute-start.2 = (bf16[24,8192]{1,0:T(8,128)(2,1)}, bf16[24,8192]{1,0:T(8,128)(2,1)S(1)}, u32[]{:S(2)}, u32[]{:S(2)}) collective-permute-start(bf16[24,8192]{1,0:T(8,128)(2,1)} %get-tuple-element.13), channel_id=1, source_target_pairs={{0,48},{16,64},{32,80},{48,96},{64,112},{80,0},{96,16},{112,32},{1... | collective-permute-start | bytes 1179656 | tf_op jit(solution)/shard_map/ppermute | solution.py:226
  316.2 17.3 %collective-permute-start.1 = (bf16[24,8192]{1,0:T(8,128)(2,1)}, bf16[24,8192]{1,0:T(8,128)(2,1)S(1)}, u32[]{:S(2)}, u32[]{:S(2)}) collective-permute-start(bf16[24,8192]{1,0:T(8,128)(2,1)} %get-tuple-element.14), channel_id=1, source_target_pairs={{0,32},{16,48},{32,64},{48,80},{64,96},{80,112},{96,0},{112,16},{1... | collective-permute-start | bytes 1179656 | tf_op jit(solution)/shard_map/ppermute | solution.py:226
Sparse Core Ops, SparseCore 0:
  10.9 88.0 all-gather.2
  139.7 84.0 reduce-scatter.4
  226.8 92.0 reduce-scatter.2

commit v8 on v6

--- a/solution.py
+++ b/solution.py
@@ -218,6 +218,95 @@
     )(x)
 
 
+def image_kernel(n, tiles, g_ref, wk_ref, wv_ref, o_ref, buf, send_sems, recv_sems, local_sem):
+    me = lax.axis_index("section")
+    row = lax.axis_index("dp")
+    rows = g_ref.shape[0] // n
+    half = g_ref.shape[1] // 2
+    tile_w = wk_ref.shape[0] // tiles
+    barrier = pltpu.get_barrier_semaphore()
+    for k in range(1, n):
+        pl.semaphore_signal(
+            barrier, inc=1, device_id=(lax.rem(me + k, n), row), device_id_type=MESH_ID
+        )
+    pl.semaphore_wait(barrier, n - 1)
+
+    def compute(t):
+        cols = pl.ds(pl.multiple_of(t * tile_w, tile_w), tile_w)
+        dims = (((1,), (1,)), ((), ()))
+        acc = lax.dot_general(
+            g_ref[:, pl.ds(0, half)], wk_ref[cols, :], dims, preferred_element_type=jnp.float32
+        )
+        acc = acc + lax.dot_general(
+            g_ref[:, pl.ds(half, half)], wv_ref[cols, :], dims, preferred_element_type=jnp.float32
+        )
+        buf[:, cols] = acc.astype(buf.dtype)
+
+    def send(t):
+        cols = pl.ds(pl.multiple_of(t * tile_w, tile_w), tile_w)
+        for k in range(1, n):
+            peer = lax.rem(me + k, n)
+            pltpu.make_async_remote_copy(
+                src_ref=buf.at[pl.ds(pl.multiple_of(peer * rows, 16), rows), cols],
+                dst_ref=o_ref.at[me, :, cols],
+                send_sem=send_sems.at[k],
+                recv_sem=recv_sems.at[k],
+                device_id=(peer, row),
+                device_id_type=MESH_ID,
+            ).start()
+
+    compute(0)
+
+    def body(t, carry):
+        compute(t)
+        send(t - 1)
+        return carry
+
+    lax.fori_loop(1, tiles, body, 0)
+    send(tiles - 1)
+    own = pl.ds(pl.multiple_of(me * rows, 16), rows)
+    local = pltpu.make_async_copy(buf.at[own, :], o_ref.at[me], local_sem)
+    local.start()
+    for k in range(1, n):
+        peer = lax.rem(me + k, n)
+        whole = pltpu.make_async_remote_copy(
+            src_ref=buf.at[pl.ds(pl.multiple_of(peer * rows, 16), rows), :],
+            dst_ref=o_ref.at[me],
+            send_sem=send_sems.at[k],
+            recv_sem=recv_sems.at[k],
+            device_id=(peer, row),
+            device_id_type=MESH_ID,
+        )
+        whole.wait_send()
+        whole.wait_recv()
+    local.wait()
+
+
+def image_exchange(g, w_key, w_value, n):
+    total_rows, kv = g.shape
+    width = w_key.shape[0]
+    tiles = 8
+    return pl.pallas_call(
+        functools.partial(image_kernel, n, tiles),
+        out_shape=jax.ShapeDtypeStruct((n, total_rows // n, width), jnp.bfloat16),
+        in_specs=[pl.BlockSpec(memory_space=pltpu.VMEM)] * 3,
+        out_specs=pl.BlockSpec(memory_space=pl.ANY),
+        scratch_shapes=[
+            pltpu.VMEM((total_rows, width), jnp.bfloat16),
+            pltpu.SemaphoreType.DMA((n,)),
+            pltpu.SemaphoreType.DMA((n,)),
+            pltpu.SemaphoreType.DMA(()),
+        ],
+        compiler_params=pltpu.CompilerParams(
+            collective_id=3, has_side_effects=True, vmem_limit_bytes=60 * 1024 * 1024
+        ),
+        cost_estimate=pl.CostEstimate(
+            flops=2 * total_rows * kv * width, bytes_accessed=2 * (kv + total_rows) * width,
+            transcendentals=0,
+        ),
+    )(g, w_key, w_value)
+
+
 def shards(queries, image_tokens, key_weight, value_weight, cotangent, tile_counts, text_lengths):
     n_section = lax.axis_size("section")
     samples_here, chunk, model_width = image_tokens.shape
@@ -255,9 +344,6 @@
         query_list.append(query_gradient)
         key_list.append(key_gradient)
         value_list.append(value_gradient)
-        term = jnp.einsum("tk,dk->td", key_gradient, w_key, preferred_element_type=jnp.float32)
-        term = term + jnp.einsum("tk,dk->td", value_gradient, w_value, preferred_element_type=jnp.float32)
-        image_list.append(term.astype(jnp.bfloat16).reshape(n_section, chunk, model_width))
     all_tokens = jnp.concatenate(token_list, axis=0)
     value_term = jnp.einsum(
         "td,tk->dk", all_tokens, jnp.concatenate(value_list, axis=0),
@@ -270,8 +356,16 @@
     ).astype(jnp.bfloat16)
     key_sum = lax.psum_scatter(key_term, "dp", scatter_dimension=0, tiled=True)
     query_out = jnp.stack(query_list)[None]
-    received = exchange(jnp.stack(image_list), n_section, True, 1)
-    image_out = jnp.sum(received.astype(jnp.float32), axis=1).astype(jnp.bfloat16)
+    kv_grads = jnp.concatenate([jnp.stack(key_list), jnp.stack(value_list)], axis=-1)
+    by_slot = kv_grads.reshape(samples_here, n_section, chunk, -1).transpose(1, 0, 2, 3)
+    received = image_exchange(
+        by_slot.reshape(n_section * samples_here * chunk, -1), w_key, w_value, n_section
+    )
+    image_out = (
+        jnp.sum(received.astype(jnp.float32), axis=0)
+        .reshape(samples_here, chunk, model_width)
+        .astype(jnp.bfloat16)
+    )
     return (
         query_out,
         image_out,

time: 347 us -> 319 us (0.919)
  matrix products: 111 us -> 84.1 us
    dot_general x4 -> x0, matrix products: 25.2 us -> none  [the longest x2 12.6 us: shards(): jnp.einsum('tk,dk->td', key_gradient, w_key, preferred_element_type=jnp.f...]
  transfers between devices with their start and end apart: 3 -> 3, of which waited for: 1 -> 1; matrix products, arithmetic and copies ran while one was open for 34% -> 27% of each run, Pallas kernels for 52% -> 57%
where the time goes in v8:
time: 319 us; the launch traced here: 318 us
  Pallas kernels  182 us (57%)
  matrix products  84.1 us (26%)
  local copies, waits for them, and re-layouts  20.1 us (6%)
  between operations  15.4 us (5%)
  waiting for transfers between devices  9.18 us (3%)
  other arithmetic  7.73 us (2%)
    pallas_call x1, Pallas kernels, image_exchange(): pl.pallas_call(functools.partial(image_kernel, n, tiles), out_shape=jax.S...  126 us
    pallas_call x1, Pallas kernels, relay_gather(): pl.pallas_call(relay_gather_kernel, out_shape=jax.ShapeDtypeStruct((sampl...  55.3 us
    dot_general x2, matrix products, shards(): jnp.dot(tokens, w_value, preferred_element_type=jnp.float32)  13.2 us
    dot_general x2, matrix products, shards(): jnp.dot(tokens, w_key, preferred_element_type=jnp.float32)  13.1 us
    dot_general x2, matrix products, attend_one(): jnp.einsum('hgln,lhgd->nhd', score_grad, heads_of_queries, preferred_elem...  12.5 us
    dot_general x2, matrix products, attend_one(): jnp.einsum('hgln,nhd->lhgd', score_grad, heads_of_keys, preferred_element...  12 us
    dot_general x1, matrix products, shards(): jnp.einsum('td,tk->dk', all_tokens, jnp.concatenate(key_list, axis=0), pr...  9.8 us
    all_gather x1, waiting for transfers between devices, shards(): lax.all_gather(image_tokens[i], 'section', axis=0, tiled=True)  9.12 us
  transfers between devices with their start and end apart: 3, of which 1 were waited for; matrix products, arithmetic and copies ran while one was open for 27% of the time, Pallas kernels for 57%

profile of v8, /device:TPU:38, one launch (start us, length us, event | category | flops | bytes accessed | tf_op | source)
XLA Modules:
  0.0 318.4 jit_solution(5158574161799982180)
XLA Ops:
  7.2 2.0 fusion.103
  9.3 1.3 fusion.104
  11.9 1.7 fusion.102
  17.6 55.3 %shard_map.102 = bf16[1,8,24,8192]{3,2,1,0:T(8,128)(2,1)} custom-call(bf16[1,24,8192]{2,1,0:T(8,128)(2,1)} %get-tuple-element.8.x_ref), custom_call_target="tpu_custom_call" | custom-call | tf_op jit(solution)/shard_map/pallas_call | solution.py:183
  72.9 6.2 %convolution_convert_fusion.7 = bf16[192,512]{1,0:T(8,128)(2,1)S(1)} fusion(bf16[192,8192]{1,0:T(8,128)(2,1)} %bitcast.192, bf16[1,8192,512]{2,1,0:T(8,128)(2,1)} %param.9), kind=kOutput, calls=%fused_computation.57 | convolution fusion | flops 1610711040 | bytes 11730944 | tf_op jit(solution)/shard_map/dot_general | solution.py:334
  81.1 3.4 %fusion.111 = (f32[4,8,128]{2,1,0:T(8,128)}, f32[4,8,128,192]{2,3,1,0:T(8,128)}) fusion(pred[192]{0:T(512)(128)(4,1)S(1)} %iota_compare_fusion.1, bf16[128,4,8,128]{0,3,2,1:T(8,128)(2,1)S(1)} %bitcast.199, bf16[192,4,128,1]{2,1,0,3:T(4,128)(2,1)S(1)} %bitcast.210), kind=kOutput, calls=%fused_computation.120 | convolution fusion | flops 204472512 | bytes 4407488 | tf_op jit(solution)/shard_map/sub | solution.py:38
  84.5 2.7 fusion.45
  87.9 9.1 %all-gather.3.cloned.1.call-done = bf16[1,192,8192]{2,1,0:T(8,128)(2,1)} async-done(((bf16[1,24,8192]{2,1,0:T(8,128)(2,1)}), bf16[1,192,8192]{2,1,0:T(8,128)(2,1)}) %all-gather.3.cloned.1.call-update) | async-done | bytes 3145744 | tf_op jit(solution)/shard_map/all_gather | solution.py:320
  97.0 6.8 %convolution_convert_fusion.5 = bf16[192,512]{1,0:T(8,128)(2,1)} fusion(bf16[1,192,8192]{2,1,0:T(8,128)(2,1)} %all-gather.3.cloned.1.call-done, bf16[1,8192,512]{2,1,0:T(8,128)(2,1)} %param.9), kind=kOutput, calls=%fused_computation.55 | convolution fusion | flops 1610711040 | bytes 11730944 | tf_op jit(solution)/shard_map/dot_general | solution.py:334
  104.9 3.4 %fusion.106 = (f32[4,8,128]{2,1,0:T(8,128)}, f32[4,8,128,192]{2,3,1,0:T(8,128)}) fusion(pred[192]{0:T(512)(128)(4,1)S(1)} %iota_compare_fusion, bf16[128,4,8,128]{0,3,2,1:T(8,128)(2,1)S(1)} %bitcast.198, bf16[192,4,128,1]{2,1,0,3:T(4,128)(2,1)S(1)} %bitcast.212), kind=kOutput, calls=%fused_computation.119 | convolution fusion | flops 204472512 | bytes 4407488 | tf_op jit(solution)/shard_map/sub | solution.py:38
  108.2 2.8 fusion.42
  112.1 6.7 %convolution_convert_fusion = bf16[8192,512]{1,0:T(8,128)(2,1)} fusion(bf16[192,8192]{1,0:T(8,128)(2,1)S(1)} %bitcast.215, bf16[192,8192]{1,0:T(8,128)(2,1)S(1)} %bitcast.194, bf16[192,512]{1,0:T(8,128)(2,1)S(1)} %copy_bitcast_fusion, bf16[192,512]{1,0:T(8,128)(2,1)S(1)} %copy-done.13), kind=kOutput, calls=%fused_computation.4 | convolution fusion | flops 3238789120 | bytes 15073280 | tf_op jit(solution)/shard_map/td,tk->dk/dot_general | solution.py:348
  119.1 6.8 %convolution_convert_fusion.6 = bf16[192,512]{1,0:T(8,128)(2,1)} fusion(bf16[192,8192]{1,0:T(8,128)(2,1)} %bitcast.193, bf16[1,8192,512]{2,1,0:T(8,128)(2,1)} %param.10), kind=kOutput, calls=%fused_computation.56 | convolution fusion | flops 1610711040 | bytes 11730944 | tf_op jit(solution)/shard_map/dot_general | solution.py:335
  127.0 2.3 fusion.54
  129.3 6.2 %fusion.40 = bf16[4,192,128]{2,1,0:T(8,128)(2,1)S(1)} fusion(bf16[128,4,8,128]{0,3,2,1:T(8,128)(2,1)S(1)} %bitcast.200, f32[4,192,128,8]{2,1,3,0:T(8,128)} %fusion.54, f32[4,8,128,192]{2,3,1,0:T(8,128)} %get-tuple-element.17, f32[4,8,128]{2,1,0:T(8,128)} %get-tuple-element.16), kind=kOutput, calls=%fused_computation.50 | convolution fusion | flops 206934208 | bytes 7553024 | tf_op jit(solution)/shard_map/hgln,lhgd->nhd/dot_general | solution.py:52
  136.3 6.4 %convolution_convert_fusion.4 = bf16[192,512]{1,0:T(8,128)(2,1)S(1)} fusion(bf16[1,192,8192]{2,1,0:T(8,128)(2,1)} %all-gather.3.cloned.1.call-done, bf16[1,8192,512]{2,1,0:T(8,128)(2,1)} %param.10), kind=kOutput, calls=%fused_computation.54 | convolution fusion | flops 1610711040 | bytes 11730944 | tf_op jit(solution)/shard_map/dot_general | solution.py:335
  142.7 2.3 fusion.55
  145.0 6.3 %fusion.41 = bf16[4,192,128]{2,1,0:T(8,128)(2,1)S(1)} fusion(bf16[128,4,8,128]{0,3,2,1:T(8,128)(2,1)} %bitcast.197, f32[4,192,128,8]{2,1,3,0:T(8,128)} %fusion.55, f32[4,8,128,192]{2,3,1,0:T(8,128)} %get-tuple-element.15, f32[4,8,128]{2,1,0:T(8,128)} %get-tuple-element.14), kind=kOutput, calls=%fused_computation.51 | convolution fusion | flops 206934208 | bytes 7553024 | tf_op jit(solution)/shard_map/hgln,lhgd->nhd/dot_general | solution.py:52
  151.3 9.8 %convolution_convert_fusion.1 = bf16[8192,512]{1,0:T(8,128)(2,1)} fusion(bf16[192,8192]{1,0:T(8,128)(2,1)} %bitcast.214, bf16[192,8192]{1,0:T(8,128)(2,1)S(1)} %bitcast.195, bf16[192,512]{1,0:T(8,128)(2,1)S(1)} %copy_bitcast_fusion.2, bf16[192,512]{1,0:T(8,128)(2,1)} %copy_bitcast_fusion.3), kind=kOutput, calls=%fused_computation.5 | convolution fusion | flops 3238789120 | bytes 15073280 | tf_op jit(solution)/shard_map/td,tk->dk/dot_general | solution.py:353
  162.1 6.0 %convolution_convert_fusion.3 = bf16[4,128,8,128]{3,1,2,0:T(8,128)(2,1)S(1)} fusion(f32[4,192,128,8]{2,1,3,0:T(8,128)} %fusion.54, bf16[192,4,128,1]{2,1,0,3:T(4,128)(2,1)S(1)} %bitcast.211, f32[4,8,128,192]{2,3,1,0:T(8,128)} %get-tuple-element.17, f32[4,8,128]{2,1,0:T(8,128)S(1)} %copy-done.17), kind=kOutput, calls=%fused_computation.41 | convolution fusion | flops 207360192 | bytes 7553024 | tf_op jit(solution)/shard_map/hgln,nhd->lhgd/dot_general | solution.py:49
  169.4 6.0 %convolution_convert_fusion.2 = bf16[4,128,8,128]{3,1,2,0:T(8,128)(2,1)S(1)} fusion(f32[4,192,128,8]{2,1,3,0:T(8,128)} %fusion.55, bf16[192,4,128,1]{2,1,0,3:T(4,128)(2,1)} %bitcast.213, f32[4,8,128,192]{2,3,1,0:T(8,128)} %get-tuple-element.15, f32[4,8,128]{2,1,0:T(8,128)S(1)} %copy-done.16), kind=kOutput, calls=%fused_computation.40 | convolution fusion | flops 207360192 | bytes 7553024 | tf_op jit(solution)/shard_map/hgln,nhd->lhgd/dot_general | solution.py:49
  179.3 126.3 %shard_map.103 = bf16[8,48,8192]{2,1,0:T(8,128)(2,1)} custom-call(bf16[384,1024]{1,0:T(8,128)(2,1)} %bitcast.191, bf16[8192,512]{1,0:T(8,128)(2,1)} %bitcast.186, bf16[8192,512]{1,0:T(8,128)(2,1)} %bitcast.185), custom_call_target="tpu_custom_call" | custom-call | flops 6442450944 | bytes 23068672 | tf_op jit(solution)/shard_map/pallas_call | solution.py:289
  305.6 4.8 %reduce_sum.52 = bf16[48,8192]{1,0:T(8,128)(2,1)} reduce(bf16[8,48,8192]{2,1,0:T(8,128)(2,1)} %shard_map.103, bf16[]{:T(256)} %constant.12.clone.1), dimensions={0}, to_apply=%region_6.7 | reduce | flops 2752512 | bytes 7077890 | tf_op jit(solution)/shard_map/reduce_sum | solution.py:365
  310.4 1.5 maximum_bitcast_fusion
  (74 shorter events, 16.9 us)
Async XLA Ops:
  7.2 89.9 %all-gather.3.cloned.1.call-start = ((), (), s32[]{:S(2)}) async-start(), calls=%async_computation.4 | async-start | bytes 3538944 | tf_op jit(solution)/shard_map/all_gather | solution.py:320
  9.3 302.6 %reduce-scatter.5.cloned.1.call-start = ((), (), s32[]{:S(2)}) async-start(), calls=%async_computation.3 | async-start | bytes 8912896 | tf_op jit(solution)/shard_map/reduce_scatter | solution.py:352
  14.9 2.0 copy-start.2
  72.8 6.4 %copy-start.14 = (s32[2]{0:T(128)S(1)}, s32[2]{0:T(128)}, u32[]{:S(2)}) copy-start(s32[2]{0:T(128)} %param.13) | copy-start | bytes 28
  72.8 8.3 %copy-start.4 = (bf16[1,1,128,4096]{2,3,1,0:T(8,128)(2,1)S(1)}, bf16[1,1,128,4096]{2,3,1,0:T(8,128)(2,1)}, u32[]{:S(2)}) copy-start(bf16[1,1,128,4096]{2,3,1,0:T(8,128)(2,1)} %copy.72) | copy-start | bytes 3145732
  79.2 8.0 %copy-start.10 = (bf16[192,4,128]{2,1,0:T(4,128)(2,1)}, bf16[192,4,128]{2,1,0:T(4,128)(2,1)S(1)}, u32[]{:S(2)}) copy-start(bf16[192,4,128]{2,1,0:T(4,128)(2,1)S(1)} %reshape.84) | copy-start | bytes 589828
  87.9 16.9 %copy-start.3 = (bf16[1,1,128,4096]{2,3,1,0:T(8,128)(2,1)S(1)}, bf16[1,1,128,4096]{2,3,1,0:T(8,128)(2,1)}, u32[]{:S(2)}) copy-start(bf16[1,1,128,4096]{2,3,1,0:T(8,128)(2,1)} %copy.73) | copy-start | bytes 3145732
  104.8 6.3 %copy-start.12 = (bf16[192,4,128]{2,1,0:T(4,128)(2,1)}, bf16[192,4,128]{2,1,0:T(4,128)(2,1)S(1)}, u32[]{:S(2)}) copy-start(bf16[192,4,128]{2,1,0:T(4,128)(2,1)S(1)} %reshape.86) | copy-start | bytes 589828
  108.2 3.6 %copy-start = (bf16[1,8,24,8192]{3,2,1,0:T(8,128)(2,1)S(1)}, bf16[1,8,24,8192]{3,2,1,0:T(8,128)(2,1)}, u32[]{:S(2)}) copy-start(bf16[1,8,24,8192]{3,2,1,0:T(8,128)(2,1)} %shard_map.102) | copy-start | bytes 9437188
  108.2 3.6 %copy-start.13 = (bf16[192,512]{1,0:T(8,128)(2,1)S(1)}, bf16[192,512]{1,0:T(8,128)(2,1)}, u32[]{:S(2)}) copy-start(bf16[192,512]{1,0:T(8,128)(2,1)} %copy_bitcast_fusion.1) | copy-start | bytes 589828
  108.2 3.9 %copy-start.15 = (bf16[1,192,8192]{2,1,0:T(8,128)(2,1)S(1)}, bf16[1,192,8192]{2,1,0:T(8,128)(2,1)}, u32[]{:S(2)}) copy-start(bf16[1,192,8192]{2,1,0:T(8,128)(2,1)} %all-gather.3.cloned.1.call-done) | copy-start | bytes 9437188
  111.1 0.7 copy-start.6
  118.9 193.0 %reduce-scatter.3.cloned.1.call-start = ((), (), s32[]{:S(2)}) async-start(), calls=%async_computation.2 | async-start | bytes 8912896 | tf_op jit(solution)/shard_map/reduce_scatter | solution.py:357
  125.9 3.4 %copy-start.5 = (bf16[1,1,128,4096]{2,3,1,0:T(8,128)(2,1)S(1)}, bf16[1,1,128,4096]{2,3,1,0:T(8,128)(2,1)}, u32[]{:S(2)}) copy-start(bf16[1,1,128,4096]{2,3,1,0:T(8,128)(2,1)} %copy.72) | copy-start | bytes 3145732
  135.5 7.1 %copy-start.8 = (bf16[4,192,128]{2,1,0:T(8,128)(2,1)}, bf16[4,192,128]{2,1,0:T(8,128)(2,1)S(1)}, u32[]{:S(2)}) copy-start(bf16[4,192,128]{2,1,0:T(8,128)(2,1)S(1)} %fusion.40) | copy-start | bytes 589828
  145.0 6.3 %copy-start.1 = (bf16[1,8,24,8192]{3,2,1,0:T(8,128)(2,1)S(1)}, bf16[1,8,24,8192]{3,2,1,0:T(8,128)(2,1)}, u32[]{:S(2)}) copy-start(bf16[1,8,24,8192]{3,2,1,0:T(8,128)(2,1)} %shard_map.102) | copy-start | bytes 9437188
  151.3 9.9 %copy-start.7 = (bf16[4,192,128]{2,1,0:T(8,128)(2,1)}, bf16[4,192,128]{2,1,0:T(8,128)(2,1)S(1)}, u32[]{:S(2)}) copy-start(bf16[4,192,128]{2,1,0:T(8,128)(2,1)S(1)} %fusion.41) | copy-start | bytes 589828
  161.1 0.9 copy-start.11
  161.1 0.9 copy-start.17
  162.1 7.0 %copy-start.9 = (bf16[4,192,128]{2,1,0:T(8,128)(2,1)S(1)}, bf16[4,192,128]{2,1,0:T(8,128)(2,1)}, u32[]{:S(2)}) copy-start(bf16[4,192,128]{2,1,0:T(8,128)(2,1)} %copy-done.8) | copy-start | bytes 589828
  168.1 1.3 copy-start.16
Sparse Core Ops, SparseCore 0:
  10.9 86.1 all-gather.2
  119.0 75.1 reduce-scatter.4
  197.2 100.2 reduce-scatter.2

commit v9 on v8

--- a/solution.py
+++ b/solution.py
@@ -282,21 +282,144 @@
     local.wait()
 
 
+def image_relay_kernel(tiles, g_ref, wk_ref, wv_ref, o_ref, buf, stage, local_sem,
+                       direct_send, direct_recv, hop_send, hop_recv, fwd_send, fwd_recv):
+    s = lax.axis_index("section")
+    r = lax.axis_index("dp")
+    y = lax.rem(s, 4)
+    z = (s // 4) * 2 + r // 8
+    xc = lax.rem(r, 8)
+    rows = g_ref.shape[0] // 8
+    half = g_ref.shape[1] // 2
+    lanes = wk_ref.shape[0] // 2
+    tile_w = wk_ref.shape[0] // tiles
+
+    def sec(zz, yy):
+        return (lax.rem(zz, 4) // 2) * 4 + yy
+
+    def dpi(zz):
+        return lax.rem(zz, 2) * 8 + xc
+
+    def block(section):
+        return pl.ds(pl.multiple_of(section * rows, 16), rows)
+
+    up, down = z + 1, z + 3
+    near = [(sec(z, lax.rem(y + j, 4)), r) for j in range(1, 4)]
+    peers = list(near)
+    for yy in range(4):
+        peers.append((sec(up, yy), dpi(up)))
+        peers.append((sec(down, yy), dpi(down)))
+    barrier = pltpu.get_barrier_semaphore()
+    for peer in peers:
+        pl.semaphore_signal(barrier, inc=1, device_id=peer, device_id_type=MESH_ID)
+    pl.semaphore_wait(barrier, len(peers))
+
+    def compute(t, carry):
+        cols = pl.ds(pl.multiple_of(t * tile_w, tile_w), tile_w)
+        dims = (((1,), (1,)), ((), ()))
+        acc = lax.dot_general(
+            g_ref[:, pl.ds(0, half)], wk_ref[cols, :], dims, preferred_element_type=jnp.float32
+        )
+        acc = acc + lax.dot_general(
+            g_ref[:, pl.ds(half, half)], wv_ref[cols, :], dims, preferred_element_type=jnp.float32
+        )
+        buf[:, cols] = acc.astype(buf.dtype)
+        return carry
+
+    lax.fori_loop(0, tiles, compute, 0)
+    local = pltpu.make_async_copy(buf.at[block(s), :], o_ref.at[s], local_sem)
+    local.start()
+    sends = []
+    for j in range(1, 4):
+        copy = pltpu.make_async_remote_copy(
+            src_ref=buf.at[block(near[j - 1][0]), :],
+            dst_ref=o_ref.at[s],
+            send_sem=direct_send.at[j],
+            recv_sem=direct_recv.at[j],
+            device_id=near[j - 1],
+            device_id_type=MESH_ID,
+        )
+        copy.start()
+        sends.append(copy)
+    far_plane = z + 2
+    hops = {}
+    for side, (target, part) in enumerate(((up, pl.ds(0, lanes)), (down, pl.ds(lanes, lanes)))):
+        for yy in range(4):
+            copy = pltpu.make_async_remote_copy(
+                src_ref=buf.at[block(sec(far_plane, yy)), part],
+                dst_ref=stage.at[side, yy],
+                send_sem=hop_send.at[side, yy],
+                recv_sem=hop_recv.at[side, yy],
+                device_id=(sec(target, y), dpi(target)),
+                device_id_type=MESH_ID,
+            )
+            copy.start()
+            hops[side, yy] = copy
+    routes = ((down, up, pl.ds(0, lanes)), (up, down, pl.ds(lanes, lanes)))
+    forwards = []
+    for side, (origin, target, part) in enumerate(routes):
+        for yy in range(4):
+            hops[side, yy].wait_recv()
+            copy = pltpu.make_async_remote_copy(
+                src_ref=stage.at[side, yy],
+                dst_ref=o_ref.at[sec(origin, y), :, part],
+                send_sem=fwd_send.at[side, yy],
+                recv_sem=fwd_recv.at[side, y],
+                device_id=(sec(target, yy), dpi(target)),
+                device_id_type=MESH_ID,
+            )
+            copy.start()
+            forwards.append(copy)
+    for copy in sends:
+        copy.wait()
+    for copy in hops.values():
+        copy.wait_send()
+    for copy in forwards:
+        copy.wait_send()
+    for side, (origin, target, part) in enumerate(routes):
+        for yy in range(4):
+            pltpu.make_async_remote_copy(
+                src_ref=stage.at[side, yy],
+                dst_ref=o_ref.at[sec(origin, y), :, part],
+                send_sem=fwd_send.at[side, yy],
+                recv_sem=fwd_recv.at[side, yy],
+                device_id=(sec(target, yy), dpi(target)),
+                device_id_type=MESH_ID,
+            ).wait_recv()
+    local.wait()
+
+
 def image_exchange(g, w_key, w_value, n):
     total_rows, kv = g.shape
     width = w_key.shape[0]
     tiles = 8
-    return pl.pallas_call(
-        functools.partial(image_kernel, n, tiles),
-        out_shape=jax.ShapeDtypeStruct((n, total_rows // n, width), jnp.bfloat16),
-        in_specs=[pl.BlockSpec(memory_space=pltpu.VMEM)] * 3,
-        out_specs=pl.BlockSpec(memory_space=pl.ANY),
-        scratch_shapes=[
+    if n == 8 and lax.axis_size("dp") == 16:
+        body = functools.partial(image_relay_kernel, tiles)
+        scratch = [
+            pltpu.VMEM((total_rows, width), jnp.bfloat16),
+            pltpu.VMEM((2, 4, total_rows // n, width // 2), jnp.bfloat16),
+            pltpu.SemaphoreType.DMA(()),
+            pltpu.SemaphoreType.DMA((4,)),
+            pltpu.SemaphoreType.DMA((4,)),
+            pltpu.SemaphoreType.DMA((2, 4)),
+            pltpu.SemaphoreType.DMA((2, 4)),
+            pltpu.SemaphoreType.DMA((2, 4)),
+            pltpu.SemaphoreType.DMA((2, 4)),
+        ]
+    else:
+        body = functools.partial(image_kernel, n, tiles)
+        scratch = [
             pltpu.VMEM((total_rows, width), jnp.bfloat16),
             pltpu.SemaphoreType.DMA((n,)),
             pltpu.SemaphoreType.DMA((n,)),
             pltpu.SemaphoreType.DMA(()),
-        ],
+        ]
+    return pl.pallas_call(
+        body,
+        out_shape=jax.ShapeDtypeStruct((n, total_rows // n, width), jnp.bfloat16),
+        in_specs=[pl.BlockSpec(memory_space=pltpu.VMEM)] * 3,
+        out_specs=pl.BlockSpec(memory_space=pl.ANY),
+        scratch_shapes=scratch,
         compiler_params=pltpu.CompilerParams(
             collective_id=3, has_side_effects=True, vmem_limit_bytes=60 * 1024 * 1024
         ),

time: 319 us -> 361 us (1.13)
  Pallas kernels: 182 us -> 220 us
    pallas_call x1, Pallas kernels: 126 us -> 165 us  [image_exchange(): pl.pallas_call(body, out_shape=jax.ShapeDtypeStruct((n, total_rows // n,...]
  transfers between devices with their start and end apart: 3 -> 3, of which waited for: 1 -> 1; matrix products, arithmetic and copies ran while one was open for 27% -> 24% of each run, Pallas kernels for 57% -> 62%
where the time goes in v9:
time: 361 us; the launch traced here: 357 us
  Pallas kernels  220 us (61%)
  matrix products  84.1 us (23%)
  local copies, waits for them, and re-layouts  20.1 us (6%)
  between operations  15.4 us (4%)
  waiting for transfers between devices  9.18 us (3%)
  other arithmetic  7.73 us (2%)
    pallas_call x1, Pallas kernels, image_exchange(): pl.pallas_call(body, out_shape=jax.ShapeDtypeStruct((n, total_rows // n,...  165 us
    pallas_call x1, Pallas kernels, relay_gather(): pl.pallas_call(relay_gather_kernel, out_shape=jax.ShapeDtypeStruct((sampl...  55.3 us
    dot_general x2, matrix products, shards(): jnp.dot(tokens, w_value, preferred_element_type=jnp.float32)  13.2 us
    dot_general x2, matrix products, shards(): jnp.dot(tokens, w_key, preferred_element_type=jnp.float32)  13.1 us
    dot_general x2, matrix products, attend_one(): jnp.einsum('hgln,lhgd->nhd', score_grad, heads_of_queries, preferred_elem...  12.5 us
    dot_general x2, matrix products, attend_one(): jnp.einsum('hgln,nhd->lhgd', score_grad, heads_of_keys, preferred_element...  12 us
    dot_general x1, matrix products, shards(): jnp.einsum('td,tk->dk', all_tokens, jnp.concatenate(key_list, axis=0), pr...  9.8 us
    all_gather x1, waiting for transfers between devices, shards(): lax.all_gather(image_tokens[i], 'section', axis=0, tiled=True)  9.12 us
  transfers between devices with their start and end apart: 3, of which 1 were waited for; matrix products, arithmetic and copies ran while one was open for 24% of the time, Pallas kernels for 62%

profile of v9, /device:TPU:38, one launch (start us, length us, event | category | flops | bytes accessed | tf_op | source)
XLA Modules:
  0.0 357.4 jit_solution(11257426271758147685)
XLA Ops:
  7.2 2.0 fusion.103
  9.3 1.3 fusion.104
  11.9 1.7 fusion.102
  17.6 55.3 %shard_map.102 = bf16[1,8,24,8192]{3,2,1,0:T(8,128)(2,1)} custom-call(bf16[1,24,8192]{2,1,0:T(8,128)(2,1)} %get-tuple-element.8.x_ref), custom_call_target="tpu_custom_call" | custom-call | tf_op jit(solution)/shard_map/pallas_call | solution.py:183
  72.9 6.2 %convolution_convert_fusion.7 = bf16[192,512]{1,0:T(8,128)(2,1)S(1)} fusion(bf16[192,8192]{1,0:T(8,128)(2,1)} %bitcast.192, bf16[1,8192,512]{2,1,0:T(8,128)(2,1)} %param.9), kind=kOutput, calls=%fused_computation.57 | convolution fusion | flops 1610711040 | bytes 11730944 | tf_op jit(solution)/shard_map/dot_general | solution.py:457
  81.1 3.4 fusion.111
  84.5 2.7 fusion.45
  87.9 9.1 %all-gather.3.cloned.1.call-done = bf16[1,192,8192]{2,1,0:T(8,128)(2,1)} async-done(((bf16[1,24,8192]{2,1,0:T(8,128)(2,1)}), bf16[1,192,8192]{2,1,0:T(8,128)(2,1)}) %all-gather.3.cloned.1.call-update) | async-done | bytes 3145744 | tf_op jit(solution)/shard_map/all_gather | solution.py:443
  97.0 6.8 %convolution_convert_fusion.5 = bf16[192,512]{1,0:T(8,128)(2,1)} fusion(bf16[1,192,8192]{2,1,0:T(8,128)(2,1)} %all-gather.3.cloned.1.call-done, bf16[1,8192,512]{2,1,0:T(8,128)(2,1)} %param.9), kind=kOutput, calls=%fused_computation.55 | convolution fusion | flops 1610711040 | bytes 11730944 | tf_op jit(solution)/shard_map/dot_general | solution.py:457
  104.9 3.4 fusion.106
  108.2 2.8 fusion.42
  112.1 6.7 %convolution_convert_fusion = bf16[8192,512]{1,0:T(8,128)(2,1)} fusion(bf16[192,8192]{1,0:T(8,128)(2,1)S(1)} %bitcast.215, bf16[192,8192]{1,0:T(8,128)(2,1)S(1)} %bitcast.194, bf16[192,512]{1,0:T(8,128)(2,1)S(1)} %copy_bitcast_fusion, bf16[192,512]{1,0:T(8,128)(2,1)S(1)} %copy-done.13), kind=kOutput, calls=%fused_computation.4 | convolution fusion | flops 3238789120 | bytes 15073280 | tf_op jit(solution)/shard_map/td,tk->dk/dot_general | solution.py:471
  119.1 6.8 %convolution_convert_fusion.6 = bf16[192,512]{1,0:T(8,128)(2,1)} fusion(bf16[192,8192]{1,0:T(8,128)(2,1)} %bitcast.193, bf16[1,8192,512]{2,1,0:T(8,128)(2,1)} %param.10), kind=kOutput, calls=%fused_computation.56 | convolution fusion | flops 1610711040 | bytes 11730944 | tf_op jit(solution)/shard_map/dot_general | solution.py:458
  127.0 2.3 fusion.54
  129.3 6.2 %fusion.40 = bf16[4,192,128]{2,1,0:T(8,128)(2,1)S(1)} fusion(bf16[128,4,8,128]{0,3,2,1:T(8,128)(2,1)S(1)} %bitcast.200, f32[4,192,128,8]{2,1,3,0:T(8,128)} %fusion.54, f32[4,8,128,192]{2,3,1,0:T(8,128)} %get-tuple-element.17, f32[4,8,128]{2,1,0:T(8,128)} %get-tuple-element.16), kind=kOutput, calls=%fused_computation.50 | convolution fusion | flops 206934208 | bytes 7553024 | tf_op jit(solution)/shard_map/hgln,lhgd->nhd/dot_general | solution.py:52
  136.3 6.4 %convolution_convert_fusion.4 = bf16[192,512]{1,0:T(8,128)(2,1)S(1)} fusion(bf16[1,192,8192]{2,1,0:T(8,128)(2,1)} %all-gather.3.cloned.1.call-done, bf16[1,8192,512]{2,1,0:T(8,128)(2,1)} %param.10), kind=kOutput, calls=%fused_computation.54 | convolution fusion | flops 1610711040 | bytes 11730944 | tf_op jit(solution)/shard_map/dot_general | solution.py:458
  142.7 2.3 fusion.55
  145.0 6.3 %fusion.41 = bf16[4,192,128]{2,1,0:T(8,128)(2,1)S(1)} fusion(bf16[128,4,8,128]{0,3,2,1:T(8,128)(2,1)} %bitcast.197, f32[4,192,128,8]{2,1,3,0:T(8,128)} %fusion.55, f32[4,8,128,192]{2,3,1,0:T(8,128)} %get-tuple-element.15, f32[4,8,128]{2,1,0:T(8,128)} %get-tuple-element.14), kind=kOutput, calls=%fused_computation.51 | convolution fusion | flops 206934208 | bytes 7553024 | tf_op jit(solution)/shard_map/hgln,lhgd->nhd/dot_general | solution.py:52
  151.3 9.8 %convolution_convert_fusion.1 = bf16[8192,512]{1,0:T(8,128)(2,1)} fusion(bf16[192,8192]{1,0:T(8,128)(2,1)} %bitcast.214, bf16[192,8192]{1,0:T(8,128)(2,1)S(1)} %bitcast.195, bf16[192,512]{1,0:T(8,128)(2,1)S(1)} %copy_bitcast_fusion.2, bf16[192,512]{1,0:T(8,128)(2,1)} %copy_bitcast_fusion.3), kind=kOutput, calls=%fused_computation.5 | convolution fusion | flops 3238789120 | bytes 15073280 | tf_op jit(solution)/shard_map/td,tk->dk/dot_general | solution.py:476
  162.1 6.0 %convolution_convert_fusion.3 = bf16[4,128,8,128]{3,1,2,0:T(8,128)(2,1)S(1)} fusion(f32[4,192,128,8]{2,1,3,0:T(8,128)} %fusion.54, bf16[192,4,128,1]{2,1,0,3:T(4,128)(2,1)S(1)} %bitcast.211, f32[4,8,128,192]{2,3,1,0:T(8,128)} %get-tuple-element.17, f32[4,8,128]{2,1,0:T(8,128)S(1)} %copy-done.17), kind=kOutput, calls=%fused_computation.41 | convolution fusion | flops 207360192 | bytes 7553024 | tf_op jit(solution)/shard_map/hgln,nhd->lhgd/dot_general | solution.py:49
  169.4 6.0 %convolution_convert_fusion.2 = bf16[4,128,8,128]{3,1,2,0:T(8,128)(2,1)S(1)} fusion(f32[4,192,128,8]{2,1,3,0:T(8,128)} %fusion.55, bf16[192,4,128,1]{2,1,0,3:T(4,128)(2,1)} %bitcast.213, f32[4,8,128,192]{2,3,1,0:T(8,128)} %get-tuple-element.15, f32[4,8,128]{2,1,0:T(8,128)S(1)} %copy-done.16), kind=kOutput, calls=%fused_computation.40 | convolution fusion | flops 207360192 | bytes 7553024 | tf_op jit(solution)/shard_map/hgln,nhd->lhgd/dot_general | solution.py:49
  179.3 165.2 %shard_map.103 = bf16[8,48,8192]{2,1,0:T(8,128)(2,1)} custom-call(bf16[384,1024]{1,0:T(8,128)(2,1)} %bitcast.191, bf16[8192,512]{1,0:T(8,128)(2,1)} %bitcast.186, bf16[8192,512]{1,0:T(8,128)(2,1)} %bitcast.185), custom_call_target="tpu_custom_call" | custom-call | flops 6442450944 | bytes 23068672 | tf_op jit(solution)/shard_map/pallas_call | solution.py:417
  344.5 4.8 %reduce_sum.52 = bf16[48,8192]{1,0:T(8,128)(2,1)} reduce(bf16[8,48,8192]{2,1,0:T(8,128)(2,1)} %shard_map.103, bf16[]{:T(256)} %constant.12.clone.1), dimensions={0}, to_apply=%region_6.7 | reduce | flops 2752512 | bytes 7077890 | tf_op jit(solution)/shard_map/reduce_sum | solution.py:488
  349.3 1.5 maximum_bitcast_fusion
  (74 shorter events, 16.9 us)
Async XLA Ops:
  7.2 89.9 %all-gather.3.cloned.1.call-start = ((), (), s32[]{:S(2)}) async-start(), calls=%async_computation.4 | async-start | bytes 3538944 | tf_op jit(solution)/shard_map/all_gather | solution.py:443
  9.3 341.6 %reduce-scatter.5.cloned.1.call-start = ((), (), s32[]{:S(2)}) async-start(), calls=%async_computation.3 | async-start | bytes 8912896 | tf_op jit(solution)/shard_map/reduce_scatter | solution.py:475
  14.9 2.0 copy-start.2
  72.8 6.4 %copy-start.14 = (s32[2]{0:T(128)S(1)}, s32[2]{0:T(128)}, u32[]{:S(2)}) copy-start(s32[2]{0:T(128)} %param.13) | copy-start | bytes 28
  72.8 8.3 %copy-start.4 = (bf16[1,1,128,4096]{2,3,1,0:T(8,128)(2,1)S(1)}, bf16[1,1,128,4096]{2,3,1,0:T(8,128)(2,1)}, u32[]{:S(2)}) copy-start(bf16[1,1,128,4096]{2,3,1,0:T(8,128)(2,1)} %copy.72) | copy-start | bytes 3145732
  79.2 8.0 %copy-start.10 = (bf16[192,4,128]{2,1,0:T(4,128)(2,1)}, bf16[192,4,128]{2,1,0:T(4,128)(2,1)S(1)}, u32[]{:S(2)}) copy-start(bf16[192,4,128]{2,1,0:T(4,128)(2,1)S(1)} %reshape.84) | copy-start | bytes 589828
  87.9 16.9 %copy-start.3 = (bf16[1,1,128,4096]{2,3,1,0:T(8,128)(2,1)S(1)}, bf16[1,1,128,4096]{2,3,1,0:T(8,128)(2,1)}, u32[]{:S(2)}) copy-start(bf16[1,1,128,4096]{2,3,1,0:T(8,128)(2,1)} %copy.73) | copy-start | bytes 3145732
  104.8 6.3 %copy-start.12 = (bf16[192,4,128]{2,1,0:T(4,128)(2,1)}, bf16[192,4,128]{2,1,0:T(4,128)(2,1)S(1)}, u32[]{:S(2)}) copy-start(bf16[192,4,128]{2,1,0:T(4,128)(2,1)S(1)} %reshape.86) | copy-start | bytes 589828
  108.2 3.6 copy-start
  108.2 3.6 copy-start.13
  108.2 3.9 %copy-start.15 = (bf16[1,192,8192]{2,1,0:T(8,128)(2,1)S(1)}, bf16[1,192,8192]{2,1,0:T(8,128)(2,1)}, u32[]{:S(2)}) copy-start(bf16[1,192,8192]{2,1,0:T(8,128)(2,1)} %all-gather.3.cloned.1.call-done) | copy-start | bytes 9437188
  111.1 0.7 copy-start.6
  118.9 232.0 %reduce-scatter.3.cloned.1.call-start = ((), (), s32[]{:S(2)}) async-start(), calls=%async_computation.2 | async-start | bytes 8912896 | tf_op jit(solution)/shard_map/reduce_scatter | solution.py:480
  125.9 3.4 copy-start.5
  135.5 7.1 %copy-start.8 = (bf16[4,192,128]{2,1,0:T(8,128)(2,1)}, bf16[4,192,128]{2,1,0:T(8,128)(2,1)S(1)}, u32[]{:S(2)}) copy-start(bf16[4,192,128]{2,1,0:T(8,128)(2,1)S(1)} %fusion.40) | copy-start | bytes 589828
  145.0 6.3 %copy-start.1 = (bf16[1,8,24,8192]{3,2,1,0:T(8,128)(2,1)S(1)}, bf16[1,8,24,8192]{3,2,1,0:T(8,128)(2,1)}, u32[]{:S(2)}) copy-start(bf16[1,8,24,8192]{3,2,1,0:T(8,128)(2,1)} %shard_map.102) | copy-start | bytes 9437188
  151.3 9.9 %copy-start.7 = (bf16[4,192,128]{2,1,0:T(8,128)(2,1)}, bf16[4,192,128]{2,1,0:T(8,128)(2,1)S(1)}, u32[]{:S(2)}) copy-start(bf16[4,192,128]{2,1,0:T(8,128)(2,1)S(1)} %fusion.41) | copy-start | bytes 589828
  161.1 0.9 copy-start.11
  161.1 0.9 copy-start.17
  162.1 7.0 %copy-start.9 = (bf16[4,192,128]{2,1,0:T(8,128)(2,1)S(1)}, bf16[4,192,128]{2,1,0:T(8,128)(2,1)}, u32[]{:S(2)}) copy-start(bf16[4,192,128]{2,1,0:T(8,128)(2,1)} %copy-done.8) | copy-start | bytes 589828
  168.1 1.3 copy-start.16
Sparse Core Ops, SparseCore 0:
  10.9 86.1 all-gather.2
  119.0 72.6 reduce-scatter.4
  194.7 89.4 reduce-scatter.2

commit v10 on v8

--- a/solution.py
+++ b/solution.py
@@ -325,38 +325,37 @@
     else:
         first = exchange(image_tokens[:1], n_section, False, 0)
     token_list = [first.reshape(image_len, model_width)] + late
-    query_list = []
-    key_list = []
-    value_list = []
-    image_list = []
+    keys_list = []
+    values_list = []
     for sample_index in range(samples_here):
         tokens = token_list[sample_index]
-        keys = jnp.dot(tokens, w_key, preferred_element_type=jnp.float32).astype(jnp.bfloat16)
-        values = jnp.dot(tokens, w_value, preferred_element_type=jnp.float32).astype(jnp.bfloat16)
-        query_gradient, key_gradient, value_gradient = attend_one(
-            query_local[sample_index],
-            keys,
-            values,
-            cotan_local[sample_index],
-            tile_counts[sample_index] * tile_len,
-            text_lengths[sample_index],
-        )
-        query_list.append(query_gradient)
-        key_list.append(key_gradient)
-        value_list.append(value_gradient)
+        keys_list.append(
+            jnp.dot(tokens, w_key, preferred_element_type=jnp.float32).astype(jnp.bfloat16)
+        )
+        values_list.append(
+            jnp.dot(tokens, w_value, preferred_element_type=jnp.float32).astype(jnp.bfloat16)
+        )
+    query_grads, key_grads, value_grads = jax.vmap(attend_one)(
+        query_local,
+        jnp.stack(keys_list),
+        jnp.stack(values_list),
+        cotan_local,
+        tile_counts * tile_len,
+        text_lengths,
+    )
     all_tokens = jnp.concatenate(token_list, axis=0)
     value_term = jnp.einsum(
-        "td,tk->dk", all_tokens, jnp.concatenate(value_list, axis=0),
+        "td,tk->dk", all_tokens, value_grads.reshape(samples_here * image_len, -1),
         preferred_element_type=jnp.float32,
     ).astype(jnp.bfloat16)
     value_sum = lax.psum_scatter(value_term, "dp", scatter_dimension=0, tiled=True)
     key_term = jnp.einsum(
-        "td,tk->dk", all_tokens, jnp.concatenate(key_list, axis=0),
+        "td,tk->dk", all_tokens, key_grads.reshape(samples_here * image_len, -1),
         preferred_element_type=jnp.float32,
     ).astype(jnp.bfloat16)
     key_sum = lax.psum_scatter(key_term, "dp", scatter_dimension=0, tiled=True)
-    query_out = jnp.stack(query_list)[None]
-    kv_grads = jnp.concatenate([jnp.stack(key_list), jnp.stack(value_list)], axis=-1)
+    query_out = query_grads[None]
+    kv_grads = jnp.concatenate([key_grads, value_grads], axis=-1)
     by_slot = kv_grads.reshape(samples_here, n_section, chunk, -1).transpose(1, 0, 2, 3)
     received = image_exchange(
         by_slot.reshape(n_section * samples_here * chunk, -1), w_key, w_value, n_section

time: 319 us -> 320 us (level); the launches traced: 318 us -> 314 us
  matrix products: 84.1 us -> 73.7 us
  local copies, waits for them, and re-layouts: 20.1 us -> 12.4 us
  waiting for transfers between devices: 9.18 us -> 16.3 us
  Pallas kernels: 182 us -> 188 us
    pallas_call x1, Pallas kernels: 126 us -> 137 us  [image_exchange(): pl.pallas_call(functools.partial(image_kernel, n, tiles), out_shape=jax.S...]
    sub x2 -> x0, matrix products: 6.78 us -> none  [attend_one(): raised = jnp.exp(scores - row_max)]
    sub x0 -> x1, other arithmetic: none -> 4.48 us  [attend_one(): raised = jnp.exp(scores - row_max)]
    pallas_call x1, Pallas kernels: 55.3 us -> 51.1 us  [relay_gather(): pl.pallas_call(relay_gather_kernel, out_shape=jax.ShapeDtypeStruct((sampl...]
    all_gather x1, waiting for transfers between devices: 9.12 us -> 13.1 us  [shards(): lax.all_gather(image_tokens[i], 'section', axis=0, tiled=True)]
    reshape x8 -> x0, local copies, waits for them, and re-layouts: 3.62 us -> none  [the longest x2 1.12 us: attend_one(): heads_of_values = value_rows.reshape(total_keys, KEY_VALUE_HEADS, HEAD_SIZE)]
    slice x3 -> x0, local copies, waits for them, and re-layouts: 3.58 us -> none  [the longest x1 1.68 us: shards(): query_local[sample_index]]
    dot_general x2 -> x3, matrix products: 16.5 us -> 19.3 us  [the longest x1 9.69 us: shards(): jnp.einsum('td,tk->dk', all_tokens, key_grads.reshape(samples_here * imag...]
  transfers between devices with their start and end apart: 3 -> 3, of which waited for: 1 -> 2; matrix products, arithmetic and copies ran while one was open for 27% -> 16% of each run, Pallas kernels for 57% -> 60%
where the time goes in v10:
time: 320 us; the launch traced here: 314 us
  Pallas kernels  188 us (59%)
  matrix products  73.7 us (23%)
  waiting for transfers between devices  16.3 us (5%)
  between operations  14 us (4%)
  local copies, waits for them, and re-layouts  12.4 us (4%)
  other arithmetic  9.67 us (3%)
    pallas_call x1, Pallas kernels, image_exchange(): pl.pallas_call(functools.partial(image_kernel, n, tiles), out_shape=jax.S...  137 us
    pallas_call x1, Pallas kernels, relay_gather(): pl.pallas_call(relay_gather_kernel, out_shape=jax.ShapeDtypeStruct((sampl...  51.1 us
    all_gather x1, waiting for transfers between devices, shards(): lax.all_gather(image_tokens[i], 'section', axis=0, tiled=True)  13.1 us
    dot_general x2, matrix products, shards(): jnp.dot(tokens, w_key, preferred_element_type=jnp.float32)  12.8 us
    dot_general x1, matrix products, attend_one(): jnp.einsum('hgln,lhgd->nhd', score_grad, heads_of_queries, preferred_elem...  11.4 us
    dot_general x2, matrix products, shards(): jnp.dot(tokens, w_value, preferred_element_type=jnp.float32)  11.3 us
    dot_general x1, matrix products, attend_one(): jnp.einsum('hgln,nhd->lhgd', score_grad, heads_of_keys, preferred_element...  10.9 us
    dot_general x1, matrix products, shards(): jnp.einsum('td,tk->dk', all_tokens, key_grads.reshape(samples_here * imag...  9.69 us
  transfers between devices with their start and end apart: 3, of which 2 were waited for; matrix products, arithmetic and copies ran while one was open for 16% of the time, Pallas kernels for 60%

profile of v10, /device:TPU:38, one launch (start us, length us, event | category | flops | bytes accessed | tf_op | source)
XLA Modules:
  0.0 313.9 jit_solution(5080274159977999845)
XLA Ops:
  7.2 2.0 fusion.67
  9.3 51.1 %shard_map.102 = bf16[1,8,24,8192]{3,2,1,0:T(8,128)(2,1)} custom-call(bf16[1,24,8192]{2,1,0:T(8,128)(2,1)} %get-tuple-element.12.x_ref), custom_call_target="tpu_custom_call" | custom-call | tf_op jit(solution)/shard_map/pallas_call | solution.py:183
  60.5 6.7 %convolution_convert_fusion.5 = bf16[192,512]{1,0:T(8,128)(2,1)S(1)} fusion(bf16[192,8192]{1,0:T(8,128)(2,1)} %bitcast.132, bf16[1,8192,512]{2,1,0:T(8,128)(2,1)} %param.9), kind=kOutput, calls=%fused_computation.39 | convolution fusion | flops 1610711040 | bytes 11730944 | tf_op jit(solution)/shard_map/dot_general | solution.py:333
  67.2 3.4 %copy.36 = bf16[32,8,32,128]{3,2,1,0:T(8,128)(2,1)} copy(bf16[32,8,32,128]{3,1,2,0:T(8,128)(2,1)} %bitcast.136) | data formatting | bytes 4194304
  70.6 5.2 %convolution_convert_fusion.3 = bf16[192,512]{1,0:T(8,128)(2,1)S(1)} fusion(bf16[192,8192]{1,0:T(8,128)(2,1)S(1)} %bitcast.134, bf16[1,8192,512]{2,1,0:T(8,128)(2,1)} %param.10), kind=kOutput, calls=%fused_computation.37 | convolution fusion | flops 1610711040 | bytes 11730944 | tf_op jit(solution)/shard_map/dot_general | solution.py:336
  75.9 2.1 copy.37
  78.2 13.1 %all-gather.3.cloned.1.call-done = bf16[1,192,8192]{2,1,0:T(8,128)(2,1)} async-done(((bf16[1,24,8192]{2,1,0:T(8,128)(2,1)}), bf16[1,192,8192]{2,1,0:T(8,128)(2,1)}) %all-gather.3.cloned.1.call-update) | async-done | bytes 3145744 | tf_op jit(solution)/shard_map/all_gather | solution.py:320
  91.2 6.1 %convolution_convert_fusion.4 = bf16[192,512]{1,0:T(8,128)(2,1)S(1)} fusion(bf16[1,192,8192]{2,1,0:T(8,128)(2,1)} %all-gather.3.cloned.1.call-done, bf16[1,8192,512]{2,1,0:T(8,128)(2,1)} %param.9), kind=kOutput, calls=%fused_computation.38 | convolution fusion | flops 1610711040 | bytes 11730944 | tf_op jit(solution)/shard_map/dot_general | solution.py:333
  97.5 6.1 %convolution_convert_fusion.2 = bf16[192,512]{1,0:T(8,128)(2,1)S(1)} fusion(bf16[1,8192,512]{2,1,0:T(8,128)(2,1)} %param.10, bf16[1,192,8192]{2,1,0:T(8,128)(2,1)} %all-gather.3.cloned.1.call-done), kind=kOutput, calls=%fused_computation.36 | convolution fusion | flops 1610711040 | bytes 11730944 | tf_op jit(solution)/shard_map/dot_general | solution.py:336
  103.7 2.6 fusion.19
  106.3 4.5 %fusion.68 = (f32[2,4,8,128]{3,2,1,0:T(8,128)S(1)}, f32[2,4,8,128,192]{3,4,2,1,0:T(8,128)}) fusion(f32[2,4,192,128,8]{3,2,4,1,0:T(8,128)S(1)} %fusion.19, pred[2,192]{1,0:T(4,128)(4,1)S(1)} %iota_compare_fusion), kind=kOutput, calls=%fused_computation.74 | output fusion | flops 9437375 | bytes 12616064 | tf_op jit(solution)/shard_map/vmap()/sub | solution.py:38
  110.8 3.7 %fusion.21 = f32[2,4,192,128,8]{3,2,4,1,0:T(8,128)} fusion(bf16[2,128,4,8,128]{4,3,2,1,0:T(8,128)(2,1)S(1)} %bitcast.127, pred[2,128]{1,0:T(4,128)(4,1)S(1)} %iota_compare_fusion.1, bf16[1,192,4,128]{3,1,2,0:T(8,128)(2,1)S(1)} %copy.23, bf16[1,192,4,128]{3,1,2,0:T(8,128)(2,1)S(1)} %copy.22), kind=kOutput, calls=%fused_computation.29 | convolution fusion | flops 404488192 | bytes 8782080 | tf_op jit(solution)/shard_map/vmap(lhgd,nhd->hgln)/dot_general | solution.py:44
  114.5 11.4 %fusion.34 = bf16[2,192,4,128]{3,1,2,0:T(8,128)(2,1)S(1)} fusion(bf16[2,128,4,8,128]{4,3,2,1,0:T(8,128)(2,1)} %bitcast.130, f32[2,4,192,128,8]{3,2,4,1,0:T(8,128)} %fusion.21, f32[2,4,8,128,192]{3,4,2,1,0:T(8,128)} %get-tuple-element.15, f32[2,4,8,128]{3,2,1,0:T(8,128)S(1)} %get-tuple-element.14), kind=kOutput, calls=%fused_computation.34 | convolution fusion | flops 413868224 | bytes 15106048 | tf_op jit(solution)/shard_map/vmap(hgln,lhgd->nhd)/dot_general | solution.py:52
  125.9 0.3 copy.26
  126.2 9.7 %convolution_convert_fusion.1 = bf16[8192,512]{1,0:T(8,128)(2,1)} fusion(bf16[192,8192]{1,0:T(8,128)(2,1)} %bitcast.142, bf16[192,8192]{1,0:T(8,128)(2,1)} %bitcast.133, bf16[48,8,4,128]{3,2,1,0:T(4,128)(2,1)S(1)} %bitcast.139), kind=kOutput, calls=%fused_computation.3 | convolution fusion | flops 3238002688 | bytes 15073280 | tf_op jit(solution)/shard_map/td,tk->dk/dot_general | solution.py:352
  136.0 4.4 %fusion.37 = bf16[2,192,4,128]{3,1,2,0:T(8,128)(2,1)S(1)} fusion(bf16[2,128,4,8,128]{4,3,2,1,0:T(8,128)(2,1)S(1)} %bitcast.128, pred[2,128]{1,0:T(4,128)(4,1)S(1)} %iota_compare_fusion.1, f32[2,4,8,128,192]{3,4,2,1,0:T(8,128)} %get-tuple-element.15, f32[2,4,8,128]{3,2,1,0:T(8,128)S(1)} %get-tuple-element.14), kind=kOutput, calls=%fused_computation.35 | convolution fusion | flops 407044096 | bytes 8814848 | tf_op jit(solution)/shard_map/vmap(hgln,lhgd->nhd)/dot_general | solution.py:41
  140.4 0.3 copy.27
  140.7 7.0 %convolution_convert_fusion = bf16[8192,512]{1,0:T(8,128)(2,1)} fusion(bf16[192,8192]{1,0:T(8,128)(2,1)S(1)} %bitcast.143, bf16[192,8192]{1,0:T(8,128)(2,1)S(1)} %bitcast.135, bf16[48,8,4,128]{3,2,1,0:T(4,128)(2,1)S(1)} %bitcast.140), kind=kOutput, calls=%fused_computation.2 | convolution fusion | flops 3238002688 | bytes 15073280 | tf_op jit(solution)/shard_map/td,tk->dk/dot_general | solution.py:347
  148.1 1.0 copy.28
  149.1 10.9 %fusion.17 = bf16[2,4,128,8,128]{4,2,3,1,0:T(8,128)(2,1)S(1)} fusion(f32[2,4,192,128,8]{3,2,4,1,0:T(8,128)} %fusion.21, bf16[1,192,4,128]{3,1,2,0:T(8,128)(2,1)S(1)} %copy.20, bf16[1,192,4,128]{3,1,2,0:T(8,128)(2,1)S(1)} %copy.19, f32[2,4,8,128,192]{3,4,2,1,0:T(8,128)} %get-tuple-element.15, f32[2,4,8,128]{3,2,1,0:T(8,128)S(1)} %get-tuple-element.14), kind=kOutput, calls=%fused_computation.25 | convolution fusion | flops 415506624 | bytes 15106048 | tf_op jit(solution)/shard_map/vmap(hgln,nhd->lhgd)/dot_general | solution.py:49
  160.0 2.7 copy.31
  162.7 136.6 %shard_map.103 = bf16[8,48,8192]{2,1,0:T(8,128)(2,1)} custom-call(bf16[384,1024]{1,0:T(8,128)(2,1)} %bitcast.131, bf16[8192,512]{1,0:T(8,128)(2,1)} %bitcast.126, bf16[8192,512]{1,0:T(8,128)(2,1)} %bitcast.125), custom_call_target="tpu_custom_call" | custom-call | flops 6442450944 | bytes 23068672 | tf_op jit(solution)/shard_map/pallas_call | solution.py:289
  299.3 4.9 %reduce_sum.32 = bf16[48,8192]{1,0:T(8,128)(2,1)} reduce(bf16[8,48,8192]{2,1,0:T(8,128)(2,1)} %shard_map.103, bf16[]{:T(256)} %constant.10.clone.1), dimensions={0}, to_apply=%region_3.4 | reduce | flops 2752512 | bytes 7077890 | tf_op jit(solution)/shard_map/reduce_sum | solution.py:364
  304.3 3.1 %reduce-scatter.5.cloned.1.call-done = bf16[512,512]{1,0:T(8,128)(2,1)} async-done(((bf16[8192,512]{1,0:T(8,128)(2,1)}), bf16[512,512]{1,0:T(8,128)(2,1)}) %reduce-scatter.5.cloned.1.call-update) | async-done | bytes 524304 | tf_op jit(solution)/shard_map/reduce_scatter | solution.py:351
  (31 shorter events, 1.1 us)
Async XLA Ops:
  7.2 84.1 %all-gather.3.cloned.1.call-start = ((), (), s32[]{:S(2)}) async-start(), calls=%async_computation.4 | async-start | bytes 3538944 | tf_op jit(solution)/shard_map/all_gather | solution.py:320
  9.3 295.0 %reduce-scatter.3.cloned.1.call-start = ((), (), s32[]{:S(2)}) async-start(), calls=%async_computation.2 | async-start | bytes 8912896 | tf_op jit(solution)/shard_map/reduce_scatter | solution.py:356
  60.5 10.2 %copy-start = (bf16[1,8,24,8192]{3,2,1,0:T(8,128)(2,1)S(1)}, bf16[1,8,24,8192]{3,2,1,0:T(8,128)(2,1)}, u32[]{:S(2)}) copy-start(bf16[1,8,24,8192]{3,2,1,0:T(8,128)(2,1)} %shard_map.102) | copy-start | bytes 9437188
  70.6 7.4 %copy-start.3 = (s32[2]{0:T(128)S(1)}, s32[2]{0:T(128)}, u32[]{:S(2)}) copy-start(s32[2]{0:T(128)} %param.12) | copy-start | bytes 28
  70.6 7.4 %copy-start.4 = (s32[2]{0:T(128)S(1)}, s32[2]{0:T(128)}, u32[]{:S(2)}) copy-start(s32[2]{0:T(128)} %param.13) | copy-start | bytes 28
  135.9 171.5 %reduce-scatter.5.cloned.1.call-start = ((), (), s32[]{:S(2)}) async-start(), calls=%async_computation.3 | async-start | bytes 8912896 | tf_op jit(solution)/shard_map/reduce_scatter | solution.py:351
  136.0 4.7 %copy-start.1 = (bf16[1,8,24,8192]{3,2,1,0:T(8,128)(2,1)S(1)}, bf16[1,8,24,8192]{3,2,1,0:T(8,128)(2,1)}, u32[]{:S(2)}) copy-start(bf16[1,8,24,8192]{3,2,1,0:T(8,128)(2,1)} %shard_map.102) | copy-start | bytes 9437188
  136.0 4.7 %copy-start.2 = (bf16[1,192,8192]{2,1,0:T(8,128)(2,1)S(1)}, bf16[1,192,8192]{2,1,0:T(8,128)(2,1)}, u32[]{:S(2)}) copy-start(bf16[1,192,8192]{2,1,0:T(8,128)(2,1)} %all-gather.3.cloned.1.call-done) | copy-start | bytes 9437188
Sparse Core Ops, SparseCore 0:
  10.9 80.3 all-gather.2
  136.1 90.4 reduce-scatter.2
  229.6 77.8 reduce-scatter.4

commit v11 on v10

--- a/solution.py
+++ b/solution.py
@@ -56,6 +56,62 @@
         query_gradient.reshape(total_rows, QUERY_HEADS * HEAD_SIZE),
         key_gradient.reshape(total_keys, KEY_VALUE_HEADS * HEAD_SIZE),
         value_gradient.reshape(total_keys, KEY_VALUE_HEADS * HEAD_SIZE),
+    )
+
+
+def attend_front(queries, key_rows, cotangent, key_limit, row_limit):
+    total_rows = queries.shape[0]
+    total_keys = key_rows.shape[0]
+    group_width = QUERY_HEADS // KEY_VALUE_HEADS
+    heads_of_queries = queries.reshape(total_rows, KEY_VALUE_HEADS, group_width, HEAD_SIZE)
+    heads_of_keys = key_rows.reshape(total_keys, KEY_VALUE_HEADS, HEAD_SIZE)
+    row_live = (jnp.arange(total_rows) < row_limit)[:, None]
+    active_cotangent = jnp.where(row_live, cotangent, jnp.zeros_like(cotangent))
+    head_gradient = active_cotangent.reshape(total_rows, KEY_VALUE_HEADS, group_width, HEAD_SIZE)
+    scaling = 1.0 / math.sqrt(HEAD_SIZE)
+    scores = (
+        jnp.einsum(
+            "lhgd,nhd->hgln", heads_of_queries, heads_of_keys, preferred_element_type=jnp.float32
+        )
+        * scaling
+    )
+    key_live = jnp.arange(total_keys) < key_limit
+    scores = jnp.where(key_live, scores, -jnp.inf)
+    row_max = jnp.max(scores, axis=-1, keepdims=True)
+    raised = jnp.exp(scores - row_max)
+    weights = raised / jnp.sum(raised, axis=-1, keepdims=True)
+    weights_low = weights.astype(jnp.bfloat16)
+    value_gradient = jnp.einsum(
+        "hgln,lhgd->nhd", weights_low, head_gradient, preferred_element_type=jnp.float32
+    ).astype(jnp.bfloat16)
+    return weights, value_gradient.reshape(total_keys, KEY_VALUE_HEADS * HEAD_SIZE)
+
+
+def attend_back(queries, key_rows, value_rows, cotangent, row_limit, weights):
+    total_rows = queries.shape[0]
+    total_keys = key_rows.shape[0]
+    group_width = QUERY_HEADS // KEY_VALUE_HEADS
+    heads_of_queries = queries.reshape(total_rows, KEY_VALUE_HEADS, group_width, HEAD_SIZE)
+    heads_of_keys = key_rows.reshape(total_keys, KEY_VALUE_HEADS, HEAD_SIZE)
+    heads_of_values = value_rows.reshape(total_keys, KEY_VALUE_HEADS, HEAD_SIZE)
+    row_live = (jnp.arange(total_rows) < row_limit)[:, None]
+    active_cotangent = jnp.where(row_live, cotangent, jnp.zeros_like(cotangent))
+    head_gradient = active_cotangent.reshape(total_rows, KEY_VALUE_HEADS, group_width, HEAD_SIZE)
+    scaling = 1.0 / math.sqrt(HEAD_SIZE)
+    prob_grad = jnp.einsum(
+        "lhgd,nhd->hgln", head_gradient, heads_of_values, preferred_element_type=jnp.float32
+    )
+    row_dot = jnp.sum(weights * prob_grad, axis=-1, keepdims=True)
+    score_grad = (weights * (prob_grad - row_dot) * scaling).astype(jnp.bfloat16)
+    query_gradient = jnp.einsum(
+        "hgln,nhd->lhgd", score_grad, heads_of_keys, preferred_element_type=jnp.float32
+    ).astype(jnp.bfloat16)
+    key_gradient = jnp.einsum(
+        "hgln,lhgd->nhd", score_grad, heads_of_queries, preferred_element_type=jnp.float32
+    ).astype(jnp.bfloat16)
+    return (
+        query_gradient.reshape(total_rows, QUERY_HEADS * HEAD_SIZE),
+        key_gradient.reshape(total_keys, KEY_VALUE_HEADS * HEAD_SIZE),
     )
 
 
@@ -335,20 +391,22 @@
         values_list.append(
             jnp.dot(tokens, w_value, preferred_element_type=jnp.float32).astype(jnp.bfloat16)
         )
-    query_grads, key_grads, value_grads = jax.vmap(attend_one)(
-        query_local,
-        jnp.stack(keys_list),
-        jnp.stack(values_list),
-        cotan_local,
-        tile_counts * tile_len,
-        text_lengths,
+    keys_both = jnp.stack(keys_list)
+    values_both = jnp.stack(values_list)
+    key_limits = tile_counts * tile_len
+    weights, value_grads = jax.vmap(attend_front)(
+        query_local, keys_both, cotan_local, key_limits, text_lengths
     )
     all_tokens = jnp.concatenate(token_list, axis=0)
     value_term = jnp.einsum(
         "td,tk->dk", all_tokens, value_grads.reshape(samples_here * image_len, -1),
         preferred_element_type=jnp.float32,
     ).astype(jnp.bfloat16)
+    value_term, weights = lax.optimization_barrier((value_term, weights))
     value_sum = lax.psum_scatter(value_term, "dp", scatter_dimension=0, tiled=True)
+    query_grads, key_grads = jax.vmap(attend_back)(
+        query_local, keys_both, values_both, cotan_local, text_lengths, weights
+    )
     key_term = jnp.einsum(
         "td,tk->dk", all_tokens, key_grads.reshape(samples_here * image_len, -1),
         preferred_element_type=jnp.float32,

time: 320 us -> 315 us (0.984); the launches traced: 314 us -> 314 us
  local copies, waits for them, and re-layouts: 12.4 us -> 19 us
  Pallas kernels: 188 us -> 182 us
    pallas_call x1, Pallas kernels: 137 us -> 127 us  [image_exchange(): pl.pallas_call(functools.partial(image_kernel, n, tiles), out_shape=jax.S...]
    unnamed x13 -> x25, local copies, waits for them, and re-layouts: 8.21 us -> 13.8 us
    all_gather x1, waiting for transfers between devices: 13.1 us -> 17.7 us  [shards(): lax.all_gather(image_tokens[i], 'section', axis=0, tiled=True)]
    pallas_call x1, Pallas kernels: 51.1 us -> 55.3 us  [relay_gather(): pl.pallas_call(relay_gather_kernel, out_shape=jax.ShapeDtypeStruct((sampl...]
  transfers between devices with their start and end apart: 3 -> 3, of which waited for: 2 -> 1; matrix products, arithmetic and copies ran while one was open for 16% -> 23% of each run, Pallas kernels for 60% -> 58%
where the time goes in v11:
time: 315 us; the launch traced here: 314 us
  Pallas kernels  182 us (58%)
  matrix products  71.5 us (23%)
  local copies, waits for them, and re-layouts  19 us (6%)
  waiting for transfers between devices  17.7 us (6%)
  between operations  14 us (4%)
  other arithmetic  9.16 us (3%)
    pallas_call x1, Pallas kernels, image_exchange(): pl.pallas_call(functools.partial(image_kernel, n, tiles), out_shape=jax.S...  127 us
    pallas_call x1, Pallas kernels, relay_gather(): pl.pallas_call(relay_gather_kernel, out_shape=jax.ShapeDtypeStruct((sampl...  55.3 us
    all_gather x1, waiting for transfers between devices, shards(): lax.all_gather(image_tokens[i], 'section', axis=0, tiled=True)  17.7 us
    unnamed x25, local copies, waits for them, and re-layouts  13.8 us
    dot_general x1, matrix products, attend_back(): jnp.einsum('hgln,lhgd->nhd', score_grad, heads_of_queries, preferred_elem...  12.7 us
    dot_general x2, matrix products, shards(): jnp.dot(tokens, w_value, preferred_element_type=jnp.float32)  12.7 us
    dot_general x2, matrix products, shards(): jnp.dot(tokens, w_key, preferred_element_type=jnp.float32)  12.3 us
    dot_general x1, matrix products, attend_back(): jnp.einsum('hgln,nhd->lhgd', score_grad, heads_of_keys, preferred_element...  10.6 us
  transfers between devices with their start and end apart: 3, of which 1 were waited for; matrix products, arithmetic and copies ran while one was open for 23% of the time, Pallas kernels for 58%

profile of v11, /device:TPU:38, one launch (start us, length us, event | category | flops | bytes accessed | tf_op | source)
XLA Modules:
  0.0 313.8 jit_solution(3909398033446058387)
XLA Ops:
  7.2 2.0 fusion.67
  9.3 3.4 %copy.36 = bf16[32,8,32,128]{3,2,1,0:T(8,128)(2,1)} copy(bf16[32,8,32,128]{3,1,2,0:T(8,128)(2,1)} %bitcast.136) | data formatting | bytes 4194304
  12.7 2.1 copy.37
  14.8 55.3 %shard_map.102 = bf16[1,8,24,8192]{3,2,1,0:T(8,128)(2,1)} custom-call(bf16[1,24,8192]{2,1,0:T(8,128)(2,1)} %get-tuple-element.16.x_ref), custom_call_target="tpu_custom_call" | custom-call | tf_op jit(solution)/shard_map/pallas_call | solution.py:239
  70.1 6.2 %convolution_convert_fusion.5 = bf16[192,512]{1,0:T(8,128)(2,1)S(1)} fusion(bf16[192,8192]{1,0:T(8,128)(2,1)} %bitcast.132, bf16[1,8192,512]{2,1,0:T(8,128)(2,1)} %param.9), kind=kOutput, calls=%fused_computation.39 | convolution fusion | flops 1610711040 | bytes 11730944 | tf_op jit(solution)/shard_map/dot_general | solution.py:389
  76.5 17.7 %all-gather.3.cloned.1.call-done = bf16[1,192,8192]{2,1,0:T(8,128)(2,1)} async-done(((bf16[1,24,8192]{2,1,0:T(8,128)(2,1)}), bf16[1,192,8192]{2,1,0:T(8,128)(2,1)}) %all-gather.3.cloned.1.call-update) | async-done | bytes 3145744 | tf_op jit(solution)/shard_map/all_gather | solution.py:376
  94.2 6.1 %convolution_convert_fusion.4 = bf16[192,512]{1,0:T(8,128)(2,1)S(1)} fusion(bf16[1,192,8192]{2,1,0:T(8,128)(2,1)} %all-gather.3.cloned.1.call-done, bf16[1,8192,512]{2,1,0:T(8,128)(2,1)} %param.9), kind=kOutput, calls=%fused_computation.38 | convolution fusion | flops 1610711040 | bytes 11730944 | tf_op jit(solution)/shard_map/dot_general | solution.py:389
  101.1 2.6 fusion.19
  103.7 2.7 fusion.68
  106.4 1.4 broadcast_divide_fusion
  107.9 3.2 %copy-done = f32[2,4,8,128,192]{3,4,2,1,0:T(8,128)} copy-done((f32[2,4,8,128,192]{3,4,2,1,0:T(8,128)}, f32[2,4,8,128,192]{3,4,2,1,0:T(8,128)S(1)}, u32[]{:S(2)}) %copy-start) | copy-done | bytes 6291480
  111.0 1.4 fusion.37
  113.0 6.7 %convolution_convert_fusion.1 = bf16[8192,512]{1,0:T(8,128)(2,1)} fusion(bf16[192,8192]{1,0:T(8,128)(2,1)S(1)} %bitcast.143, bf16[192,8192]{1,0:T(8,128)(2,1)S(1)} %bitcast.134, bf16[48,8,4,128]{3,2,1,0:T(4,128)(2,1)S(1)} %bitcast.139), kind=kOutput, calls=%fused_computation.3 | convolution fusion | flops 3238002688 | bytes 15073280 | tf_op jit(solution)/shard_map/td,tk->dk/dot_general | solution.py:401
  120.0 6.1 %convolution_convert_fusion.3 = bf16[192,512]{1,0:T(8,128)(2,1)S(1)} fusion(bf16[192,8192]{1,0:T(8,128)(2,1)} %bitcast.133, bf16[1,8192,512]{2,1,0:T(8,128)(2,1)} %param.10), kind=kOutput, calls=%fused_computation.37 | convolution fusion | flops 1610711040 | bytes 11730944 | tf_op jit(solution)/shard_map/dot_general | solution.py:392
  126.2 6.5 %convolution_convert_fusion.2 = bf16[192,512]{1,0:T(8,128)(2,1)S(1)} fusion(bf16[1,8192,512]{2,1,0:T(8,128)(2,1)} %param.10, bf16[1,192,8192]{2,1,0:T(8,128)(2,1)} %all-gather.3.cloned.1.call-done), kind=kOutput, calls=%fused_computation.36 | convolution fusion | flops 1610711040 | bytes 11730944 | tf_op jit(solution)/shard_map/dot_general | solution.py:392
  132.8 3.7 %fusion.21 = f32[2,4,192,128,8]{3,2,4,1,0:T(8,128)} fusion(bf16[2,128,4,8,128]{4,3,2,1,0:T(8,128)(2,1)S(1)} %bitcast.126, pred[2,128]{1,0:T(4,128)(4,1)S(1)} %iota_compare_fusion.1, bf16[1,192,4,128]{3,1,2,0:T(8,128)(2,1)S(1)} %copy.25, bf16[1,192,4,128]{3,1,2,0:T(8,128)(2,1)S(1)} %copy.24), kind=kOutput, calls=%fused_computation.29 | convolution fusion | flops 404488192 | bytes 8782080 | tf_op jit(solution)/shard_map/vmap(lhgd,nhd->hgln)/dot_general | solution.py:101
  136.6 12.7 %fusion.34 = bf16[2,192,4,128]{3,1,2,0:T(8,128)(2,1)} fusion(bf16[2,128,4,8,128]{4,3,2,1,0:T(8,128)(2,1)} %bitcast.130, f32[2,4,8,128,192]{3,4,2,1,0:T(8,128)} %copy-done, f32[2,4,192,128,8]{3,2,4,1,0:T(8,128)} %fusion.21), kind=kOutput, calls=%fused_computation.34 | convolution fusion | flops 410722496 | bytes 15073280 | tf_op jit(solution)/shard_map/vmap(hgln,lhgd->nhd)/dot_general | solution.py:109
  149.3 1.3 copy.27
  151.4 8.8 %convolution_convert_fusion = bf16[8192,512]{1,0:T(8,128)(2,1)} fusion(bf16[192,8192]{1,0:T(8,128)(2,1)} %bitcast.142, bf16[192,8192]{1,0:T(8,128)(2,1)S(1)} %bitcast.135, bf16[48,8,4,128]{3,2,1,0:T(4,128)(2,1)S(1)} %bitcast.140), kind=kOutput, calls=%fused_computation.2 | convolution fusion | flops 3238002688 | bytes 15073280 | tf_op jit(solution)/shard_map/td,tk->dk/dot_general | solution.py:410
  161.3 10.6 %fusion.17 = bf16[2,4,128,8,128]{4,2,3,1,0:T(8,128)(2,1)S(1)} fusion(f32[2,4,8,128,192]{3,4,2,1,0:T(8,128)} %copy-done, f32[2,4,192,128,8]{3,2,4,1,0:T(8,128)} %fusion.21, bf16[1,192,4,128]{3,1,2,0:T(8,128)(2,1)} %copy-done.7, bf16[1,192,4,128]{3,1,2,0:T(8,128)(2,1)S(1)} %copy-done.6), kind=kOutput, calls=%fused_computation.25 | convolution fusion | flops 412360896 | bytes 15073280 | tf_op jit(solution)/shard_map/vmap(hgln,nhd->lhgd)/dot_general | solution.py:106
  171.9 2.7 copy.31
  174.7 1.0 copy.29
  175.6 126.8 %shard_map.103 = bf16[8,48,8192]{2,1,0:T(8,128)(2,1)} custom-call(bf16[384,1024]{1,0:T(8,128)(2,1)} %bitcast.131, bf16[8192,512]{1,0:T(8,128)(2,1)} %bitcast.127, bf16[8192,512]{1,0:T(8,128)(2,1)} %bitcast.128), custom_call_target="tpu_custom_call" | custom-call | flops 6442450944 | bytes 23068672 | tf_op jit(solution)/shard_map/pallas_call | solution.py:345
  302.4 4.8 %reduce_sum.32 = bf16[48,8192]{1,0:T(8,128)(2,1)} reduce(bf16[8,48,8192]{2,1,0:T(8,128)(2,1)} %shard_map.103, bf16[]{:T(256)} %constant.1.clone.1), dimensions={0}, to_apply=%region_3.4 | reduce | flops 2752512 | bytes 7077890 | tf_op jit(solution)/shard_map/reduce_sum | solution.py:422
  (44 shorter events, 3.9 us)
Async XLA Ops:
  7.2 87.0 %all-gather.3.cloned.1.call-start = ((), (), s32[]{:S(2)}) async-start(), calls=%async_computation.4 | async-start | bytes 3538944 | tf_op jit(solution)/shard_map/all_gather | solution.py:376
  9.3 298.0 %reduce-scatter.5.cloned.1.call-start = ((), (), s32[]{:S(2)}) async-start(), calls=%async_computation.3 | async-start | bytes 8912896 | tf_op jit(solution)/shard_map/reduce_scatter | solution.py:406
  70.1 6.3 %copy-start.9 = (s32[2]{0:T(128)S(1)}, s32[2]{0:T(128)}, u32[]{:S(2)}) copy-start(s32[2]{0:T(128)} %param.13) | copy-start | bytes 28
  70.1 6.4 %copy-start.10 = (s32[2]{0:T(128)S(1)}, s32[2]{0:T(128)}, u32[]{:S(2)}) copy-start(s32[2]{0:T(128)} %param.12) | copy-start | bytes 28
  76.4 24.1 %copy-start.5 = (bf16[1,192,4,128]{3,1,2,0:T(8,128)(2,1)}, bf16[1,192,4,128]{3,1,2,0:T(8,128)(2,1)S(1)}, u32[]{:S(2)}) copy-start(bf16[1,192,4,128]{3,1,2,0:T(8,128)(2,1)S(1)} %copy.19) | copy-start | bytes 589828
  100.4 0.7 copy-start.7
  107.8 3.2 %copy-start = (f32[2,4,8,128,192]{3,4,2,1,0:T(8,128)}, f32[2,4,8,128,192]{3,4,2,1,0:T(8,128)S(1)}, u32[]{:S(2)}) copy-start(f32[2,4,8,128,192]{3,4,2,1,0:T(8,128)S(1)} %broadcast_divide_fusion) | copy-start | bytes 18874372
  107.9 4.9 %copy-start.1 = (bf16[1,8,24,8192]{3,2,1,0:T(8,128)(2,1)S(1)}, bf16[1,8,24,8192]{3,2,1,0:T(8,128)(2,1)}, u32[]{:S(2)}) copy-start(bf16[1,8,24,8192]{3,2,1,0:T(8,128)(2,1)} %shard_map.102) | copy-start | bytes 9437188
  107.9 5.1 %copy-start.8 = (bf16[1,192,8192]{2,1,0:T(8,128)(2,1)S(1)}, bf16[1,192,8192]{2,1,0:T(8,128)(2,1)}, u32[]{:S(2)}) copy-start(bf16[1,192,8192]{2,1,0:T(8,128)(2,1)} %all-gather.3.cloned.1.call-done) | copy-start | bytes 9437188
  119.7 187.5 %reduce-scatter.3.cloned.1.call-start = ((), (), s32[]{:S(2)}) async-start(), calls=%async_computation.2 | async-start | bytes 8912896 | tf_op jit(solution)/shard_map/reduce_scatter | solution.py:414
  136.6 14.8 %copy-start.2 = (bf16[1,8,24,8192]{3,2,1,0:T(8,128)(2,1)S(1)}, bf16[1,8,24,8192]{3,2,1,0:T(8,128)(2,1)}, u32[]{:S(2)}) copy-start(bf16[1,8,24,8192]{3,2,1,0:T(8,128)(2,1)} %shard_map.102) | copy-start | bytes 9437188
  150.6 0.7 copy-start.3
  160.1 1.0 copy-start.4
  160.1 1.2 copy-start.6
Sparse Core Ops, SparseCore 0:
  10.9 83.2 all-gather.2
  119.9 74.5 reduce-scatter.4
  197.4 96.6 reduce-scatter.2

commit v12 on v11

--- a/solution.py
+++ b/solution.py
@@ -394,9 +394,14 @@
     keys_both = jnp.stack(keys_list)
     values_both = jnp.stack(values_list)
     key_limits = tile_counts * tile_len
-    weights, value_grads = jax.vmap(attend_front)(
-        query_local, keys_both, cotan_local, key_limits, text_lengths
-    )
+    fronts = [
+        attend_front(
+            query_local[i], keys_list[i], cotan_local[i], key_limits[i], text_lengths[i]
+        )
+        for i in range(samples_here)
+    ]
+    weights = jnp.stack([front[0] for front in fronts])
+    value_grads = jnp.stack([front[1] for front in fronts])
     all_tokens = jnp.concatenate(token_list, axis=0)
     value_term = jnp.einsum(
         "td,tk->dk", all_tokens, value_grads.reshape(samples_here * image_len, -1),

time: 315 us -> 327 us (1.038)
  waiting for transfers between devices: 17.7 us -> 4.62 us
  other arithmetic: 9.16 us -> 20.3 us
  local copies, waits for them, and re-layouts: 19 us -> 27.1 us
  matrix products: 71.5 us -> 76.3 us
    all_gather x1, waiting for transfers between devices: 17.7 us -> 4.57 us  [shards(): lax.all_gather(image_tokens[i], 'section', axis=0, tiled=True)]
    another operation x0 -> x4, other arithmetic: none -> 11.6 us  [the longest x3 11.6 us: shards(): weights = jnp.stack([front[0] for front in fronts])]
    sub x0 -> x2, matrix products: none -> 6.32 us  [attend_front(): raised = jnp.exp(scores - row_max)]
    slice x0 -> x3, local copies, waits for them, and re-layouts: none -> 3.99 us  [the longest x1 2.69 us: shards(): query_local[i]]
    unnamed x25 -> x50, local copies, waits for them, and re-layouts: 13.8 us -> 15.5 us
  transfers between devices with their start and end apart: 3 -> 3, of which waited for: 1 -> 1; matrix products, arithmetic and copies ran while one was open for 23% -> 28% of each run, Pallas kernels for 58% -> 56%
where the time goes in v12:
time: 327 us; the launch traced here: 325 us
  Pallas kernels  182 us (56%)
  matrix products  76.3 us (23%)
  local copies, waits for them, and re-layouts  27.1 us (8%)
  other arithmetic  20.3 us (6%)
  between operations  14.1 us (4%)
  waiting for transfers between devices  4.62 us (1%)
    pallas_call x1, Pallas kernels, image_exchange(): pl.pallas_call(functools.partial(image_kernel, n, tiles), out_shape=jax.S...  126 us
    pallas_call x1, Pallas kernels, relay_gather(): pl.pallas_call(relay_gather_kernel, out_shape=jax.ShapeDtypeStruct((sampl...  56.3 us
    unnamed x50, local copies, waits for them, and re-layouts  15.5 us
    dot_general x1, matrix products, attend_back(): jnp.einsum('hgln,lhgd->nhd', score_grad, heads_of_queries, preferred_elem...  12.6 us
    dot_general x2, matrix products, shards(): jnp.dot(tokens, w_key, preferred_element_type=jnp.float32)  12.3 us
    dot_general x2, matrix products, shards(): jnp.dot(tokens, w_value, preferred_element_type=jnp.float32)  11.8 us
    another operation x3, other arithmetic, shards(): weights = jnp.stack([front[0] for front in fronts])  11.6 us
    dot_general x1, matrix products, attend_back(): jnp.einsum('hgln,nhd->lhgd', score_grad, heads_of_keys, preferred_element...  10.5 us
  transfers between devices with their start and end apart: 3, of which 1 were waited for; matrix products, arithmetic and copies ran while one was open for 28% of the time, Pallas kernels for 56%

profile of v12, /device:TPU:38, one launch (start us, length us, event | category | flops | bytes accessed | tf_op | source)
XLA Modules:
  0.0 325.0 jit_solution(6341448316735846663)
XLA Ops:
  7.2 2.0 fusion.111
  9.3 2.7 fusion.110
  12.0 2.4 copy.57
  18.3 56.3 %shard_map.102 = bf16[1,8,24,8192]{3,2,1,0:T(8,128)(2,1)} custom-call(bf16[1,24,8192]{2,1,0:T(8,128)(2,1)} %get-tuple-element.20.x_ref), custom_call_target="tpu_custom_call" | custom-call | tf_op jit(solution)/shard_map/pallas_call | solution.py:239
  74.6 6.1 %convolution_convert_fusion.5 = bf16[192,512]{1,0:T(8,128)(2,1)S(1)} fusion(bf16[192,8192]{1,0:T(8,128)(2,1)} %bitcast.175, bf16[1,8192,512]{2,1,0:T(8,128)(2,1)} %param.9), kind=kOutput, calls=%fused_computation.54 | convolution fusion | flops 1610711040 | bytes 11730944 | tf_op jit(solution)/shard_map/dot_general | solution.py:389
  83.5 2.3 fusion.119
  85.8 2.8 fusion.54
  91.9 2.1 fusion.34
  94.1 4.6 %all-gather.3.cloned.1.call-done = bf16[1,192,8192]{2,1,0:T(8,128)(2,1)} async-done(((bf16[1,24,8192]{2,1,0:T(8,128)(2,1)}), bf16[1,192,8192]{2,1,0:T(8,128)(2,1)}) %all-gather.3.cloned.1.call-update) | async-done | bytes 3145744 | tf_op jit(solution)/shard_map/all_gather | solution.py:376
  98.6 6.1 %convolution_convert_fusion.4 = bf16[192,512]{1,0:T(8,128)(2,1)S(1)} fusion(bf16[1,192,8192]{2,1,0:T(8,128)(2,1)} %all-gather.3.cloned.1.call-done, bf16[1,8192,512]{2,1,0:T(8,128)(2,1)} %param.9), kind=kOutput, calls=%fused_computation.53 | convolution fusion | flops 1610711040 | bytes 11730944 | tf_op jit(solution)/shard_map/dot_general | solution.py:389
  105.5 4.0 %fusion.114 = (f32[4,8,128]{2,1,0:T(8,128)S(1)}, f32[4,8,128,192]{2,3,1,0:T(8,128)}) fusion(pred[192]{0:T(512)(128)(4,1)} %iota_compare_fusion.1, bf16[128,4,8,128]{0,3,2,1:T(8,128)(2,1)} %bitcast.182, bf16[192,4,128,1]{2,1,0,3:T(4,128)(2,1)} %bitcast.189), kind=kOutput, calls=%fused_computation.115 | convolution fusion | flops 204472512 | bytes 4407488 | tf_op jit(solution)/shard_map/sub | solution.py:81
  109.5 4.2 %fusion.35 = f32[1,4,8,128,192]{3,4,2,1,0:T(8,128)} fusion(f32[4,8,128,192]{2,3,1,0:T(8,128)} %get-tuple-element.27, f32[4,8,128]{2,1,0:T(8,128)S(1)} %get-tuple-element.26), kind=kLoop, calls=%fused_computation.44 | loop fusion | flops 786432 | bytes 6307840 | tf_op jit(solution)/shard_map/stack | solution.py:403
  115.5 5.3 %pad_maximum_fusion.1 = f32[2,4,8,128,192]{3,4,2,1,0:T(8,128)} fusion(f32[1,4,8,128,192]{3,4,2,1,0:T(8,128)} %fusion.35, f32[1,4,8,128,192]{3,4,2,1,0:T(8,128)S(1)} %fusion.34), kind=kLoop, calls=%fused_computation.6 | loop fusion | flops 1572864 | bytes 12582912 | tf_op jit(solution)/shard_map/stack | solution.py:403
  120.8 6.8 %convolution_convert_fusion.1 = bf16[8192,512]{1,0:T(8,128)(2,1)} fusion(bf16[384,512]{1,0:T(8,128)(2,1)S(1)} %bitcast.187, bf16[192,8192]{1,0:T(8,128)(2,1)S(1)} %bitcast.191, bf16[192,8192]{1,0:T(8,128)(2,1)S(1)} %bitcast.176), kind=kOutput, calls=%fused_computation.4 | convolution fusion | flops 3238002688 | bytes 15073280 | tf_op jit(solution)/shard_map/td,tk->dk/dot_general | solution.py:406
  127.8 2.2 copy.61
  132.7 5.2 %convolution_convert_fusion.3 = bf16[192,512]{1,0:T(8,128)(2,1)S(1)} fusion(bf16[192,8192]{1,0:T(8,128)(2,1)S(1)} %bitcast.177, bf16[1,8192,512]{2,1,0:T(8,128)(2,1)} %param.10), kind=kOutput, calls=%fused_computation.52 | convolution fusion | flops 1610711040 | bytes 11730944 | tf_op jit(solution)/shard_map/dot_general | solution.py:392
  138.1 6.5 %convolution_convert_fusion.2 = bf16[192,512]{1,0:T(8,128)(2,1)S(1)} fusion(bf16[1,8192,512]{2,1,0:T(8,128)(2,1)} %param.10, bf16[1,192,8192]{2,1,0:T(8,128)(2,1)} %all-gather.3.cloned.1.call-done), kind=kOutput, calls=%fused_computation.51 | convolution fusion | flops 1610711040 | bytes 11730944 | tf_op jit(solution)/shard_map/dot_general | solution.py:392
  144.8 3.7 %fusion.18 = f32[2,4,192,128,8]{3,2,4,1,0:T(8,128)} fusion(bf16[2,128,4,8,128]{4,3,2,1,0:T(8,128)(2,1)S(1)} %bitcast.171, pred[2,128]{1,0:T(4,128)(4,1)S(1)} %iota_compare_fusion, bf16[1,192,4,128]{3,1,2,0:T(8,128)(2,1)S(1)} %copy.35, bf16[1,192,4,128]{3,1,2,0:T(8,128)(2,1)S(1)} %copy.34), kind=kOutput, calls=%fused_computation.27 | convolution fusion | flops 404488192 | bytes 8782080 | tf_op jit(solution)/shard_map/vmap(lhgd,nhd->hgln)/dot_general | solution.py:101
  148.5 12.6 %fusion.39 = bf16[2,192,4,128]{3,1,2,0:T(8,128)(2,1)} fusion(bf16[2,128,4,8,128]{4,3,2,1,0:T(8,128)(2,1)} %bitcast.179, f32[2,4,8,128,192]{3,4,2,1,0:T(8,128)} %pad_maximum_fusion.1, f32[2,4,192,128,8]{3,2,4,1,0:T(8,128)} %fusion.18), kind=kOutput, calls=%fused_computation.46 | convolution fusion | flops 410722496 | bytes 15073280 | tf_op jit(solution)/shard_map/vmap(hgln,lhgd->nhd)/dot_general | solution.py:109
  163.2 8.7 %convolution_convert_fusion = bf16[8192,512]{1,0:T(8,128)(2,1)} fusion(bf16[192,8192]{1,0:T(8,128)(2,1)} %bitcast.190, bf16[192,8192]{1,0:T(8,128)(2,1)S(1)} %bitcast.178, bf16[48,8,4,128]{3,2,1,0:T(4,128)(2,1)S(1)} %bitcast.181), kind=kOutput, calls=%fused_computation.3 | convolution fusion | flops 3238002688 | bytes 15073280 | tf_op jit(solution)/shard_map/td,tk->dk/dot_general | solution.py:415
  173.4 10.5 %fusion.20 = bf16[2,4,128,8,128]{4,2,3,1,0:T(8,128)(2,1)S(1)} fusion(f32[2,4,8,128,192]{3,4,2,1,0:T(8,128)} %pad_maximum_fusion.1, f32[2,4,192,128,8]{3,2,4,1,0:T(8,128)} %fusion.18, bf16[1,192,4,128]{3,1,2,0:T(8,128)(2,1)S(1)} %copy.23, bf16[1,192,4,128]{3,1,2,0:T(8,128)(2,1)S(1)} %copy.22), kind=kOutput, calls=%fused_computation.29 | convolution fusion | flops 412360896 | bytes 15073280 | tf_op jit(solution)/shard_map/vmap(hgln,nhd->lhgd)/dot_general | solution.py:106
  183.9 2.7 copy.43
  187.7 126.0 %shard_map.103 = bf16[8,48,8192]{2,1,0:T(8,128)(2,1)} custom-call(bf16[384,1024]{1,0:T(8,128)(2,1)} %bitcast.174, bf16[8192,512]{1,0:T(8,128)(2,1)} %bitcast.169, bf16[8192,512]{1,0:T(8,128)(2,1)} %bitcast.170), custom_call_target="tpu_custom_call" | custom-call | flops 6442450944 | bytes 23068672 | tf_op jit(solution)/shard_map/pallas_call | solution.py:345
  313.6 4.8 %reduce_sum.42 = bf16[48,8192]{1,0:T(8,128)(2,1)} reduce(bf16[8,48,8192]{2,1,0:T(8,128)(2,1)} %shard_map.103, bf16[]{:T(256)} %constant.5.clone.1), dimensions={0}, to_apply=%region_5.6 | reduce | flops 2752512 | bytes 7077890 | tf_op jit(solution)/shard_map/reduce_sum | solution.py:427
  (85 shorter events, 20.1 us)
Async XLA Ops:
  7.2 91.5 %all-gather.3.cloned.1.call-start = ((), (), s32[]{:S(2)}) async-start(), calls=%async_computation.4 | async-start | bytes 3538944 | tf_op jit(solution)/shard_map/all_gather | solution.py:376
  9.3 309.2 %reduce-scatter.5.cloned.1.call-start = ((), (), s32[]{:S(2)}) async-start(), calls=%async_computation.3 | async-start | bytes 8912896 | tf_op jit(solution)/shard_map/reduce_scatter | solution.py:411
  12.0 3.7 %copy-start = (bf16[1,2,128,4096]{3,2,1,0:T(8,128)(2,1)S(1)}, bf16[1,2,128,4096]{3,2,1,0:T(8,128)(2,1)}, u32[]{:S(2)}) copy-start(bf16[1,2,128,4096]{3,2,1,0:T(8,128)(2,1)} %param.11) | copy-start | bytes 6291460
  74.6 6.2 %copy-start.19 = (s32[2]{0:T(128)S(1)}, s32[2]{0:T(128)}, u32[]{:S(2)}) copy-start(s32[2]{0:T(128)} %param.12) | copy-start | bytes 28
  74.6 7.6 %copy-start.16 = (s32[2]{0:T(128)S(1)}, s32[2]{0:T(128)}, u32[]{:S(2)}) copy-start(s32[2]{0:T(128)} %param.13) | copy-start | bytes 28
  80.7 2.7 copy-start.10
  85.8 2.8 copy-start.5
  104.8 4.7 %copy-start.12 = (bf16[192,512]{1,0:T(8,128)(2,1)}, bf16[192,512]{1,0:T(8,128)(2,1)S(1)}, u32[]{:S(2)}) copy-start(bf16[192,512]{1,0:T(8,128)(2,1)S(1)} %convolution_convert_fusion.4) | copy-start | bytes 589828
  109.5 4.2 %copy-start.6 = (f32[4,8,128,192]{2,3,1,0:T(8,128)S(1)}, f32[4,8,128,192]{2,3,1,0:T(8,128)}, u32[]{:S(2)}) copy-start(f32[4,8,128,192]{2,3,1,0:T(8,128)} %get-tuple-element.27) | copy-start | bytes 9437188
  109.5 4.2 %copy-start.9 = (bf16[16,8,32,128]{3,2,1,0:T(8,128)(2,1)S(1)}, bf16[16,8,32,128]{3,2,1,0:T(8,128)(2,1)}, u32[]{:S(2)}) copy-start(bf16[16,8,32,128]{3,2,1,0:T(8,128)(2,1)} %copy.60) | copy-start | bytes 3145732
  109.5 4.2 %copy-start.20 = (pred[128]{0:T(512)(128)(4,1)S(1)}, pred[128]{0:T(512)(128)(4,1)}, u32[]{:S(2)}) copy-start(pred[128]{0:T(512)(128)(4,1)} %iota_compare_fusion.3) | copy-start | bytes 388
  115.5 5.3 %copy-start.14 = (bf16[1,192,512]{2,1,0:T(8,128)(2,1)S(1)}, bf16[1,192,512]{2,1,0:T(8,128)(2,1)}, u32[]{:S(2)}) copy-start(bf16[1,192,512]{2,1,0:T(8,128)(2,1)} %stack_reshape.6) | copy-start | bytes 589828
  115.5 5.3 %copy-start.15 = (bf16[1,192,512]{2,1,0:T(8,128)(2,1)S(1)}, bf16[1,192,512]{2,1,0:T(8,128)(2,1)}, u32[]{:S(2)}) copy-start(bf16[1,192,512]{2,1,0:T(8,128)(2,1)} %stack_reshape.7) | copy-start | bytes 589828
  115.5 5.3 %copy-start.2 = (bf16[1,8,24,8192]{3,2,1,0:T(8,128)(2,1)S(1)}, bf16[1,8,24,8192]{3,2,1,0:T(8,128)(2,1)}, u32[]{:S(2)}) copy-start(bf16[1,8,24,8192]{3,2,1,0:T(8,128)(2,1)} %shard_map.102) | copy-start | bytes 9437188
  115.5 5.3 %copy-start.18 = (bf16[1,192,8192]{2,1,0:T(8,128)(2,1)S(1)}, bf16[1,192,8192]{2,1,0:T(8,128)(2,1)}, u32[]{:S(2)}) copy-start(bf16[1,192,8192]{2,1,0:T(8,128)(2,1)} %all-gather.3.cloned.1.call-done) | copy-start | bytes 9437188
  127.6 190.9 %reduce-scatter.3.cloned.1.call-start = ((), (), s32[]{:S(2)}) async-start(), calls=%async_computation.2 | async-start | bytes 8912896 | tf_op jit(solution)/shard_map/reduce_scatter | solution.py:419
  127.8 2.2 copy-start.1
  130.1 2.6 copy-start.3
  132.7 5.3 %copy-start.17 = (s32[2]{0:T(128)S(1)}, s32[2]{0:T(128)}, u32[]{:S(2)}) copy-start(s32[2]{0:T(128)} %param.13) | copy-start | bytes 28
  148.5 14.7 %copy-start.4 = (bf16[1,8,24,8192]{3,2,1,0:T(8,128)(2,1)S(1)}, bf16[1,8,24,8192]{3,2,1,0:T(8,128)(2,1)}, u32[]{:S(2)}) copy-start(bf16[1,8,24,8192]{3,2,1,0:T(8,128)(2,1)} %shard_map.102) | copy-start | bytes 9437188
  162.5 0.7 copy-start.7
  171.9 0.9 copy-start.11
  171.9 1.1 copy-start.13
  171.9 1.3 copy-start.8
Sparse Core Ops, SparseCore 0:
  10.9 87.6 all-gather.2
  127.7 74.2 reduce-scatter.4
  205.0 99.4 reduce-scatter.2

commit v13 on v11

--- a/solution.py
+++ b/solution.py
@@ -274,12 +274,24 @@
     )(x)
 
 
-def image_kernel(n, tiles, g_ref, wk_ref, wv_ref, o_ref, buf, send_sems, recv_sems, local_sem):
+def image_kernel(n, tiles, g_ref, wk_hbm, wv_hbm, o_ref, buf, wk_ref, wv_ref, weight_sems,
+                 send_sems, recv_sems, local_sem):
     me = lax.axis_index("section")
     row = lax.axis_index("dp")
     rows = g_ref.shape[0] // n
     half = g_ref.shape[1] // 2
     tile_w = wk_ref.shape[0] // tiles
+
+    def weight_copies(t):
+        part = pl.ds(pl.multiple_of(t * tile_w, tile_w), tile_w)
+        return [
+            pltpu.make_async_copy(src.at[part], dst.at[part], weight_sems.at[i, t])
+            for i, (src, dst) in enumerate(((wk_hbm, wk_ref), (wv_hbm, wv_ref)))
+        ]
+
+    for t in range(tiles):
+        for copy in weight_copies(t):
+            copy.start()
     barrier = pltpu.get_barrier_semaphore()
     for k in range(1, n):
         pl.semaphore_signal(
@@ -288,6 +300,8 @@
     pl.semaphore_wait(barrier, n - 1)
 
     def compute(t):
+        for copy in weight_copies(t):
+            copy.wait()
         cols = pl.ds(pl.multiple_of(t * tile_w, tile_w), tile_w)
         dims = (((1,), (1,)), ((), ()))
         acc = lax.dot_general(
@@ -345,10 +359,17 @@
     return pl.pallas_call(
         functools.partial(image_kernel, n, tiles),
         out_shape=jax.ShapeDtypeStruct((n, total_rows // n, width), jnp.bfloat16),
-        in_specs=[pl.BlockSpec(memory_space=pltpu.VMEM)] * 3,
+        in_specs=[
+            pl.BlockSpec(memory_space=pltpu.VMEM),
+            pl.BlockSpec(memory_space=pl.ANY),
+            pl.BlockSpec(memory_space=pl.ANY),
+        ],
         out_specs=pl.BlockSpec(memory_space=pl.ANY),
         scratch_shapes=[
             pltpu.VMEM((total_rows, width), jnp.bfloat16),
+            pltpu.VMEM(w_key.shape, w_key.dtype),
+            pltpu.VMEM(w_value.shape, w_value.dtype),
+            pltpu.SemaphoreType.DMA((2, tiles)),
             pltpu.SemaphoreType.DMA((n,)),
             pltpu.SemaphoreType.DMA((n,)),
             pltpu.SemaphoreType.DMA(()),

time: 315 us -> 314 us (level)
  no operation moved by 1% of the time
where the time goes in v13:
time: 314 us; the launch traced here: 312 us
  Pallas kernels  180 us (57%)
  matrix products  71.5 us (23%)
  local copies, waits for them, and re-layouts  19 us (6%)
  waiting for transfers between devices  17.7 us (6%)
  between operations  14 us (4%)
  other arithmetic  9.16 us (3%)
    pallas_call x1, Pallas kernels, image_exchange(): pl.pallas_call(functools.partial(image_kernel, n, tiles), out_shape=jax.S...  125 us
    pallas_call x1, Pallas kernels, relay_gather(): pl.pallas_call(relay_gather_kernel, out_shape=jax.ShapeDtypeStruct((sampl...  55.3 us
    all_gather x1, waiting for transfers between devices, shards(): lax.all_gather(image_tokens[i], 'section', axis=0, tiled=True)  17.7 us
    unnamed x25, local copies, waits for them, and re-layouts  13.8 us
    dot_general x1, matrix products, attend_back(): jnp.einsum('hgln,lhgd->nhd', score_grad, heads_of_queries, preferred_elem...  12.7 us
    dot_general x2, matrix products, shards(): jnp.dot(tokens, w_value, preferred_element_type=jnp.float32)  12.7 us
    dot_general x2, matrix products, shards(): jnp.dot(tokens, w_key, preferred_element_type=jnp.float32)  12.3 us
    dot_general x1, matrix products, attend_back(): jnp.einsum('hgln,nhd->lhgd', score_grad, heads_of_keys, preferred_element...  10.6 us
  transfers between devices with their start and end apart: 3, of which 1 were waited for; matrix products, arithmetic and copies ran while one was open for 23% of the time, Pallas kernels for 58%

profile of v13, /device:TPU:38, one launch (start us, length us, event | category | flops | bytes accessed | tf_op | source)
XLA Modules:
  0.0 312.0 jit_solution(10141406248628549637)
XLA Ops:
  7.2 2.0 fusion.67
  9.3 3.4 %copy.36 = bf16[32,8,32,128]{3,2,1,0:T(8,128)(2,1)} copy(bf16[32,8,32,128]{3,1,2,0:T(8,128)(2,1)} %bitcast.136) | data formatting | bytes 4194304
  12.7 2.1 copy.37
  14.8 55.3 %shard_map.102 = bf16[1,8,24,8192]{3,2,1,0:T(8,128)(2,1)} custom-call(bf16[1,24,8192]{2,1,0:T(8,128)(2,1)} %get-tuple-element.16.x_ref), custom_call_target="tpu_custom_call" | custom-call | tf_op jit(solution)/shard_map/pallas_call | solution.py:239
  70.1 6.2 %convolution_convert_fusion.5 = bf16[192,512]{1,0:T(8,128)(2,1)S(1)} fusion(bf16[192,8192]{1,0:T(8,128)(2,1)} %bitcast.132, bf16[1,8192,512]{2,1,0:T(8,128)(2,1)} %param.9), kind=kOutput, calls=%fused_computation.39 | convolution fusion | flops 1610711040 | bytes 11730944 | tf_op jit(solution)/shard_map/dot_general | solution.py:410
  76.5 17.7 %all-gather.3.cloned.1.call-done = bf16[1,192,8192]{2,1,0:T(8,128)(2,1)} async-done(((bf16[1,24,8192]{2,1,0:T(8,128)(2,1)}), bf16[1,192,8192]{2,1,0:T(8,128)(2,1)}) %all-gather.3.cloned.1.call-update) | async-done | bytes 3145744 | tf_op jit(solution)/shard_map/all_gather | solution.py:397
  94.2 6.1 %convolution_convert_fusion.4 = bf16[192,512]{1,0:T(8,128)(2,1)S(1)} fusion(bf16[1,192,8192]{2,1,0:T(8,128)(2,1)} %all-gather.3.cloned.1.call-done, bf16[1,8192,512]{2,1,0:T(8,128)(2,1)} %param.9), kind=kOutput, calls=%fused_computation.38 | convolution fusion | flops 1610711040 | bytes 11730944 | tf_op jit(solution)/shard_map/dot_general | solution.py:410
  101.1 2.6 fusion.19
  103.7 2.7 fusion.68
  106.4 1.4 broadcast_divide_fusion
  107.9 3.2 %copy-done = f32[2,4,8,128,192]{3,4,2,1,0:T(8,128)} copy-done((f32[2,4,8,128,192]{3,4,2,1,0:T(8,128)}, f32[2,4,8,128,192]{3,4,2,1,0:T(8,128)S(1)}, u32[]{:S(2)}) %copy-start) | copy-done | bytes 6291480
  111.0 1.4 fusion.37
  113.0 6.7 %convolution_convert_fusion.1 = bf16[8192,512]{1,0:T(8,128)(2,1)} fusion(bf16[192,8192]{1,0:T(8,128)(2,1)S(1)} %bitcast.143, bf16[192,8192]{1,0:T(8,128)(2,1)S(1)} %bitcast.134, bf16[48,8,4,128]{3,2,1,0:T(4,128)(2,1)S(1)} %bitcast.139), kind=kOutput, calls=%fused_computation.3 | convolution fusion | flops 3238002688 | bytes 15073280 | tf_op jit(solution)/shard_map/td,tk->dk/dot_general | solution.py:422
  120.0 6.1 %convolution_convert_fusion.3 = bf16[192,512]{1,0:T(8,128)(2,1)S(1)} fusion(bf16[192,8192]{1,0:T(8,128)(2,1)} %bitcast.133, bf16[1,8192,512]{2,1,0:T(8,128)(2,1)} %param.10), kind=kOutput, calls=%fused_computation.37 | convolution fusion | flops 1610711040 | bytes 11730944 | tf_op jit(solution)/shard_map/dot_general | solution.py:413
  126.2 6.5 %convolution_convert_fusion.2 = bf16[192,512]{1,0:T(8,128)(2,1)S(1)} fusion(bf16[1,8192,512]{2,1,0:T(8,128)(2,1)} %param.10, bf16[1,192,8192]{2,1,0:T(8,128)(2,1)} %all-gather.3.cloned.1.call-done), kind=kOutput, calls=%fused_computation.36 | convolution fusion | flops 1610711040 | bytes 11730944 | tf_op jit(solution)/shard_map/dot_general | solution.py:413
  132.8 3.7 %fusion.21 = f32[2,4,192,128,8]{3,2,4,1,0:T(8,128)} fusion(bf16[2,128,4,8,128]{4,3,2,1,0:T(8,128)(2,1)S(1)} %bitcast.126, pred[2,128]{1,0:T(4,128)(4,1)S(1)} %iota_compare_fusion.1, bf16[1,192,4,128]{3,1,2,0:T(8,128)(2,1)S(1)} %copy.25, bf16[1,192,4,128]{3,1,2,0:T(8,128)(2,1)S(1)} %copy.24), kind=kOutput, calls=%fused_computation.29 | convolution fusion | flops 404488192 | bytes 8782080 | tf_op jit(solution)/shard_map/vmap(lhgd,nhd->hgln)/dot_general | solution.py:101
  136.6 12.7 %fusion.34 = bf16[2,192,4,128]{3,1,2,0:T(8,128)(2,1)} fusion(bf16[2,128,4,8,128]{4,3,2,1,0:T(8,128)(2,1)} %bitcast.130, f32[2,4,8,128,192]{3,4,2,1,0:T(8,128)} %copy-done, f32[2,4,192,128,8]{3,2,4,1,0:T(8,128)} %fusion.21), kind=kOutput, calls=%fused_computation.34 | convolution fusion | flops 410722496 | bytes 15073280 | tf_op jit(solution)/shard_map/vmap(hgln,lhgd->nhd)/dot_general | solution.py:109
  149.3 1.3 copy.27
  151.4 8.8 %convolution_convert_fusion = bf16[8192,512]{1,0:T(8,128)(2,1)} fusion(bf16[192,8192]{1,0:T(8,128)(2,1)} %bitcast.142, bf16[192,8192]{1,0:T(8,128)(2,1)S(1)} %bitcast.135, bf16[48,8,4,128]{3,2,1,0:T(4,128)(2,1)S(1)} %bitcast.140), kind=kOutput, calls=%fused_computation.2 | convolution fusion | flops 3238002688 | bytes 15073280 | tf_op jit(solution)/shard_map/td,tk->dk/dot_general | solution.py:431
  161.3 10.6 %fusion.17 = bf16[2,4,128,8,128]{4,2,3,1,0:T(8,128)(2,1)S(1)} fusion(f32[2,4,8,128,192]{3,4,2,1,0:T(8,128)} %copy-done, f32[2,4,192,128,8]{3,2,4,1,0:T(8,128)} %fusion.21, bf16[1,192,4,128]{3,1,2,0:T(8,128)(2,1)} %copy-done.7, bf16[1,192,4,128]{3,1,2,0:T(8,128)(2,1)S(1)} %copy-done.6), kind=kOutput, calls=%fused_computation.25 | convolution fusion | flops 412360896 | bytes 15073280 | tf_op jit(solution)/shard_map/vmap(hgln,nhd->lhgd)/dot_general | solution.py:106
  171.9 2.7 copy.31
  174.7 1.0 copy.29
  175.6 125.0 %shard_map.103 = bf16[8,48,8192]{2,1,0:T(8,128)(2,1)} custom-call(bf16[384,1024]{1,0:T(8,128)(2,1)} %bitcast.131, bf16[8192,512]{1,0:T(8,128)(2,1)} %bitcast.127, bf16[8192,512]{1,0:T(8,128)(2,1)} %bitcast.128), custom_call_target="tpu_custom_call" | custom-call | flops 6442450944 | bytes 23068672 | tf_op jit(solution)/shard_map/pallas_call | solution.py:359
  300.7 4.8 %reduce_sum.32 = bf16[48,8192]{1,0:T(8,128)(2,1)} reduce(bf16[8,48,8192]{2,1,0:T(8,128)(2,1)} %shard_map.103, bf16[]{:T(256)} %constant.1.clone.1), dimensions={0}, to_apply=%region_3.4 | reduce | flops 2752512 | bytes 7077890 | tf_op jit(solution)/shard_map/reduce_sum | solution.py:443
  (44 shorter events, 3.9 us)
Async XLA Ops:
  7.2 87.0 %all-gather.3.cloned.1.call-start = ((), (), s32[]{:S(2)}) async-start(), calls=%async_computation.4 | async-start | bytes 3538944 | tf_op jit(solution)/shard_map/all_gather | solution.py:397
  9.3 296.2 %reduce-scatter.5.cloned.1.call-start = ((), (), s32[]{:S(2)}) async-start(), calls=%async_computation.3 | async-start | bytes 8912896 | tf_op jit(solution)/shard_map/reduce_scatter | solution.py:427
  70.1 6.3 %copy-start.9 = (s32[2]{0:T(128)S(1)}, s32[2]{0:T(128)}, u32[]{:S(2)}) copy-start(s32[2]{0:T(128)} %param.13) | copy-start | bytes 28
  70.1 6.4 %copy-start.10 = (s32[2]{0:T(128)S(1)}, s32[2]{0:T(128)}, u32[]{:S(2)}) copy-start(s32[2]{0:T(128)} %param.12) | copy-start | bytes 28
  76.4 24.1 %copy-start.5 = (bf16[1,192,4,128]{3,1,2,0:T(8,128)(2,1)}, bf16[1,192,4,128]{3,1,2,0:T(8,128)(2,1)S(1)}, u32[]{:S(2)}) copy-start(bf16[1,192,4,128]{3,1,2,0:T(8,128)(2,1)S(1)} %copy.19) | copy-start | bytes 589828
  100.4 0.7 copy-start.7
  107.8 3.2 %copy-start = (f32[2,4,8,128,192]{3,4,2,1,0:T(8,128)}, f32[2,4,8,128,192]{3,4,2,1,0:T(8,128)S(1)}, u32[]{:S(2)}) copy-start(f32[2,4,8,128,192]{3,4,2,1,0:T(8,128)S(1)} %broadcast_divide_fusion) | copy-start | bytes 18874372
  107.9 4.9 %copy-start.1 = (bf16[1,8,24,8192]{3,2,1,0:T(8,128)(2,1)S(1)}, bf16[1,8,24,8192]{3,2,1,0:T(8,128)(2,1)}, u32[]{:S(2)}) copy-start(bf16[1,8,24,8192]{3,2,1,0:T(8,128)(2,1)} %shard_map.102) | copy-start | bytes 9437188
  107.9 5.1 %copy-start.8 = (bf16[1,192,8192]{2,1,0:T(8,128)(2,1)S(1)}, bf16[1,192,8192]{2,1,0:T(8,128)(2,1)}, u32[]{:S(2)}) copy-start(bf16[1,192,8192]{2,1,0:T(8,128)(2,1)} %all-gather.3.cloned.1.call-done) | copy-start | bytes 9437188
  119.7 185.8 %reduce-scatter.3.cloned.1.call-start = ((), (), s32[]{:S(2)}) async-start(), calls=%async_computation.2 | async-start | bytes 8912896 | tf_op jit(solution)/shard_map/reduce_scatter | solution.py:435
  136.6 14.8 %copy-start.2 = (bf16[1,8,24,8192]{3,2,1,0:T(8,128)(2,1)S(1)}, bf16[1,8,24,8192]{3,2,1,0:T(8,128)(2,1)}, u32[]{:S(2)}) copy-start(bf16[1,8,24,8192]{3,2,1,0:T(8,128)(2,1)} %shard_map.102) | copy-start | bytes 9437188
  150.6 0.7 copy-start.3
  160.1 1.0 copy-start.4
  160.1 1.2 copy-start.6
Sparse Core Ops, SparseCore 0:
  10.9 83.2 all-gather.2
  119.9 78.3 reduce-scatter.4
  201.3 93.0 reduce-scatter.2

commit v14 on v13

--- a/solution.py
+++ b/solution.py
@@ -274,8 +274,8 @@
     )(x)
 
 
-def image_kernel(n, tiles, g_ref, wk_hbm, wv_hbm, o_ref, buf, wk_ref, wv_ref, weight_sems,
-                 send_sems, recv_sems, local_sem):
+def image_kernel(n, tiles, g_ref, wk_hbm, wv_hbm, o_ref, buf, recv, acc, wk_ref, wv_ref,
+                 weight_sems, send_sems, recv_sems):
     me = lax.axis_index("section")
     row = lax.axis_index("dp")
     rows = g_ref.shape[0] // n
@@ -318,7 +318,7 @@
             peer = lax.rem(me + k, n)
             pltpu.make_async_remote_copy(
                 src_ref=buf.at[pl.ds(pl.multiple_of(peer * rows, 16), rows), cols],
-                dst_ref=o_ref.at[me, :, cols],
+                dst_ref=recv.at[me, :, cols],
                 send_sem=send_sems.at[k],
                 recv_sem=recv_sems.at[k],
                 device_id=(peer, row),
@@ -335,21 +335,21 @@
     lax.fori_loop(1, tiles, body, 0)
     send(tiles - 1)
     own = pl.ds(pl.multiple_of(me * rows, 16), rows)
-    local = pltpu.make_async_copy(buf.at[own, :], o_ref.at[me], local_sem)
-    local.start()
+    acc[...] = buf[own, :].astype(jnp.float32)
     for k in range(1, n):
         peer = lax.rem(me + k, n)
         whole = pltpu.make_async_remote_copy(
             src_ref=buf.at[pl.ds(pl.multiple_of(peer * rows, 16), rows), :],
-            dst_ref=o_ref.at[me],
+            dst_ref=recv.at[me],
             send_sem=send_sems.at[k],
             recv_sem=recv_sems.at[k],
             device_id=(peer, row),
             device_id_type=MESH_ID,
         )
+        whole.wait_recv()
+        acc[...] += recv[lax.rem(me + n - k, n)].astype(jnp.float32)
         whole.wait_send()
-        whole.wait_recv()
-    local.wait()
+    o_ref[...] = acc[...].astype(o_ref.dtype)
 
 
 def image_exchange(g, w_key, w_value, n):
@@ -358,21 +358,22 @@
     tiles = 8
     return pl.pallas_call(
         functools.partial(image_kernel, n, tiles),
-        out_shape=jax.ShapeDtypeStruct((n, total_rows // n, width), jnp.bfloat16),
+        out_shape=jax.ShapeDtypeStruct((total_rows // n, width), jnp.bfloat16),
         in_specs=[
             pl.BlockSpec(memory_space=pltpu.VMEM),
             pl.BlockSpec(memory_space=pl.ANY),
             pl.BlockSpec(memory_space=pl.ANY),
         ],
-        out_specs=pl.BlockSpec(memory_space=pl.ANY),
+        out_specs=pl.BlockSpec(memory_space=pltpu.VMEM),
         scratch_shapes=[
             pltpu.VMEM((total_rows, width), jnp.bfloat16),
+            pltpu.VMEM((n, total_rows // n, width), jnp.bfloat16),
+            pltpu.VMEM((total_rows // n, width), jnp.float32),
             pltpu.VMEM(w_key.shape, w_key.dtype),
             pltpu.VMEM(w_value.shape, w_value.dtype),
             pltpu.SemaphoreType.DMA((2, tiles)),
             pltpu.SemaphoreType.DMA((n,)),
             pltpu.SemaphoreType.DMA((n,)),
-            pltpu.SemaphoreType.DMA(()),
         ],
         compiler_params=pltpu.CompilerParams(
             collective_id=3, has_side_effects=True, vmem_limit_bytes=60 * 1024 * 1024
@@ -439,11 +440,7 @@
     received = image_exchange(
         by_slot.reshape(n_section * samples_here * chunk, -1), w_key, w_value, n_section
     )
-    image_out = (
-        jnp.sum(received.astype(jnp.float32), axis=0)
-        .reshape(samples_here, chunk, model_width)
-        .astype(jnp.bfloat16)
-    )
+    image_out = received.reshape(samples_here, chunk, model_width)
     return (
         query_out,
         image_out,

time: 314 us -> 312 us (level)
  other arithmetic: 9.16 us -> 4.34 us
    reduce_sum x1 -> x0, other arithmetic: 4.82 us -> none  [shards(): jnp.sum(received.astype(jnp.float32), axis=0)]
    unnamed x25 -> x26, local copies, waits for them, and re-layouts: 13.8 us -> 15.2 us
  transfers between devices with their start and end apart: 3 -> 3, of which waited for: 1 -> 1; matrix products, arithmetic and copies ran while one was open for 23% -> 21% of each run, Pallas kernels for 58% -> 59%
where the time goes in v14:
time: 312 us; the launch traced here: 311 us
  Pallas kernels  182 us (58%)
  matrix products  71.6 us (23%)
  local copies, waits for them, and re-layouts  20.4 us (7%)
  waiting for transfers between devices  17.7 us (6%)
  between operations  14 us (4%)
  other arithmetic  4.34 us (1%)
    pallas_call x1, Pallas kernels, image_exchange(): pl.pallas_call(functools.partial(image_kernel, n, tiles), out_shape=jax.S...  127 us
    pallas_call x1, Pallas kernels, relay_gather(): pl.pallas_call(relay_gather_kernel, out_shape=jax.ShapeDtypeStruct((sampl...  55.3 us
    all_gather x1, waiting for transfers between devices, shards(): lax.all_gather(image_tokens[i], 'section', axis=0, tiled=True)  17.7 us
    unnamed x26, local copies, waits for them, and re-layouts  15.2 us
    dot_general x1, matrix products, attend_back(): jnp.einsum('hgln,lhgd->nhd', score_grad, heads_of_queries, preferred_elem...  12.7 us
    dot_general x2, matrix products, shards(): jnp.dot(tokens, w_value, preferred_element_type=jnp.float32)  12.6 us
    dot_general x2, matrix products, shards(): jnp.dot(tokens, w_key, preferred_element_type=jnp.float32)  12.3 us
    dot_general x1, matrix products, attend_back(): jnp.einsum('hgln,nhd->lhgd', score_grad, heads_of_keys, preferred_element...  10.6 us
  transfers between devices with their start and end apart: 3, of which 1 were waited for; matrix products, arithmetic and copies ran while one was open for 21% of the time, Pallas kernels for 59%

profile of v14, /device:TPU:38, one launch (start us, length us, event | category | flops | bytes accessed | tf_op | source)
XLA Modules:
  0.0 310.6 jit_solution(12383706921803851136)
XLA Ops:
  7.2 2.0 fusion.67
  9.3 3.4 %copy.36 = bf16[32,8,32,128]{3,2,1,0:T(8,128)(2,1)} copy(bf16[32,8,32,128]{3,1,2,0:T(8,128)(2,1)} %bitcast.133) | data formatting | bytes 4194304
  12.7 2.1 copy.37
  14.8 55.3 %shard_map.102 = bf16[1,8,24,8192]{3,2,1,0:T(8,128)(2,1)} custom-call(bf16[1,24,8192]{2,1,0:T(8,128)(2,1)} %get-tuple-element.16.x_ref), custom_call_target="tpu_custom_call" | custom-call | tf_op jit(solution)/shard_map/pallas_call | solution.py:239
  70.1 6.2 %convolution_convert_fusion.5 = bf16[192,512]{1,0:T(8,128)(2,1)S(1)} fusion(bf16[192,8192]{1,0:T(8,128)(2,1)} %bitcast.129, bf16[1,8192,512]{2,1,0:T(8,128)(2,1)} %param.9), kind=kOutput, calls=%fused_computation.39 | convolution fusion | flops 1610711040 | bytes 11730944 | tf_op jit(solution)/shard_map/dot_general | solution.py:411
  76.5 17.7 %all-gather.3.cloned.1.call-done = bf16[1,192,8192]{2,1,0:T(8,128)(2,1)} async-done(((bf16[1,24,8192]{2,1,0:T(8,128)(2,1)}), bf16[1,192,8192]{2,1,0:T(8,128)(2,1)}) %all-gather.3.cloned.1.call-update) | async-done | bytes 3145744 | tf_op jit(solution)/shard_map/all_gather | solution.py:398
  94.2 6.1 %convolution_convert_fusion.4 = bf16[192,512]{1,0:T(8,128)(2,1)S(1)} fusion(bf16[1,192,8192]{2,1,0:T(8,128)(2,1)} %all-gather.3.cloned.1.call-done, bf16[1,8192,512]{2,1,0:T(8,128)(2,1)} %param.9), kind=kOutput, calls=%fused_computation.38 | convolution fusion | flops 1610711040 | bytes 11730944 | tf_op jit(solution)/shard_map/dot_general | solution.py:411
  100.5 2.7 fusion.19
  103.2 2.7 fusion.68
  105.9 1.4 broadcast_divide_fusion
  107.3 3.2 %copy-done = f32[2,4,8,128,192]{3,4,2,1,0:T(8,128)} copy-done((f32[2,4,8,128,192]{3,4,2,1,0:T(8,128)}, f32[2,4,8,128,192]{3,4,2,1,0:T(8,128)S(1)}, u32[]{:S(2)}) %copy-start) | copy-done | bytes 6291480
  110.5 1.4 fusion.37
  112.4 6.7 %convolution_convert_fusion.1 = bf16[8192,512]{1,0:T(8,128)(2,1)} fusion(bf16[192,8192]{1,0:T(8,128)(2,1)S(1)} %bitcast.143, bf16[192,8192]{1,0:T(8,128)(2,1)S(1)} %bitcast.131, bf16[48,8,4,128]{3,2,1,0:T(4,128)(2,1)S(1)} %bitcast.136), kind=kOutput, calls=%fused_computation.3 | convolution fusion | flops 3238002688 | bytes 15073280 | tf_op jit(solution)/shard_map/td,tk->dk/dot_general | solution.py:423
  119.4 6.1 %convolution_convert_fusion.3 = bf16[192,512]{1,0:T(8,128)(2,1)S(1)} fusion(bf16[192,8192]{1,0:T(8,128)(2,1)} %bitcast.130, bf16[1,8192,512]{2,1,0:T(8,128)(2,1)} %param.10), kind=kOutput, calls=%fused_computation.37 | convolution fusion | flops 1610711040 | bytes 11730944 | tf_op jit(solution)/shard_map/dot_general | solution.py:414
  125.6 6.5 %convolution_convert_fusion.2 = bf16[192,512]{1,0:T(8,128)(2,1)S(1)} fusion(bf16[1,8192,512]{2,1,0:T(8,128)(2,1)} %param.10, bf16[1,192,8192]{2,1,0:T(8,128)(2,1)} %all-gather.3.cloned.1.call-done), kind=kOutput, calls=%fused_computation.36 | convolution fusion | flops 1610711040 | bytes 11730944 | tf_op jit(solution)/shard_map/dot_general | solution.py:414
  132.2 3.7 %fusion.21 = f32[2,4,192,128,8]{3,2,4,1,0:T(8,128)} fusion(bf16[2,128,4,8,128]{4,3,2,1,0:T(8,128)(2,1)S(1)} %bitcast.126, pred[2,128]{1,0:T(4,128)(4,1)S(1)} %iota_compare_fusion.1, bf16[1,192,4,128]{3,1,2,0:T(8,128)(2,1)S(1)} %copy.25, bf16[1,192,4,128]{3,1,2,0:T(8,128)(2,1)S(1)} %copy.24), kind=kOutput, calls=%fused_computation.29 | convolution fusion | flops 404488192 | bytes 8782080 | tf_op jit(solution)/shard_map/vmap(lhgd,nhd->hgln)/dot_general | solution.py:101
  136.0 12.7 %fusion.34 = bf16[2,192,4,128]{3,1,2,0:T(8,128)(2,1)} fusion(bf16[2,128,4,8,128]{4,3,2,1,0:T(8,128)(2,1)} %bitcast.128, f32[2,4,8,128,192]{3,4,2,1,0:T(8,128)} %copy-done, f32[2,4,192,128,8]{3,2,4,1,0:T(8,128)} %fusion.21), kind=kOutput, calls=%fused_computation.34 | convolution fusion | flops 410722496 | bytes 15073280 | tf_op jit(solution)/shard_map/vmap(hgln,lhgd->nhd)/dot_general | solution.py:109
  148.7 1.3 copy.27
  150.8 8.7 %convolution_convert_fusion = bf16[8192,512]{1,0:T(8,128)(2,1)} fusion(bf16[192,8192]{1,0:T(8,128)(2,1)} %bitcast.142, bf16[192,8192]{1,0:T(8,128)(2,1)S(1)} %bitcast.132, bf16[48,8,4,128]{3,2,1,0:T(4,128)(2,1)S(1)} %bitcast.137), kind=kOutput, calls=%fused_computation.2 | convolution fusion | flops 3238002688 | bytes 15073280 | tf_op jit(solution)/shard_map/td,tk->dk/dot_general | solution.py:432
  160.7 10.6 %fusion.17 = bf16[2,4,128,8,128]{4,2,3,1,0:T(8,128)(2,1)S(1)} fusion(f32[2,4,8,128,192]{3,4,2,1,0:T(8,128)} %copy-done, f32[2,4,192,128,8]{3,2,4,1,0:T(8,128)} %fusion.21, bf16[1,192,4,128]{3,1,2,0:T(8,128)(2,1)} %copy-done.7, bf16[1,192,4,128]{3,1,2,0:T(8,128)(2,1)S(1)} %copy-done.6), kind=kOutput, calls=%fused_computation.25 | convolution fusion | flops 412360896 | bytes 15073280 | tf_op jit(solution)/shard_map/vmap(hgln,nhd->lhgd)/dot_general | solution.py:106
  171.3 2.7 copy.31
  174.1 1.0 copy.29
  175.0 126.9 %shard_map.103 = bf16[48,8192]{1,0:T(8,128)(2,1)} custom-call(bf16[384,1024]{1,0:T(8,128)(2,1)} %bitcast.139, bf16[8192,512]{1,0:T(8,128)(2,1)} %bitcast.140, bf16[8192,512]{1,0:T(8,128)(2,1)} %bitcast.141), custom_call_target="tpu_custom_call" | custom-call | flops 6442450944 | bytes 23068672 | tf_op jit(solution)/shard_map/pallas_call | solution.py:359
  302.0 2.1 copy.68
  (44 shorter events, 3.3 us)
Async XLA Ops:
  7.2 87.0 %all-gather.3.cloned.1.call-start = ((), (), s32[]{:S(2)}) async-start(), calls=%async_computation.4 | async-start | bytes 3538944 | tf_op jit(solution)/shard_map/all_gather | solution.py:398
  9.3 292.7 %reduce-scatter.5.cloned.1.call-start = ((), (), s32[]{:S(2)}) async-start(), calls=%async_computation.3 | async-start | bytes 8912896 | tf_op jit(solution)/shard_map/reduce_scatter | solution.py:428
  70.1 6.3 %copy-start.9 = (s32[2]{0:T(128)S(1)}, s32[2]{0:T(128)}, u32[]{:S(2)}) copy-start(s32[2]{0:T(128)} %param.13) | copy-start | bytes 28
  70.1 6.4 %copy-start.10 = (s32[2]{0:T(128)S(1)}, s32[2]{0:T(128)}, u32[]{:S(2)}) copy-start(s32[2]{0:T(128)} %param.12) | copy-start | bytes 28
  76.4 24.1 %copy-start.5 = (bf16[1,192,4,128]{3,1,2,0:T(8,128)(2,1)}, bf16[1,192,4,128]{3,1,2,0:T(8,128)(2,1)S(1)}, u32[]{:S(2)}) copy-start(bf16[1,192,4,128]{3,1,2,0:T(8,128)(2,1)S(1)} %copy.19) | copy-start | bytes 589828
  100.4 5.4 %copy-start.7 = (bf16[1,192,4,128]{3,1,2,0:T(8,128)(2,1)}, bf16[1,192,4,128]{3,1,2,0:T(8,128)(2,1)S(1)}, u32[]{:S(2)}) copy-start(bf16[1,192,4,128]{3,1,2,0:T(8,128)(2,1)S(1)} %copy.20) | copy-start | bytes 589828
  107.3 3.2 %copy-start = (f32[2,4,8,128,192]{3,4,2,1,0:T(8,128)}, f32[2,4,8,128,192]{3,4,2,1,0:T(8,128)S(1)}, u32[]{:S(2)}) copy-start(f32[2,4,8,128,192]{3,4,2,1,0:T(8,128)S(1)} %broadcast_divide_fusion) | copy-start | bytes 18874372
  107.3 4.9 %copy-start.1 = (bf16[1,8,24,8192]{3,2,1,0:T(8,128)(2,1)S(1)}, bf16[1,8,24,8192]{3,2,1,0:T(8,128)(2,1)}, u32[]{:S(2)}) copy-start(bf16[1,8,24,8192]{3,2,1,0:T(8,128)(2,1)} %shard_map.102) | copy-start | bytes 9437188
  107.3 5.1 %copy-start.8 = (bf16[1,192,8192]{2,1,0:T(8,128)(2,1)S(1)}, bf16[1,192,8192]{2,1,0:T(8,128)(2,1)}, u32[]{:S(2)}) copy-start(bf16[1,192,8192]{2,1,0:T(8,128)(2,1)} %all-gather.3.cloned.1.call-done) | copy-start | bytes 9437188
  119.2 182.9 %reduce-scatter.3.cloned.1.call-start = ((), (), s32[]{:S(2)}) async-start(), calls=%async_computation.2 | async-start | bytes 8912896 | tf_op jit(solution)/shard_map/reduce_scatter | solution.py:436
  136.0 14.8 %copy-start.2 = (bf16[1,8,24,8192]{3,2,1,0:T(8,128)(2,1)S(1)}, bf16[1,8,24,8192]{3,2,1,0:T(8,128)(2,1)}, u32[]{:S(2)}) copy-start(bf16[1,8,24,8192]{3,2,1,0:T(8,128)(2,1)} %shard_map.102) | copy-start | bytes 9437188
  150.0 0.7 copy-start.3
  159.5 1.0 copy-start.4
  159.5 1.2 copy-start.6
Sparse Core Ops, SparseCore 0:
  10.9 83.2 all-gather.2
  119.3 78.3 reduce-scatter.4
  200.7 93.1 reduce-scatter.2

commit v15 on v14

--- a/solution.py
+++ b/solution.py
@@ -402,6 +402,7 @@
         first = relay_gather(image_tokens[:1], n_section)
     else:
         first = exchange(image_tokens[:1], n_section, False, 0)
+    first, query_local, cotan_local = lax.optimization_barrier((first, query_local, cotan_local))
     token_list = [first.reshape(image_len, model_width)] + late
     keys_list = []
     values_list = []

time: 312 us -> 318 us (1.019)
  local copies, waits for them, and re-layouts: 20.4 us -> 33.7 us
  matrix products: 71.6 us -> 59.7 us
  other arithmetic: 4.34 us -> 7.96 us
    convert_element_type x0 -> x2, local copies, waits for them, and re-layouts: none -> 15.5 us  [the longest x1 7.85 us: attend_back(): (weights * (prob_grad - row_dot) * scaling).astype(jnp.bfloat16)]
    dot_general x1, matrix products: 12.7 us -> 3.73 us  [attend_back(): jnp.einsum('hgln,lhgd->nhd', score_grad, heads_of_queries, preferred_elem...]
    sub x0 -> x1, matrix products: none -> 8.76 us  [attend_back(): prob_grad - row_dot]
    dot_general x1, matrix products: 10.6 us -> 2.09 us  [attend_back(): jnp.einsum('hgln,nhd->lhgd', score_grad, heads_of_keys, preferred_element...]
    unnamed x26 -> x32, local copies, waits for them, and re-layouts: 15.2 us -> 10.3 us
    convert_element_type x0 -> x1, other arithmetic: none -> 4.81 us  [attend_front(): weights_low = weights.astype(jnp.bfloat16)]
    pallas_call x1, Pallas kernels: 55.3 us -> 51.1 us  [relay_gather(): pl.pallas_call(relay_gather_kernel, out_shape=jax.ShapeDtypeStruct((sampl...]
    dot_general x1 -> x0, matrix products: 3.73 us -> none  [attend_back(): jnp.einsum('lhgd,nhd->hgln', head_gradient, heads_of_values, preferred_el...]
  transfers between devices with their start and end apart: 3 -> 3, of which waited for: 1 -> 1; matrix products, arithmetic and copies ran while one was open for 21% -> 19% of each run, Pallas kernels for 59% -> 57%
where the time goes in v15:
time: 318 us; the launch traced here: 315 us
  Pallas kernels  179 us (56%)
  matrix products  59.7 us (19%)
  local copies, waits for them, and re-layouts  33.7 us (11%)
  waiting for transfers between devices  20.5 us (6%)
  between operations  14 us (4%)
  other arithmetic  7.96 us (3%)
    pallas_call x1, Pallas kernels, image_exchange(): pl.pallas_call(functools.partial(image_kernel, n, tiles), out_shape=jax.S...  128 us
    pallas_call x1, Pallas kernels, relay_gather(): pl.pallas_call(relay_gather_kernel, out_shape=jax.ShapeDtypeStruct((sampl...  51.1 us
    all_gather x1, waiting for transfers between devices, shards(): lax.all_gather(image_tokens[i], 'section', axis=0, tiled=True)  20.4 us
    dot_general x2, matrix products, shards(): jnp.dot(tokens, w_key, preferred_element_type=jnp.float32)  12.8 us
    dot_general x2, matrix products, shards(): jnp.dot(tokens, w_value, preferred_element_type=jnp.float32)  12.7 us
    unnamed x32, local copies, waits for them, and re-layouts  10.3 us
    sub x1, matrix products, attend_back(): prob_grad - row_dot  8.76 us
    convert_element_type x1, local copies, waits for them, and re-layouts, attend_back(): (weights * (prob_grad - row_dot) * scaling).astype(jnp.bfloat16)  7.85 us
  transfers between devices with their start and end apart: 3, of which 1 were waited for; matrix products, arithmetic and copies ran while one was open for 19% of the time, Pallas kernels for 57%

profile of v15, /device:TPU:38, one launch (start us, length us, event | category | flops | bytes accessed | tf_op | source)
XLA Modules:
  0.0 315.2 jit_solution(972833521212760395)
XLA Ops:
  7.2 2.0 fusion.67
  9.3 51.1 %shard_map.102 = bf16[1,8,24,8192]{3,2,1,0:T(8,128)(2,1)} custom-call(bf16[1,24,8192]{2,1,0:T(8,128)(2,1)} %get-tuple-element.24.x_ref), custom_call_target="tpu_custom_call" | custom-call | tf_op jit(solution)/shard_map/pallas_call | solution.py:239
  60.5 6.7 %convolution_convert_fusion.6 = bf16[192,512]{1,0:T(8,128)(2,1)S(1)} fusion(bf16[192,8192]{1,0:T(8,128)(2,1)} %bitcast.113, bf16[1,8192,512]{2,1,0:T(8,128)(2,1)} %param.9), kind=kOutput, calls=%fused_computation.41 | convolution fusion | flops 1610711040 | bytes 11730944 | tf_op jit(solution)/shard_map/dot_general | solution.py:412
  68.9 1.8 copy.45
  70.8 20.4 %all-gather.3.cloned.1.call-done = bf16[1,192,8192]{2,1,0:T(8,128)(2,1)} async-done(((bf16[1,24,8192]{2,1,0:T(8,128)(2,1)}), bf16[1,192,8192]{2,1,0:T(8,128)(2,1)}) %all-gather.3.cloned.1.call-update) | async-done | bytes 3145744 | tf_op jit(solution)/shard_map/all_gather | solution.py:398
  91.2 6.1 %convolution_convert_fusion.5 = bf16[192,512]{1,0:T(8,128)(2,1)S(1)} fusion(bf16[1,192,8192]{2,1,0:T(8,128)(2,1)} %all-gather.3.cloned.1.call-done, bf16[1,8192,512]{2,1,0:T(8,128)(2,1)} %param.9), kind=kOutput, calls=%fused_computation.40 | convolution fusion | flops 1610711040 | bytes 11730944 | tf_op jit(solution)/shard_map/dot_general | solution.py:412
  97.5 2.6 fusion.19
  100.1 2.7 fusion.68
  102.8 4.8 %fusion.66 = (bf16[2,4,8,128,192]{3,4,2,1,0:T(8,128)(2,1)}, f32[2,4,8,128,192]{3,4,2,1,0:T(8,128)}) fusion(f32[2,4,8,128,192]{3,4,2,1,0:T(8,128)S(1)} %get-tuple-element.27, f32[2,4,8,128]{3,2,1,0:T(8,128)S(1)} %get-tuple-element.26), kind=kLoop, calls=%fused_computation.66 | loop fusion | flops 3145728 | bytes 15761408 | tf_op jit(solution)/shard_map/vmap()/convert_element_type | solution.py:83
  107.6 7.6 %copy.36 = bf16[2,4,8,128,192]{4,2,3,1,0:T(8,128)(2,1)} copy(bf16[2,4,8,128,192]{3,4,2,1,0:T(8,128)(2,1)} %get-tuple-element.22) | data formatting | bytes 6291456 | tf_op jit(solution)/shard_map/vmap()/convert_element_type | solution.py:83
  115.2 3.6 %fusion.40 = bf16[2,192,4,128]{3,1,2,0:T(8,128)(2,1)S(1)} fusion(bf16[2,4,8,128,192]{4,2,3,1,0:T(8,128)(2,1)} %copy.36, bf16[2,128,4,8,128]{4,3,2,1,0:T(8,128)(2,1)S(1)} %bitcast.107), kind=kOutput, calls=%fused_computation.36 | convolution fusion | flops 402849792 | bytes 5636096 | tf_op jit(solution)/shard_map/vmap(hgln,lhgd->nhd)/dot_general | solution.py:84
  119.3 6.8 %convolution_convert_fusion.1 = bf16[8192,512]{1,0:T(8,128)(2,1)} fusion(bf16[192,8192]{1,0:T(8,128)(2,1)S(1)} %bitcast.125, bf16[192,8192]{1,0:T(8,128)(2,1)S(1)} %bitcast.115, bf16[48,8,4,128]{3,2,1,0:T(4,128)(2,1)S(1)} %bitcast.119), kind=kOutput, calls=%fused_computation.3 | convolution fusion | flops 3238002688 | bytes 15073280 | tf_op jit(solution)/shard_map/td,tk->dk/dot_general | solution.py:424
  126.3 6.1 %convolution_convert_fusion.4 = bf16[192,512]{1,0:T(8,128)(2,1)S(1)} fusion(bf16[192,8192]{1,0:T(8,128)(2,1)} %bitcast.114, bf16[1,8192,512]{2,1,0:T(8,128)(2,1)} %param.10), kind=kOutput, calls=%fused_computation.39 | convolution fusion | flops 1610711040 | bytes 11730944 | tf_op jit(solution)/shard_map/dot_general | solution.py:415
  132.5 6.5 %convolution_convert_fusion.3 = bf16[192,512]{1,0:T(8,128)(2,1)S(1)} fusion(bf16[1,8192,512]{2,1,0:T(8,128)(2,1)} %param.10, bf16[1,192,8192]{2,1,0:T(8,128)(2,1)} %all-gather.3.cloned.1.call-done), kind=kOutput, calls=%fused_computation.38 | convolution fusion | flops 1610711040 | bytes 11730944 | tf_op jit(solution)/shard_map/dot_general | solution.py:415
  139.2 8.8 %fusion.4 = bf16[2,4,8,128,192]{3,4,2,1,0:T(8,128)(2,1)} fusion(f32[2,4,8,128,192]{3,4,2,1,0:T(8,128)} %get-tuple-element.12, bf16[2,128,4,8,128]{4,3,2,1,0:T(8,128)(2,1)S(1)} %bitcast.108, bf16[1,192,4,128]{3,1,2,0:T(8,128)(2,1)S(1)} %copy.26, bf16[1,192,4,128]{3,1,2,0:T(8,128)(2,1)S(1)} %copy.25), kind=kOutput, calls=%fused_computation.9 | convolution fusion | flops 814751936 | bytes 11927552 | tf_op jit(solution)/shard_map/vmap()/sub | solution.py:105
  147.9 7.8 %copy.40 = bf16[2,4,8,128,192]{4,2,3,1,0:T(8,128)(2,1)} copy(bf16[2,4,8,128,192]{3,4,2,1,0:T(8,128)(2,1)} %fusion.4) | data formatting | bytes 6291456 | tf_op jit(solution)/shard_map/vmap()/convert_element_type | solution.py:105
  155.8 3.7 %fusion.43 = bf16[2,192,4,128]{3,1,2,0:T(8,128)(2,1)S(1)} fusion(bf16[2,4,8,128,192]{4,2,3,1,0:T(8,128)(2,1)} %copy.40, bf16[2,128,4,8,128]{4,3,2,1,0:T(8,128)(2,1)S(1)} %bitcast.110), kind=kOutput, calls=%fused_computation.37 | convolution fusion | flops 402849792 | bytes 5636096 | tf_op jit(solution)/shard_map/vmap(hgln,lhgd->nhd)/dot_general | solution.py:109
  160.6 6.7 %convolution_convert_fusion = bf16[8192,512]{1,0:T(8,128)(2,1)} fusion(bf16[192,8192]{1,0:T(8,128)(2,1)S(1)} %bitcast.126, bf16[192,8192]{1,0:T(8,128)(2,1)S(1)} %bitcast.116, bf16[48,8,4,128]{3,2,1,0:T(4,128)(2,1)S(1)} %bitcast.120), kind=kOutput, calls=%fused_computation.2 | convolution fusion | flops 3238002688 | bytes 15073280 | tf_op jit(solution)/shard_map/td,tk->dk/dot_general | solution.py:433
  167.3 2.1 concatenate.15
  169.4 1.9 concatenate.14
  171.3 2.1 convolution_convert_fusion.2
  173.4 4.2 %copy.33 = bf16[1,2,128,4096]{3,2,1,0:T(8,128)(2,1)} copy(bf16[1,2,128,4096]{2,3,1,0:T(8,128)(2,1)} %bitcast.112) | data formatting | bytes 4194304
  178.6 128.0 %shard_map.103 = bf16[48,8192]{1,0:T(8,128)(2,1)} custom-call(bf16[384,1024]{1,0:T(8,128)(2,1)} %bitcast.122, bf16[8192,512]{1,0:T(8,128)(2,1)} %bitcast.123, bf16[8192,512]{1,0:T(8,128)(2,1)} %bitcast.124), custom_call_target="tpu_custom_call" | custom-call | flops 6442450944 | bytes 23068672 | tf_op jit(solution)/shard_map/pallas_call | solution.py:359
  306.6 2.1 copy.83
  (53 shorter events, 5.0 us)
Async XLA Ops:
  7.2 84.1 %all-gather.3.cloned.1.call-start = ((), (), s32[]{:S(2)}) async-start(), calls=%async_computation.4 | async-start | bytes 3538944 | tf_op jit(solution)/shard_map/all_gather | solution.py:398
  9.3 297.3 %reduce-scatter.5.cloned.1.call-start = ((), (), s32[]{:S(2)}) async-start(), calls=%async_computation.3 | async-start | bytes 8912896 | tf_op jit(solution)/shard_map/reduce_scatter | solution.py:429
  60.5 6.8 %copy-start.12 = (s32[2]{0:T(128)S(1)}, s32[2]{0:T(128)}, u32[]{:S(2)}) copy-start(s32[2]{0:T(128)} %param.13) | copy-start | bytes 28
  60.5 6.9 %copy-start.4 = (bf16[1,2,128,4096]{3,2,1,0:T(8,128)(2,1)S(1)}, bf16[1,2,128,4096]{3,2,1,0:T(8,128)(2,1)}, u32[]{:S(2)}) copy-start(bf16[1,2,128,4096]{3,2,1,0:T(8,128)(2,1)} %param.11) | copy-start | bytes 6291460
  67.3 1.6 copy-start.5
  67.5 3.2 %copy-start.13 = (s32[2]{0:T(128)S(1)}, s32[2]{0:T(128)}, u32[]{:S(2)}) copy-start(s32[2]{0:T(128)} %param.12) | copy-start | bytes 28
  115.2 4.0 %copy-start.2 = (bf16[1,8,24,8192]{3,2,1,0:T(8,128)(2,1)S(1)}, bf16[1,8,24,8192]{3,2,1,0:T(8,128)(2,1)}, u32[]{:S(2)}) copy-start(bf16[1,8,24,8192]{3,2,1,0:T(8,128)(2,1)} %shard_map.102) | copy-start | bytes 9437188
  115.2 4.1 %copy-start.10 = (bf16[1,192,8192]{2,1,0:T(8,128)(2,1)S(1)}, bf16[1,192,8192]{2,1,0:T(8,128)(2,1)}, u32[]{:S(2)}) copy-start(bf16[1,192,8192]{2,1,0:T(8,128)(2,1)} %all-gather.3.cloned.1.call-done) | copy-start | bytes 9437188
  119.2 6.9 %copy-start.6 = (bf16[2,192,4,128]{3,2,1,0:T(4,128)(2,1)}, bf16[2,192,4,128]{3,2,1,0:T(4,128)(2,1)S(1)}, u32[]{:S(2)}) copy-start(bf16[2,192,4,128]{3,2,1,0:T(4,128)(2,1)S(1)} %copy.24) | copy-start | bytes 1179652
  126.1 180.6 %reduce-scatter.3.cloned.1.call-start = ((), (), s32[]{:S(2)}) async-start(), calls=%async_computation.2 | async-start | bytes 8912896 | tf_op jit(solution)/shard_map/reduce_scatter | solution.py:437
  147.9 7.9 %copy-start.1 = (bf16[32,8,32,128]{3,2,1,0:T(8,128)(2,1)S(1)}, bf16[32,8,32,128]{3,2,1,0:T(8,128)(2,1)}, u32[]{:S(2)}) copy-start(bf16[32,8,32,128]{3,2,1,0:T(8,128)(2,1)} %copy.45) | copy-start | bytes 6291460
  155.8 4.8 %copy-start.3 = (bf16[1,8,24,8192]{3,2,1,0:T(8,128)(2,1)S(1)}, bf16[1,8,24,8192]{3,2,1,0:T(8,128)(2,1)}, u32[]{:S(2)}) copy-start(bf16[1,8,24,8192]{3,2,1,0:T(8,128)(2,1)} %shard_map.102) | copy-start | bytes 9437188
  155.8 4.8 %copy-start.11 = (bf16[1,192,8192]{2,1,0:T(8,128)(2,1)S(1)}, bf16[1,192,8192]{2,1,0:T(8,128)(2,1)}, u32[]{:S(2)}) copy-start(bf16[1,192,8192]{2,1,0:T(8,128)(2,1)} %all-gather.3.cloned.1.call-done) | copy-start | bytes 9437188
  159.8 0.7 copy-start.7
  167.3 4.0 %copy-start = (bf16[2,4,8,128,192]{3,4,2,1,0:T(8,128)(2,1)S(1)}, bf16[2,4,8,128,192]{3,4,2,1,0:T(8,128)(2,1)}, u32[]{:S(2)}) copy-start(bf16[2,4,8,128,192]{3,4,2,1,0:T(8,128)(2,1)} %fusion.4) | copy-start | bytes 9437188
  173.4 4.2 %copy-start.8 = (bf16[2,8,24,512]{3,2,1,0:T(8,128)(2,1)S(1)}, bf16[2,8,24,512]{3,2,1,0:T(8,128)(2,1)}, u32[]{:S(2)}) copy-start(bf16[2,8,24,512]{3,2,1,0:T(8,128)(2,1)} %concatenate.15) | copy-start | bytes 1179652
  173.4 4.2 %copy-start.9 = (bf16[2,8,24,512]{3,2,1,0:T(8,128)(2,1)S(1)}, bf16[2,8,24,512]{3,2,1,0:T(8,128)(2,1)}, u32[]{:S(2)}) copy-start(bf16[2,8,24,512]{3,2,1,0:T(8,128)(2,1)} %concatenate.14) | copy-start | bytes 1179652
Sparse Core Ops, SparseCore 0:
  10.9 80.3 all-gather.2
  126.2 75.8 reduce-scatter.4
  205.1 91.9 reduce-scatter.2

commit v16 on v14

--- a/solution.py
+++ b/solution.py
@@ -413,6 +413,10 @@
         values_list.append(
             jnp.dot(tokens, w_value, preferred_element_type=jnp.float32).astype(jnp.bfloat16)
         )
+        if sample_index + 1 < samples_here:
+            values_list[-1], token_list[sample_index + 1] = lax.optimization_barrier(
+                (values_list[-1], token_list[sample_index + 1])
+            )
     keys_both = jnp.stack(keys_list)
     values_both = jnp.stack(values_list)
     key_limits = tile_counts * tile_len

time: 312 us -> 308 us (0.987)
  waiting for transfers between devices: 17.7 us -> 11.6 us
  Pallas kernels: 182 us -> 187 us
    all_gather x1, waiting for transfers between devices: 17.7 us -> 11.5 us  [shards(): lax.all_gather(image_tokens[i], 'section', axis=0, tiled=True)]
    pallas_call x1, Pallas kernels: 127 us -> 132 us  [image_exchange(): pl.pallas_call(functools.partial(image_kernel, n, tiles), out_shape=jax.S...]
    unnamed x26 -> x14, local copies, waits for them, and re-layouts: 15.2 us -> 13.6 us
  transfers between devices with their start and end apart: 3 -> 3, of which waited for: 1 -> 1; matrix products, arithmetic and copies ran while one was open for 21% -> 21% of each run, Pallas kernels for 59% -> 61%
where the time goes in v16:
time: 308 us; the launch traced here: 306 us
  Pallas kernels  187 us (61%)
  matrix products  71.2 us (23%)
  local copies, waits for them, and re-layouts  17.8 us (6%)
  between operations  14 us (5%)
  waiting for transfers between devices  11.6 us (4%)
  other arithmetic  4.34 us (1%)
    pallas_call x1, Pallas kernels, image_exchange(): pl.pallas_call(functools.partial(image_kernel, n, tiles), out_shape=jax.S...  132 us
    pallas_call x1, Pallas kernels, relay_gather(): pl.pallas_call(relay_gather_kernel, out_shape=jax.ShapeDtypeStruct((sampl...  55.3 us
    unnamed x14, local copies, waits for them, and re-layouts  13.6 us
    dot_general x2, matrix products, shards(): jnp.dot(tokens, w_key, preferred_element_type=jnp.float32)  12.3 us
    dot_general x2, matrix products, shards(): jnp.dot(tokens, w_value, preferred_element_type=jnp.float32)  12.3 us
    dot_general x1, matrix products, attend_back(): jnp.einsum('hgln,lhgd->nhd', score_grad, heads_of_queries, preferred_elem...  11.8 us
    all_gather x1, waiting for transfers between devices, shards(): lax.all_gather(image_tokens[i], 'section', axis=0, tiled=True)  11.5 us
    dot_general x1, matrix products, attend_back(): jnp.einsum('hgln,nhd->lhgd', score_grad, heads_of_keys, preferred_element...  10.5 us
  transfers between devices with their start and end apart: 3, of which 1 were waited for; matrix products, arithmetic and copies ran while one was open for 21% of the time, Pallas kernels for 61%

profile of v16, /device:TPU:38, one launch (start us, length us, event | category | flops | bytes accessed | tf_op | source)
XLA Modules:
  0.0 306.3 jit_solution(7013623070492657164)
XLA Ops:
  7.2 2.0 fusion.65
  9.3 3.4 %copy.36 = bf16[32,8,32,128]{3,2,1,0:T(8,128)(2,1)} copy(bf16[32,8,32,128]{3,1,2,0:T(8,128)(2,1)} %bitcast.131) | data formatting | bytes 4194304
  12.7 2.1 copy.37
  14.8 55.3 %shard_map.102 = bf16[1,8,24,8192]{3,2,1,0:T(8,128)(2,1)} custom-call(bf16[1,24,8192]{2,1,0:T(8,128)(2,1)} %get-tuple-element.21.x_ref), custom_call_target="tpu_custom_call" | custom-call | tf_op jit(solution)/shard_map/pallas_call | solution.py:239
  70.1 6.2 %convolution_convert_fusion.5 = bf16[192,512]{1,0:T(8,128)(2,1)S(1)} fusion(bf16[192,8192]{1,0:T(8,128)(2,1)} %bitcast.127, bf16[1,8192,512]{2,1,0:T(8,128)(2,1)} %param.9), kind=kOutput, calls=%fused_computation.39 | convolution fusion | flops 1610711040 | bytes 11730944 | tf_op jit(solution)/shard_map/dot_general | solution.py:411
  76.5 6.1 %convolution_convert_fusion.4 = bf16[192,512]{1,0:T(8,128)(2,1)S(1)} fusion(bf16[192,8192]{1,0:T(8,128)(2,1)} %bitcast.128, bf16[1,8192,512]{2,1,0:T(8,128)(2,1)} %param.10), kind=kOutput, calls=%fused_computation.38 | convolution fusion | flops 1610711040 | bytes 11730944 | tf_op jit(solution)/shard_map/dot_general | solution.py:414
  82.7 11.5 %all-gather.3.cloned.1.call-done = bf16[1,192,8192]{2,1,0:T(8,128)(2,1)} async-done(((bf16[1,24,8192]{2,1,0:T(8,128)(2,1)}), bf16[1,192,8192]{2,1,0:T(8,128)(2,1)}) %all-gather.3.cloned.1.call-update) | async-done | bytes 3145744 | tf_op jit(solution)/shard_map/all_gather | solution.py:398
  94.2 6.1 %convolution_convert_fusion.3 = bf16[192,512]{1,0:T(8,128)(2,1)S(1)} fusion(bf16[192,8192]{1,0:T(8,128)(2,1)} %bitcast.140, bf16[1,8192,512]{2,1,0:T(8,128)(2,1)} %param.9), kind=kOutput, calls=%fused_computation.37 | convolution fusion | flops 1610711040 | bytes 11730944 | tf_op jit(solution)/shard_map/dot_general | solution.py:411
  100.4 2.6 fusion.19
  103.0 2.7 fusion.66
  105.7 1.4 broadcast_divide_fusion
  107.2 3.2 %copy-done = f32[2,4,8,128,192]{3,4,2,1,0:T(8,128)} copy-done((f32[2,4,8,128,192]{3,4,2,1,0:T(8,128)}, f32[2,4,8,128,192]{3,4,2,1,0:T(8,128)S(1)}, u32[]{:S(2)}) %copy-start) | copy-done | bytes 6291480
  110.4 1.4 fusion.37
  111.8 0.3 copy.23
  112.3 6.8 %convolution_convert_fusion.1 = bf16[8192,512]{1,0:T(8,128)(2,1)} fusion(bf16[192,8192]{1,0:T(8,128)(2,1)S(1)} %bitcast.143, bf16[192,8192]{1,0:T(8,128)(2,1)S(1)} %bitcast.130, bf16[48,8,4,128]{3,2,1,0:T(4,128)(2,1)S(1)} %bitcast.134), kind=kOutput, calls=%fused_computation.3 | convolution fusion | flops 3238002688 | bytes 15073280 | tf_op jit(solution)/shard_map/td,tk->dk/dot_general | solution.py:427
  119.4 6.1 %convolution_convert_fusion.2 = bf16[192,512]{1,0:T(8,128)(2,1)S(1)} fusion(bf16[192,8192]{1,0:T(8,128)(2,1)} %bitcast.141, bf16[1,8192,512]{2,1,0:T(8,128)(2,1)} %param.10), kind=kOutput, calls=%fused_computation.36 | convolution fusion | flops 1610711040 | bytes 11730944 | tf_op jit(solution)/shard_map/dot_general | solution.py:414
  125.6 3.7 %fusion.21 = f32[2,4,192,128,8]{3,2,4,1,0:T(8,128)} fusion(bf16[2,128,4,8,128]{4,3,2,1,0:T(8,128)(2,1)S(1)} %bitcast.124, pred[2,128]{1,0:T(4,128)(4,1)S(1)} %iota_compare_fusion.1, bf16[1,192,4,128]{3,1,2,0:T(8,128)(2,1)S(1)} %copy.25, bf16[1,192,4,128]{3,1,2,0:T(8,128)(2,1)S(1)} %copy.24), kind=kOutput, calls=%fused_computation.29 | convolution fusion | flops 404488192 | bytes 8782080 | tf_op jit(solution)/shard_map/vmap(lhgd,nhd->hgln)/dot_general | solution.py:101
  129.3 11.8 %fusion.34 = bf16[2,192,4,128]{3,1,2,0:T(8,128)(2,1)S(1)} fusion(bf16[2,128,4,8,128]{4,3,2,1,0:T(8,128)(2,1)} %bitcast.126, f32[2,4,8,128,192]{3,4,2,1,0:T(8,128)} %copy-done, f32[2,4,192,128,8]{3,2,4,1,0:T(8,128)} %fusion.21), kind=kOutput, calls=%fused_computation.34 | convolution fusion | flops 410722496 | bytes 15073280 | tf_op jit(solution)/shard_map/vmap(hgln,lhgd->nhd)/dot_general | solution.py:109
  141.4 9.8 %convolution_convert_fusion = bf16[8192,512]{1,0:T(8,128)(2,1)} fusion(bf16[192,8192]{1,0:T(8,128)(2,1)} %bitcast.142, bf16[192,8192]{1,0:T(8,128)(2,1)} %bitcast.129, bf16[48,8,4,128]{3,2,1,0:T(4,128)(2,1)S(1)} %bitcast.135), kind=kOutput, calls=%fused_computation.2 | convolution fusion | flops 3238002688 | bytes 15073280 | tf_op jit(solution)/shard_map/td,tk->dk/dot_general | solution.py:436
  151.6 10.5 %fusion.17 = bf16[2,4,128,8,128]{4,2,3,1,0:T(8,128)(2,1)S(1)} fusion(f32[2,4,8,128,192]{3,4,2,1,0:T(8,128)} %copy-done, f32[2,4,192,128,8]{3,2,4,1,0:T(8,128)} %fusion.21, bf16[1,192,4,128]{3,1,2,0:T(8,128)(2,1)S(1)} %copy.20, bf16[1,192,4,128]{3,1,2,0:T(8,128)(2,1)S(1)} %copy.19), kind=kOutput, calls=%fused_computation.25 | convolution fusion | flops 412360896 | bytes 15073280 | tf_op jit(solution)/shard_map/vmap(hgln,nhd->lhgd)/dot_general | solution.py:106
  162.1 2.7 copy.31
  164.9 1.0 copy.29
  165.9 131.8 %shard_map.103 = bf16[48,8192]{1,0:T(8,128)(2,1)} custom-call(bf16[384,1024]{1,0:T(8,128)(2,1)} %bitcast.137, bf16[8192,512]{1,0:T(8,128)(2,1)} %bitcast.138, bf16[8192,512]{1,0:T(8,128)(2,1)} %bitcast.139), custom_call_target="tpu_custom_call" | custom-call | flops 6442450944 | bytes 23068672 | tf_op jit(solution)/shard_map/pallas_call | solution.py:359
  297.7 2.1 copy.68
  (32 shorter events, 1.8 us)
Async XLA Ops:
  7.2 87.0 %all-gather.3.cloned.1.call-start = ((), (), s32[]{:S(2)}) async-start(), calls=%async_computation.4 | async-start | bytes 3538944 | tf_op jit(solution)/shard_map/all_gather | solution.py:398
  9.3 288.4 %reduce-scatter.5.cloned.1.call-start = ((), (), s32[]{:S(2)}) async-start(), calls=%async_computation.3 | async-start | bytes 8912896 | tf_op jit(solution)/shard_map/reduce_scatter | solution.py:432
  70.1 6.3 %copy-start.3 = (s32[2]{0:T(128)S(1)}, s32[2]{0:T(128)}, u32[]{:S(2)}) copy-start(s32[2]{0:T(128)} %param.13) | copy-start | bytes 28
  70.1 6.4 %copy-start.4 = (s32[2]{0:T(128)S(1)}, s32[2]{0:T(128)}, u32[]{:S(2)}) copy-start(s32[2]{0:T(128)} %param.12) | copy-start | bytes 28
  107.2 3.2 %copy-start = (f32[2,4,8,128,192]{3,4,2,1,0:T(8,128)}, f32[2,4,8,128,192]{3,4,2,1,0:T(8,128)S(1)}, u32[]{:S(2)}) copy-start(f32[2,4,8,128,192]{3,4,2,1,0:T(8,128)S(1)} %broadcast_divide_fusion) | copy-start | bytes 18874372
  107.2 4.9 %copy-start.1 = (bf16[1,8,24,8192]{3,2,1,0:T(8,128)(2,1)S(1)}, bf16[1,8,24,8192]{3,2,1,0:T(8,128)(2,1)}, u32[]{:S(2)}) copy-start(bf16[1,8,24,8192]{3,2,1,0:T(8,128)(2,1)} %shard_map.102) | copy-start | bytes 9437188
  107.2 5.1 %copy-start.2 = (bf16[1,192,8192]{2,1,0:T(8,128)(2,1)S(1)}, bf16[1,192,8192]{2,1,0:T(8,128)(2,1)}, u32[]{:S(2)}) copy-start(bf16[1,192,8192]{2,1,0:T(8,128)(2,1)} %all-gather.3.cloned.1.call-done) | copy-start | bytes 9437188
  119.0 178.6 %reduce-scatter.3.cloned.1.call-start = ((), (), s32[]{:S(2)}) async-start(), calls=%async_computation.2 | async-start | bytes 8912896 | tf_op jit(solution)/shard_map/reduce_scatter | solution.py:440
Sparse Core Ops, SparseCore 0:
  10.9 83.2 all-gather.2
  119.2 85.0 reduce-scatter.4
  207.2 86.6 reduce-scatter.2

commit v17 on v16

--- a/solution.py
+++ b/solution.py
@@ -405,6 +405,9 @@
     token_list = [first.reshape(image_len, model_width)] + late
     keys_list = []
     values_list = []
+    weight_list = []
+    value_grad_list = []
+    key_limits = tile_counts * tile_len
     for sample_index in range(samples_here):
         tokens = token_list[sample_index]
         keys_list.append(
@@ -413,16 +416,25 @@
         values_list.append(
             jnp.dot(tokens, w_value, preferred_element_type=jnp.float32).astype(jnp.bfloat16)
         )
+        weights_here, value_grad_here = attend_front(
+            query_local[sample_index],
+            keys_list[-1],
+            cotan_local[sample_index],
+            key_limits[sample_index],
+            text_lengths[sample_index],
+        )
         if sample_index + 1 < samples_here:
-            values_list[-1], token_list[sample_index + 1] = lax.optimization_barrier(
-                (values_list[-1], token_list[sample_index + 1])
+            values_list[-1], weights_here, value_grad_here, token_list[sample_index + 1] = (
+                lax.optimization_barrier(
+                    (values_list[-1], weights_here, value_grad_here, token_list[sample_index + 1])
+                )
             )
+        weight_list.append(weights_here)
+        value_grad_list.append(value_grad_here)
     keys_both = jnp.stack(keys_list)
     values_both = jnp.stack(values_list)
-    key_limits = tile_counts * tile_len
-    weights, value_grads = jax.vmap(attend_front)(
-        query_local, keys_both, cotan_local, key_limits, text_lengths
-    )
+    weights = jnp.stack(weight_list)
+    value_grads = jnp.stack(value_grad_list)
     all_tokens = jnp.concatenate(token_list, axis=0)
     value_term = jnp.einsum(
         "td,tk->dk", all_tokens, value_grads.reshape(samples_here * image_len, -1),

time: 308 us -> 330 us (1.071)
  other arithmetic: 4.34 us -> 16.3 us
  waiting for transfers between devices: 11.6 us -> 1.21 us
  local copies, waits for them, and re-layouts: 17.8 us -> 27.3 us
  matrix products: 71.2 us -> 78.6 us
  Pallas kernels: 187 us -> 191 us
    all_gather x1, waiting for transfers between devices: 11.5 us -> 1.13 us  [shards(): lax.all_gather(image_tokens[i], 'section', axis=0, tiled=True)]
    another operation x0 -> x3, other arithmetic: none -> 10.2 us  [the longest x2 9.26 us: shards(): weights = jnp.stack(weight_list)]
    sub x0 -> x2, matrix products: none -> 6.69 us  [attend_front(): raised = jnp.exp(scores - row_max)]
    slice x0 -> x3, local copies, waits for them, and re-layouts: none -> 3.86 us  [the longest x1 2.69 us: shards(): query_local[sample_index]]
    pallas_call x1, Pallas kernels: 132 us -> 135 us  [image_exchange(): pl.pallas_call(functools.partial(image_kernel, n, tiles), out_shape=jax.S...]
    unnamed x14 -> x47, local copies, waits for them, and re-layouts: 13.6 us -> 16.9 us
  transfers between devices with their start and end apart: 3 -> 3, of which waited for: 1 -> 1; matrix products, arithmetic and copies ran while one was open for 21% -> 25% of each run, Pallas kernels for 61% -> 58%
where the time goes in v17:
time: 330 us; the launch traced here: 329 us
  Pallas kernels  191 us (58%)
  matrix products  78.6 us (24%)
  local copies, waits for them, and re-layouts  27.3 us (8%)
  other arithmetic  16.3 us (5%)
  between operations  14.1 us (4%)
    pallas_call x1, Pallas kernels, image_exchange(): pl.pallas_call(functools.partial(image_kernel, n, tiles), out_shape=jax.S...  135 us
    pallas_call x1, Pallas kernels, relay_gather(): pl.pallas_call(relay_gather_kernel, out_shape=jax.ShapeDtypeStruct((sampl...  56.3 us
    unnamed x47, local copies, waits for them, and re-layouts  16.9 us
    dot_general x1, matrix products, attend_back(): jnp.einsum('hgln,lhgd->nhd', score_grad, heads_of_queries, preferred_elem...  12.9 us
    dot_general x2, matrix products, shards(): jnp.dot(tokens, w_key, preferred_element_type=jnp.float32)  12.3 us
    dot_general x2, matrix products, shards(): jnp.dot(tokens, w_value, preferred_element_type=jnp.float32)  12.1 us
    dot_general x1, matrix products, attend_back(): jnp.einsum('hgln,nhd->lhgd', score_grad, heads_of_keys, preferred_element...  10.5 us
    dot_general x1, matrix products, shards(): jnp.einsum('td,tk->dk', all_tokens, value_grads.reshape(samples_here * im...  9.89 us
  transfers between devices with their start and end apart: 3, of which 1 were waited for; matrix products, arithmetic and copies ran while one was open for 25% of the time, Pallas kernels for 58%

profile of v17, /device:TPU:38, one launch (start us, length us, event | category | flops | bytes accessed | tf_op | source)
XLA Modules:
  0.0 329.1 jit_solution(13362870028770792516)
XLA Ops:
  7.2 2.0 fusion.108
  9.3 2.7 fusion.107
  12.0 2.4 copy.56
  18.3 56.3 %shard_map.102 = bf16[1,8,24,8192]{3,2,1,0:T(8,128)(2,1)} custom-call(bf16[1,24,8192]{2,1,0:T(8,128)(2,1)} %get-tuple-element.29.x_ref), custom_call_target="tpu_custom_call" | custom-call | tf_op jit(solution)/shard_map/pallas_call | solution.py:239
  74.7 6.2 %convolution_convert_fusion.5 = bf16[192,512]{1,0:T(8,128)(2,1)S(1)} fusion(bf16[192,8192]{1,0:T(8,128)(2,1)} %bitcast.177, bf16[1,8192,512]{2,1,0:T(8,128)(2,1)} %param.9), kind=kOutput, calls=%fused_computation.53 | convolution fusion | flops 1610711040 | bytes 11730944 | tf_op jit(solution)/shard_map/dot_general | solution.py:414
  83.4 2.7 fusion.111
  86.2 2.2 broadcast_divide_fusion.1
  91.7 5.9 %convolution_convert_fusion.4 = bf16[192,512]{1,0:T(8,128)(2,1)} fusion(bf16[192,8192]{1,0:T(8,128)(2,1)S(1)} %bitcast.179, bf16[1,8192,512]{2,1,0:T(8,128)(2,1)} %param.10), kind=kOutput, calls=%fused_computation.52 | convolution fusion | flops 1610711040 | bytes 11730944 | tf_op jit(solution)/shard_map/dot_general | solution.py:417
  98.7 6.1 %convolution_convert_fusion.3 = bf16[192,512]{1,0:T(8,128)(2,1)S(1)} fusion(bf16[192,8192]{1,0:T(8,128)(2,1)} %bitcast.196, bf16[1,8192,512]{2,1,0:T(8,128)(2,1)} %param.9), kind=kOutput, calls=%fused_computation.51 | convolution fusion | flops 1610711040 | bytes 11730944 | tf_op jit(solution)/shard_map/dot_general | solution.py:414
  105.6 4.0 %fusion.116 = (f32[4,8,128]{2,1,0:T(8,128)S(1)}, f32[4,8,128,192]{2,3,1,0:T(8,128)}) fusion(pred[192]{0:T(512)(128)(4,1)} %iota_compare_fusion.1, bf16[128,4,8,128]{0,3,2,1:T(8,128)(2,1)} %bitcast.187, bf16[192,4,128,1]{2,1,0,3:T(4,128)(2,1)} %bitcast.193), kind=kOutput, calls=%fused_computation.114 | convolution fusion | flops 204472512 | bytes 4407488 | tf_op jit(solution)/shard_map/sub | solution.py:81
  109.6 4.2 %fusion.34 = f32[1,4,8,128,192]{3,4,2,1,0:T(8,128)} fusion(f32[4,8,128,192]{2,3,1,0:T(8,128)} %get-tuple-element.37, f32[4,8,128]{2,1,0:T(8,128)S(1)} %get-tuple-element.36), kind=kLoop, calls=%fused_computation.43 | loop fusion | flops 786432 | bytes 6307840 | tf_op jit(solution)/shard_map/stack | solution.py:436
  116.5 9.9 %convolution_convert_fusion.1 = bf16[8192,512]{1,0:T(8,128)(2,1)} fusion(bf16[384,512]{1,0:T(8,128)(2,1)S(1)} %bitcast.191, bf16[192,8192]{1,0:T(8,128)(2,1)} %bitcast.197, bf16[192,8192]{1,0:T(8,128)(2,1)} %bitcast.178), kind=kOutput, calls=%fused_computation.4 | convolution fusion | flops 3238002688 | bytes 15073280 | tf_op jit(solution)/shard_map/td,tk->dk/dot_general | solution.py:439
  126.4 5.1 %pad_maximum_fusion.1 = f32[2,4,8,128,192]{3,4,2,1,0:T(8,128)} fusion(f32[1,4,8,128,192]{3,4,2,1,0:T(8,128)} %fusion.34, f32[1,4,8,128,192]{3,4,2,1,0:T(8,128)S(1)} %bitcast.172), kind=kLoop, calls=%fused_computation.6 | loop fusion | flops 1572864 | bytes 12582912 | tf_op jit(solution)/shard_map/stack | solution.py:436
  131.6 2.2 copy.61
  133.8 1.8 copy.62
  135.8 6.1 %convolution_convert_fusion.2 = bf16[192,512]{1,0:T(8,128)(2,1)S(1)} fusion(bf16[192,8192]{1,0:T(8,128)(2,1)} %bitcast.198, bf16[1,8192,512]{2,1,0:T(8,128)(2,1)} %param.10), kind=kOutput, calls=%fused_computation.50 | convolution fusion | flops 1610711040 | bytes 11730944 | tf_op jit(solution)/shard_map/dot_general | solution.py:417
  142.0 3.7 %fusion.18 = f32[2,4,192,128,8]{3,2,4,1,0:T(8,128)} fusion(bf16[2,128,4,8,128]{4,3,2,1,0:T(8,128)(2,1)S(1)} %bitcast.173, pred[2,128]{1,0:T(4,128)(4,1)S(1)} %iota_compare_fusion, bf16[1,192,4,128]{3,1,2,0:T(8,128)(2,1)S(1)} %copy.35, bf16[1,192,4,128]{3,1,2,0:T(8,128)(2,1)S(1)} %copy.34), kind=kOutput, calls=%fused_computation.27 | convolution fusion | flops 404488192 | bytes 8782080 | tf_op jit(solution)/shard_map/vmap(lhgd,nhd->hgln)/dot_general | solution.py:101
  145.8 12.9 %fusion.41 = bf16[2,192,4,128]{3,1,2,0:T(8,128)(2,1)} fusion(bf16[2,128,4,8,128]{4,3,2,1,0:T(8,128)(2,1)} %bitcast.181, f32[2,4,8,128,192]{3,4,2,1,0:T(8,128)} %pad_maximum_fusion.1, f32[2,4,192,128,8]{3,2,4,1,0:T(8,128)} %fusion.18), kind=kOutput, calls=%fused_computation.46 | convolution fusion | flops 410722496 | bytes 15073280 | tf_op jit(solution)/shard_map/vmap(hgln,lhgd->nhd)/dot_general | solution.py:109
  158.7 1.3 copy.38
  160.8 8.8 %convolution_convert_fusion = bf16[8192,512]{1,0:T(8,128)(2,1)} fusion(bf16[192,8192]{1,0:T(8,128)(2,1)} %bitcast.199, bf16[192,8192]{1,0:T(8,128)(2,1)S(1)} %bitcast.180, bf16[48,8,4,128]{3,2,1,0:T(4,128)(2,1)S(1)} %bitcast.185), kind=kOutput, calls=%fused_computation.3 | convolution fusion | flops 3238002688 | bytes 15073280 | tf_op jit(solution)/shard_map/td,tk->dk/dot_general | solution.py:448
  171.0 10.5 %fusion.20 = bf16[2,4,128,8,128]{4,2,3,1,0:T(8,128)(2,1)S(1)} fusion(f32[2,4,8,128,192]{3,4,2,1,0:T(8,128)} %pad_maximum_fusion.1, f32[2,4,192,128,8]{3,2,4,1,0:T(8,128)} %fusion.18, bf16[1,192,4,128]{3,1,2,0:T(8,128)(2,1)S(1)} %copy.28, bf16[1,192,4,128]{3,1,2,0:T(8,128)(2,1)S(1)} %copy.27), kind=kOutput, calls=%fused_computation.29 | convolution fusion | flops 412360896 | bytes 15073280 | tf_op jit(solution)/shard_map/vmap(hgln,nhd->lhgd)/dot_general | solution.py:106
  181.5 2.7 copy.42
  185.3 135.1 %shard_map.103 = bf16[48,8192]{1,0:T(8,128)(2,1)} custom-call(bf16[384,1024]{1,0:T(8,128)(2,1)} %bitcast.190, bf16[8192,512]{1,0:T(8,128)(2,1)} %bitcast.194, bf16[8192,512]{1,0:T(8,128)(2,1)} %bitcast.195), custom_call_target="tpu_custom_call" | custom-call | flops 6442450944 | bytes 23068672 | tf_op jit(solution)/shard_map/pallas_call | solution.py:359
  320.5 2.1 copy.109
  (79 shorter events, 17.8 us)
Async XLA Ops:
  7.2 91.6 %all-gather.3.cloned.1.call-start = ((), (), s32[]{:S(2)}) async-start(), calls=%async_computation.4 | async-start | bytes 3538944 | tf_op jit(solution)/shard_map/all_gather | solution.py:398
  9.3 311.2 %reduce-scatter.5.cloned.1.call-start = ((), (), s32[]{:S(2)}) async-start(), calls=%async_computation.3 | async-start | bytes 8912896 | tf_op jit(solution)/shard_map/reduce_scatter | solution.py:444
  12.0 3.7 %copy-start = (bf16[1,2,128,4096]{3,2,1,0:T(8,128)(2,1)S(1)}, bf16[1,2,128,4096]{3,2,1,0:T(8,128)(2,1)}, u32[]{:S(2)}) copy-start(bf16[1,2,128,4096]{3,2,1,0:T(8,128)(2,1)} %param.11) | copy-start | bytes 6291460
  74.7 6.3 %copy-start.17 = (s32[2]{0:T(128)S(1)}, s32[2]{0:T(128)}, u32[]{:S(2)}) copy-start(s32[2]{0:T(128)} %param.12) | copy-start | bytes 28
  74.7 7.6 %copy-start.15 = (s32[2]{0:T(128)S(1)}, s32[2]{0:T(128)}, u32[]{:S(2)}) copy-start(s32[2]{0:T(128)} %param.13) | copy-start | bytes 28
  74.7 8.7 %copy-start.9 = (bf16[1,1,128,4096]{2,3,1,0:T(8,128)(2,1)S(1)}, bf16[1,1,128,4096]{2,3,1,0:T(8,128)(2,1)}, u32[]{:S(2)}) copy-start(bf16[1,1,128,4096]{2,3,1,0:T(8,128)(2,1)} %copy.56) | copy-start | bytes 3145732
  80.9 5.2 %copy-start.10 = (bf16[192,512]{1,0:T(8,128)(2,1)}, bf16[192,512]{1,0:T(8,128)(2,1)S(1)}, u32[]{:S(2)}) copy-start(bf16[192,512]{1,0:T(8,128)(2,1)S(1)} %convolution_convert_fusion.5) | copy-start | bytes 589828
  86.2 2.2 copy-start.2
  88.4 3.3 copy-start.3
  104.9 4.7 %copy-start.12 = (bf16[192,512]{1,0:T(8,128)(2,1)}, bf16[192,512]{1,0:T(8,128)(2,1)S(1)}, u32[]{:S(2)}) copy-start(bf16[192,512]{1,0:T(8,128)(2,1)S(1)} %convolution_convert_fusion.3) | copy-start | bytes 589828
  109.6 4.2 %copy-start.5 = (f32[4,8,128,192]{2,3,1,0:T(8,128)S(1)}, f32[4,8,128,192]{2,3,1,0:T(8,128)}, u32[]{:S(2)}) copy-start(f32[4,8,128,192]{2,3,1,0:T(8,128)} %get-tuple-element.37) | copy-start | bytes 9437188
  109.6 4.2 %copy-start.8 = (bf16[16,8,32,128]{3,2,1,0:T(8,128)(2,1)S(1)}, bf16[16,8,32,128]{3,2,1,0:T(8,128)(2,1)}, u32[]{:S(2)}) copy-start(bf16[16,8,32,128]{3,2,1,0:T(8,128)(2,1)} %copy.60) | copy-start | bytes 3145732
  109.6 4.2 %copy-start.18 = (pred[128]{0:T(512)(128)(4,1)S(1)}, pred[128]{0:T(512)(128)(4,1)}, u32[]{:S(2)}) copy-start(pred[128]{0:T(512)(128)(4,1)} %iota_compare_fusion.3) | copy-start | bytes 388
  131.5 189.0 %reduce-scatter.3.cloned.1.call-start = ((), (), s32[]{:S(2)}) async-start(), calls=%async_computation.2 | async-start | bytes 8912896 | tf_op jit(solution)/shard_map/reduce_scatter | solution.py:452
  131.6 2.3 copy-start.1
  133.8 1.8 copy-start.16
  133.8 1.9 copy-start.14
  145.8 15.0 %copy-start.4 = (bf16[1,8,24,8192]{3,2,1,0:T(8,128)(2,1)S(1)}, bf16[1,8,24,8192]{3,2,1,0:T(8,128)(2,1)}, u32[]{:S(2)}) copy-start(bf16[1,8,24,8192]{3,2,1,0:T(8,128)(2,1)} %shard_map.102) | copy-start | bytes 9437188
  160.0 0.7 copy-start.6
  169.6 0.9 copy-start.11
  169.6 1.0 copy-start.13
  169.6 1.2 copy-start.7
Sparse Core Ops, SparseCore 0:
  10.9 87.7 all-gather.2
  131.6 86.0 reduce-scatter.4
  220.7 91.6 reduce-scatter.2
